TPU v7x, 32 devices: a whole 2x2x4 slice. The times are simulated.
32 devices in a mesh: subj: 2 (over x), row: 8 (over z, y), col: 2 (over core).
Axes of the slice: x: 2, y: 2, z: 4, core: 2. Of those that a mesh axis runs over, the one named last changes fastest.
Arguments:
- series: float32 [256, 11392], P(('subj', 'row', 'col')), parts along dimension 0, may hold values from -30 to 30
- tap_values: float32 [17], replicated, may hold values from -4 to 4
- tap_count: int32 [1], replicated, may hold values from 4 to 8
- kept_frames: int32 [32], P('subj'), parts along dimension 0, may hold values from 1 to 8, 96 in all
- band_start: int32 [2], P('subj'), parts along dimension 0, may hold values from 0 to 7296
Outputs:
- fisher_band: bfloat16 [8192, 11392], P('subj', ('row', 'col')), parts along dimension 0
There are 2 independent parts, one for each index of `subj`. A program takes and returns all parts, laid end to end along the dimension named above; an argument that names none is the same for every part. Nothing has to cross between parts.
Inputs may be any that keep to these rules, and one draw needn't show every extreme that they name: `tap_count`: frames farther than this from the centre get no weight. Time block d holds frames d * 8 to (d + 1) * 8 - 1; only its first kept_frames[d] frames are kept. `band_start`: the 4096 band grayordinates lie inside the grid.
All inputs are finite; a program needn't handle non-finite values.
Results may differ from a plain program's by a relative error of at most 0.0031.
The roundings to bfloat16 on the way count: a program that leaves them out, or rounds other values in their place, can miss the bound.
Values may be sent and summed in bfloat16 or wider, within the bound.
No kernel may reach another device: no remote copies, remote signals or barrier semaphores. Data moves between devices by JAX's collectives and lax.ppermute only.
A program may use at most 128 MiB of HBM per device.

v0:
```python
import jax
import jax.numpy as jnp
from jax import lax
from jax.sharding import PartitionSpec as P

B = 4096


EPSILON = 1e-06
CLIP_LIMIT = 0.999


def with_halo(cells, sides, width):
    for axis, dim in sides:
        count = lax.axis_size(axis)
        ends = count - 1
        head = lax.slice_in_dim(cells, 0, width, axis=dim)
        tail = lax.slice_in_dim(cells, cells.shape[dim] - width, cells.shape[dim], axis=dim)
        cells = jnp.concatenate(
            [
                lax.ppermute(tail, axis, [(i, (i + 1) % count) for i in range(ends)]),
                cells,
                lax.ppermute(head, axis, [((i + 1) % count, i) for i in range(ends)]),
            ],
            axis=dim,
        )
    return cells


def tap_table(tap_values, tap_count):
    tap_reach = tap_values.shape[0] // 2
    offsets = jnp.arange(tap_values.shape[0], dtype=jnp.int32) - tap_reach
    active = (jnp.abs(offsets) <= tap_count[0]).astype(jnp.float32)
    centre = jnp.sum(active * tap_values) / jnp.sum(active)
    return active * (tap_values - centre)


def band_filter(padded, tap_weights, length):
    filtered = tap_weights[0] * padded[0:length]
    for tap_index in range(1, tap_weights.shape[0]):
        filtered = filtered + tap_weights[tap_index] * padded[tap_index : tap_index + length]
    return filtered


def fisher_z(correlation):
    clipped = jnp.clip(correlation, -CLIP_LIMIT, CLIP_LIMIT)
    return 0.5 * (jnp.log1p(clipped) - jnp.log1p(-clipped))


def body(series, tap_values, tap_count, kept_frames, band_start):
    tap_reach = tap_values.shape[0] // 2
    tap_weights = tap_table(tap_values, tap_count)
    block_len = series.shape[0]
    padded = with_halo(series, ((("row", "col"), 0),), tap_reach)
    filtered = band_filter(padded, tap_weights, block_len)
    own_kept = kept_frames[lax.axis_index(("row", "col"))]
    keep_mask = (jnp.arange(block_len, dtype=jnp.int32) < own_kept).astype(jnp.float32)[:, None]
    centered = keep_mask * filtered
    spread = lax.psum(jnp.sum(centered * centered, axis=0), ("row", "col"))
    scaled = (centered * lax.rsqrt(spread + EPSILON)).astype(jnp.bfloat16)
    columns = lax.all_to_all(scaled, ("row", "col"), split_axis=1, concat_axis=0, tiled=True)
    band_slice = lax.dynamic_slice_in_dim(scaled, band_start[0], B, 1)
    band_cols = lax.all_gather(band_slice, ("row", "col"), axis=0, tiled=True)
    correlation = lax.dot_general(
        band_cols, columns, (((0,), (0,)), ((), ())), preferred_element_type=jnp.float32
    )
    return fisher_z(correlation).astype(jnp.bfloat16)


def solution(mesh):
    placed = (P(("subj", "row", "col"), None), P(), P(), P("subj"), P("subj"))
    return jax.shard_map(
        body, mesh=mesh, in_specs=placed, out_specs=P("subj", ("row", "col")), check_vma=False
    )
```

profile of v0, /device:TPU:0, one launch (start us, length us, event | category | flops | bytes accessed | tf_op | source)
XLA Modules:
  0.0 151.6 jit_solution(5790544908060387476)
XLA Ops:
  6.5 0.0 all-gather.2.cloned.1.call-start
  6.5 2.4 %collective-permute-start = (f32[8,11392]{1,0:T(8,128)}, f32[8,11392]{1,0:T(8,128)S(1)}, u32[]{:S(2)}, u32[]{:S(2)}) collective-permute-start(f32[8,11392]{1,0:T(8,128)} %param.5), channel_id=1, source_target_pairs={{0,1},{1,2},{2,3},{3,4},{4,5},{5,6},{6,7},{7,8},{8,9},{9,10},{10,1... | collective-permute-start | bytes 1093640 | tf_op jit(solution)/shard_map/ppermute | solution.py:21
  8.9 1.3 collective-permute-start.1
  10.9 1.3 dynamic_slice.6
  12.1 1.3 convert_reduce_fusion
  13.5 0.6 compare_convert_fusion
  16.1 0.7 subtract_select_fusion
  16.7 0.7 fusion.19
  17.4 0.0 collective-permute-done
  17.5 1.0 constant_dynamic-update-slice_fusion
  18.5 0.0 collective-permute-done.1
  18.6 12.4 %multiply_reduce_fusion = (f32[11392]{0:T(1024)S(1)}, f32[8,11392]{1,0:T(8,128)S(1)}) fusion(f32[8,11392]{1,0:T(8,128)S(1)} %collective-permute-done.1, f32[]{:T(128)} %bitcast.18, f32[16,11392]{1,0:T(8,128)S(1)} %constant_dynamic-update-slice_fusion.2, f32[]{:T(128)} %bitcast.17, f32[]{:T(128)} %bitcast.16, f32[]{:T(128)} %bitcast.15, f32[]{:T(128)} %bitcast.14, ...), kind=kLoop, calls=%fused_computation.33 | loop fusion | flops 3269504 | bytes 6607460 | tf_op jit(solution)/shard_map/reduce_sum | solution.py:59
  31.0 63.9 %psum.7 = f32[11392]{0:T(1024)S(1)} all-reduce(f32[11392]{0:T(1024)S(1)} %get-tuple-element.5), channel_id=1, replica_groups=mesh['subj'=2,'row'=8,'col'=2] {'row','col'}, use_global_device_ids=true, to_apply=%region_3.0 | all-reduce | flops 11392 | bytes 91136 | tf_op jit(solution)/shard_map/psum | solution.py:59
  94.9 0.7 constant_dynamic-slice_fusion
  95.7 0.0 all-gather.2.cloned.1.call-update
  95.7 0.4 all_to_all.14
  96.1 0.1 copy.6
  96.2 12.3 %all_to_all.19 = bf16[8,16,712]{2,0,1:T(8,128)(2,1)S(1)} all-to-all(bf16[8,16,712]{2,0,1:T(8,128)(2,1)S(1)} %copy.6), channel_id=1, replica_groups=mesh['subj'=2,'row'=8,'col'=2] {'row','col'}, dimensions={1} | all-to-all | bytes 364544 | tf_op jit(solution)/shard_map/all_to_all | solution.py:61
  108.5 23.6 %all-gather.2.cloned.1.call-done = bf16[128,4096]{1,0:T(8,128)(2,1)} async-done(((bf16[8,4096]{1,0:T(8,128)(2,1)}), bf16[128,4096]{1,0:T(8,128)(2,1)}) %all-gather.2.cloned.1.call-update) | async-done | bytes 1048592 | tf_op jit(solution)/shard_map/all_gather | solution.py:63
  132.1 12.7 %multiply_convert_fusion = bf16[4096,712]{0,1:T(8,128)(2,1)} fusion(bf16[128,4096]{1,0:T(8,128)(2,1)} %all-gather.2.cloned.1.call-done, bf16[8,16,712]{2,0,1:T(8,128)(2,1)S(1)} %all_to_all.19), kind=kOutput, calls=%fused_computation | convolution fusion | flops 761167872 | bytes 7063552 | tf_op jit(solution)/shard_map/dot_general | solution.py:64
  (4 shorter events, 0.1 us)
Async XLA Ops:
  6.5 125.6 %all-gather.2.cloned.1.call-start = ((), (), s32[]{:S(2)}) async-start(), calls=%async_computation.1 | async-start | bytes 1114112 | tf_op jit(solution)/shard_map/all_gather | solution.py:63
  6.5 10.9 %collective-permute-start = (f32[8,11392]{1,0:T(8,128)}, f32[8,11392]{1,0:T(8,128)S(1)}, u32[]{:S(2)}, u32[]{:S(2)}) collective-permute-start(f32[8,11392]{1,0:T(8,128)} %param.5), channel_id=1, source_target_pairs={{0,1},{1,2},{2,3},{3,4},{4,5},{5,6},{6,7},{7,8},{8,9},{9,10},{10,1... | collective-permute-start | bytes 1093640 | tf_op jit(solution)/shard_map/ppermute | solution.py:21
  8.9 9.6 %collective-permute-start.1 = (f32[8,11392]{1,0:T(8,128)}, f32[8,11392]{1,0:T(8,128)S(1)}, u32[]{:S(2)}, u32[]{:S(2)}) collective-permute-start(f32[8,11392]{1,0:T(8,128)} %param.5), channel_id=1, source_target_pairs={{1,0},{2,1},{3,2},{4,3},{5,4},{6,5},{7,6},{8,7},{9,8},{10,9},{11,1... | collective-permute-start | bytes 1093640 | tf_op jit(solution)/shard_map/ppermute | solution.py:23
Sparse Core Ops, SparseCore 0:
  95.8 36.2 all-gather.1
where the time goes:
time: 152 us
  blocking collectives  76.2 us (50%)
  waiting for transfers between devices  23.6 us (16%)
  between operations  16.1 us (11%)
  other arithmetic  15.1 us (10%)
  matrix products  12.7 us (8%)
  local copies, waits for them, and re-layouts  4.28 us (3%)
  starting transfers between devices  3.66 us (2%)
    psum x1, blocking collectives, body(): spread = lax.psum(jnp.sum(centered * centered, axis=0), ('row', 'col'))  63.9 us
    all_gather x1, waiting for transfers between devices, body(): band_cols = lax.all_gather(band_slice, ('row', 'col'), axis=0, tiled=True)  23.6 us
    dot_general x1, matrix products, body(): lax.dot_general(band_cols, columns, (((0,), (0,)), ((), ())), preferred_e...  12.7 us
    reduce_sum x1, other arithmetic, body(): spread = lax.psum(jnp.sum(centered * centered, axis=0), ('row', 'col'))  12.4 us
    all_to_all x1, blocking collectives, body(): lax.all_to_all(scaled, ('row', 'col'), split_axis=1, concat_axis=0, tiled...  12.3 us
  transfers between devices with their start and end apart: 3, of which 1 were waited for; matrix products, arithmetic and copies ran while one was open for 4% of the time, Pallas kernels for 0%

commit v1 on v0

v1 whole, which is shorter than its diff:
```python
import functools

import jax
import jax.numpy as jnp
from jax import lax
from jax.experimental import pallas as pl
from jax.experimental.pallas import tpu as pltpu
from jax.sharding import PartitionSpec as P

B = 4096
LANES = 128
EPSILON = 1e-06
CLIP_LIMIT = 0.999
AXES = ("row", "col")


def round_up(value, unit):
    return (value + unit - 1) // unit * unit


def band_place(device, n_row):
    row, col = device // 2, device % 2
    return (col * 2 + row % 2) * (n_row // 2) + row // 2


def pack_kernel(n_row, own, own_pad, share, start_ref, series_ref, out_ref, band_ref):
    n_dev = 2 * n_row
    total = series_ref.shape[1]
    start = start_ref[0]
    base = pl.multiple_of(jnp.minimum(start // LANES * LANES, total - B - LANES), LANES)
    rest = start - base
    shift = lax.rem(LANES - rest, LANES)
    lane = lax.broadcasted_iota(jnp.int32, (8, LANES), 1)
    here = lane < LANES - rest
    before = pltpu.roll(series_ref[:, pl.ds(base, LANES)], shift, 1)
    for tile in range(B // LANES):
        after = pltpu.roll(series_ref[:, pl.ds(base + (tile + 1) * LANES, LANES)], shift, 1)
        band_ref[:, tile * LANES : (tile + 1) * LANES] = jnp.where(here, before, after)
        before = after
    for device in range(n_dev):
        place = band_place(device, n_row)
        out_ref[device, :, :own] = series_ref[:, device * own : (device + 1) * own]
        if own_pad > own:
            out_ref[device, :, own:own_pad] = jnp.zeros((8, own_pad - own), jnp.float32)
        out_ref[device, :, own_pad : own_pad + share] = band_ref[:, place * share : (place + 1) * share]


def filter_matrix(kept, frames, taps_ref, count_ref, kept_ref):
    n_taps = taps_ref.shape[0]
    reach = n_taps // 2
    shape = (kept, LANES)
    place = lax.broadcasted_iota(jnp.int32, shape, 0)

    def skip(block, carry):
        frame, seen = carry
        seen = seen + kept_ref[block]
        return frame + jnp.where(place >= seen, 8 - kept_ref[block], 0), seen

    frame, _ = lax.fori_loop(0, frames // 8, skip, (place, jnp.int32(0)), unroll=frames <= 128)
    reach_used = count_ref[0]
    tap_sum = jnp.float32(0)
    tap_number = jnp.float32(0)
    for tap in range(n_taps):
        used = abs(tap - reach) <= reach_used
        tap_sum = tap_sum + jnp.where(used, taps_ref[tap], 0.0)
        tap_number = tap_number + jnp.where(used, 1.0, 0.0)
    centre = jnp.full(shape, tap_sum, jnp.float32) / jnp.full(shape, tap_number, jnp.float32)
    pieces = []
    for tile in range(frames // LANES):
        offset = lax.broadcasted_iota(jnp.int32, shape, 1) + tile * LANES - frame
        value = jnp.zeros(shape, jnp.float32)
        for tap in range(n_taps):
            value = jnp.where(offset == tap - reach, taps_ref[tap], value)
        pieces.append(jnp.where(jnp.abs(offset) <= reach_used, value - centre, 0.0))
    return pieces[0] if len(pieces) == 1 else jnp.concatenate(pieces, 1)


def scale_kernel(own, own_pad, taps_ref, count_ref, kept_ref, raw_ref, own_ref, band_ref):
    kept = band_ref.shape[0]
    frames = raw_ref.shape[0]
    matrix = filter_matrix(kept, frames, taps_ref, count_ref, kept_ref)
    centered = jnp.dot(
        matrix, raw_ref[...], precision=lax.Precision.HIGHEST, preferred_element_type=jnp.float32
    )
    spread = jnp.sum(centered * centered, axis=0, keepdims=True)
    scaled = centered * lax.rsqrt(spread + EPSILON)
    own_ref[...] = scaled[:, :own_pad].T[:own].astype(jnp.bfloat16)
    band_ref[...] = scaled[:, own_pad : own_pad + band_ref.shape[1]].astype(jnp.bfloat16)


def fisher_kernel(place_ref, own_ref, a_ref, b_ref, c_ref, d_ref, out_ref):
    share = a_ref.shape[2]
    z = place_ref[0]
    for k, ref in enumerate((a_ref, b_ref, c_ref, d_ref)):
        @pl.when(pl.program_id(0) == k)
        def _(ref=ref):
            for step in range(ref.shape[0]):
                correlation = jnp.dot(
                    own_ref[...], ref[step], preferred_element_type=jnp.float32
                )
                clipped = jnp.clip(correlation, -CLIP_LIMIT, CLIP_LIMIT)
                z_value = 0.5 * (jnp.log(1.0 + clipped) - jnp.log(1.0 - clipped))
                where = pl.multiple_of((z ^ step) * share, share)
                out_ref[:, pl.ds(where, share)] = z_value.astype(jnp.bfloat16)


def body(series, tap_values, tap_count, kept_frames, band_start):
    n_row = lax.axis_size("row")
    n_dev = n_row * lax.axis_size("col")
    frames = 8 * n_dev
    kept = frames * 3 // 4
    own = series.shape[1] // n_dev
    own_pad = round_up(own, LANES)
    share = B // n_dev
    width = own_pad + round_up(share, LANES)
    n_quarter = n_row // 2
    smem = pl.BlockSpec(memory_space=pltpu.SMEM)
    vmem = pl.BlockSpec(memory_space=pltpu.VMEM)

    packed = pl.pallas_call(
        functools.partial(pack_kernel, n_row, own, own_pad, share),
        out_shape=jax.ShapeDtypeStruct((n_dev, 8, width), jnp.float32),
        in_specs=[smem, vmem],
        out_specs=vmem,
        scratch_shapes=[pltpu.VMEM((8, B), jnp.float32)],
        compiler_params=pltpu.CompilerParams(vmem_limit_bytes=48 << 20),
    )(band_start, series)
    raw = lax.all_to_all(packed, AXES, 0, 0, tiled=True).reshape(frames, width)
    own_rows, block = pl.pallas_call(
        functools.partial(scale_kernel, own, own_pad),
        out_shape=(
            jax.ShapeDtypeStruct((own, kept), jnp.bfloat16),
            jax.ShapeDtypeStruct((kept, share), jnp.bfloat16),
        ),
        in_specs=[smem, smem, smem, vmem],
        out_specs=(vmem, vmem),
        compiler_params=pltpu.CompilerParams(vmem_limit_bytes=48 << 20),
    )(tap_values, tap_count, kept_frames, raw)

    def swap_row(x, bits):
        return lax.ppermute(x, "row", [(i, i ^ bits) for i in range(n_row)])

    def swap_col(x):
        return lax.ppermute(x, "col", [(0, 1), (1, 0)])

    row, col = lax.axis_index("row"), lax.axis_index("col")
    first = row // 2
    line = jnp.stack([block] + [swap_row(block, 2 * step) for step in range(1, n_quarter)])
    if share % LANES:
        line = jnp.take(line, jnp.arange(n_quarter, dtype=jnp.int32) ^ first, axis=0)
        line = line.transpose(1, 0, 2).reshape(1, kept, n_quarter * share)
        first = jnp.zeros_like(first)
    line_y = swap_row(line, 1)
    line_c = swap_col(line)
    line_yc = swap_col(line_y)

    place = jnp.stack([first, col * 2 + row % 2]).astype(jnp.int32)
    out = pl.pallas_call(
        fisher_kernel,
        out_shape=jax.ShapeDtypeStruct((own, B), jnp.bfloat16),
        grid_spec=pltpu.PrefetchScalarGridSpec(
            num_scalar_prefetch=1,
            grid=(4,),
            in_specs=[vmem] * 5,
            out_specs=pl.BlockSpec((own, B // 4), lambda k, p: (0, p[1] ^ k)),
        ),
        compiler_params=pltpu.CompilerParams(vmem_limit_bytes=48 << 20),
    )(place, own_rows, line, line_y, line_c, line_yc)
    return out.T


def solution(mesh):
    placed = (P(("subj", "row", "col"), None), P(), P(), P("subj"), P("subj"))
    return jax.shard_map(
        body, mesh=mesh, in_specs=placed, out_specs=P("subj", ("row", "col")), check_vma=False
    )
```

time: 152 us -> 50 us (0.33)
  blocking collectives: 76.2 us -> 0 us
  other arithmetic: 15.1 us -> 0.1 us
  between operations: 16.1 us -> 1.34 us
  matrix products: 12.7 us -> 0 us
  starting transfers between devices: 3.66 us -> 13 us
  Pallas kernels: 0 us -> 8.65 us
  local copies, waits for them, and re-layouts: 4.28 us -> 2.29 us
    psum x1 -> x0, blocking collectives: 63.9 us -> none  [body(): spread = lax.psum(jnp.sum(centered * centered, axis=0), ('row', 'col'))]
    all_gather x1 -> x0, waiting for transfers between devices: 23.6 us -> none  [body(): band_cols = lax.all_gather(band_slice, ('row', 'col'), axis=0, tiled=True)]
    all_to_all x0 -> x1, waiting for transfers between devices: none -> 13.8 us  [body(): raw = lax.all_to_all(packed, AXES, 0, 0, tiled=True).reshape(frames, width)]
    reduce_sum x2 -> x0, other arithmetic: 13.7 us -> none  [the longest x1 12.4 us: body(): spread = lax.psum(jnp.sum(centered * centered, axis=0), ('row', 'col'))]
    dot_general x1 -> x0, matrix products: 12.7 us -> none  [body(): lax.dot_general(band_cols, columns, (((0,), (0,)), ((), ())), preferred_e...]
    all_to_all x1 -> x0, blocking collectives: 12.3 us -> none  [body(): lax.all_to_all(scaled, ('row', 'col'), split_axis=1, concat_axis=0, tiled...]
    ppermute x2 -> x6, waiting for transfers between devices: 0.01 us -> 10.5 us  [the longest x4 9.14 us: swap_row(): return lax.ppermute(x, 'row', [(i, i ^ bits) for i in range(n_row)])]
    pallas_call x0 -> x3, Pallas kernels: none -> 8.65 us  [the longest x1 6.32 us: body(): pl.pallas_call(fisher_kernel, out_shape=jax.ShapeDtypeStruct((own, B), jn...]
  transfers between devices with their start and end apart: 3 -> 7, of which waited for: 1 -> 5; matrix products, arithmetic and copies ran while one was open for 4% -> 0% of each run, Pallas kernels for 0% -> 0%
where the time goes in v1:
time: 50 us; the launch traced here: 49.7 us
  waiting for transfers between devices  24.3 us (49%)
  starting transfers between devices  13 us (26%)
  Pallas kernels  8.65 us (17%)
  local copies, waits for them, and re-layouts  2.29 us (5%)
  between operations  1.34 us (3%)
    all_to_all x1, waiting for transfers between devices, body(): raw = lax.all_to_all(packed, AXES, 0, 0, tiled=True).reshape(frames, width)  13.8 us
    ppermute x4, waiting for transfers between devices, swap_row(): return lax.ppermute(x, 'row', [(i, i ^ bits) for i in range(n_row)])  9.14 us
    all_to_all x1, starting transfers between devices, body(): raw = lax.all_to_all(packed, AXES, 0, 0, tiled=True).reshape(frames, width)  7.39 us
    pallas_call x1, Pallas kernels, body(): pl.pallas_call(fisher_kernel, out_shape=jax.ShapeDtypeStruct((own, B), jn...  6.32 us
    ppermute x4, starting transfers between devices, swap_row(): return lax.ppermute(x, 'row', [(i, i ^ bits) for i in range(n_row)])  5.58 us
    unnamed x6, local copies, waits for them, and re-layouts  2.29 us
    ppermute x2, waiting for transfers between devices, swap_col(): return lax.ppermute(x, 'col', [(0, 1), (1, 0)])  1.36 us
    pallas_call x1, Pallas kernels, body(): pl.pallas_call(functools.partial(scale_kernel, own, own_pad), out_shape=(...  1.32 us
  transfers between devices with their start and end apart: 7, of which 5 were waited for; matrix products, arithmetic and copies ran while one was open for 0% of the time, Pallas kernels for 0%

profile of v1, /device:TPU:0, one launch (start us, length us, event | category | flops | bytes accessed | tf_op | source)
XLA Modules:
  0.0 49.7 jit_solution(7960263808796263320)
XLA Ops:
  0.7 0.0 copy-start
  0.7 1.0 %copy-done = f32[8,11392]{1,0:T(8,128)S(1)} copy-done((f32[8,11392]{1,0:T(8,128)S(1)}, f32[8,11392]{1,0:T(8,128)}, u32[]{:S(2)}) %copy-start) | copy-done | bytes 364568
  1.6 1.0 %shard_map.55 = f32[16,8,1024]{2,1,0:T(8,128)} custom-call(s32[1]{0:T(128)S(6)} %copy.7.start_ref, f32[8,11392]{1,0:T(8,128)S(1)} %copy-done), custom_call_target="tpu_custom_call" | custom-call | tf_op jit(solution)/shard_map/pallas_call | solution.py:120
  2.6 7.4 %all-to-all-start = ((f32[16,8,1024]{2,1,0:T(8,128)}), f32[16,8,1024]{2,1,0:T(8,128)S(1)}, u32[]{:S(2)}, u32[]{:S(2)}) async-start(f32[16,8,1024]{2,1,0:T(8,128)} %shard_map.55), calls=%async_computation | async-start | bytes 1048576 | tf_op jit(solution)/shard_map/all_to_all | solution.py:128
  10.7 13.8 %all-to-all-done = f32[16,8,1024]{2,1,0:T(8,128)S(1)} async-done(((f32[16,8,1024]{2,1,0:T(8,128)}), f32[16,8,1024]{2,1,0:T(8,128)S(1)}, u32[]{:S(2)}, u32[]{:S(2)}) %all-to-all-start) | async-done | bytes 524320 | tf_op jit(solution)/shard_map/all_to_all | solution.py:128
  24.5 0.0 copy-start.1
  24.5 0.7 %copy-done.1 = f32[17]{0:T(128)S(1)} copy-done((f32[17]{0:T(128)S(1)}, f32[17]{0:T(128)}, u32[]{:S(2)}) %copy-start.1) | copy-done | bytes 92
  25.2 0.0 copy-start.2
  25.2 0.7 %copy-done.2 = s32[16]{0:T(128)S(1)} copy-done((s32[16]{0:T(128)S(1)}, s32[16]{0:T(128)}, u32[]{:S(2)}) %copy-start.2) | copy-done | bytes 88
  25.8 1.3 %shard_map.56 = (bf16[712,96]{1,0:T(8,128)(2,1)S(1)}, bf16[96,256]{1,0:T(8,128)(2,1)S(1)}) custom-call(f32[17]{0:T(128)S(1)} %copy-done.1, s32[1]{0:T(128)S(6)} %copy.6.count_ref, s32[16]{0:T(128)S(1)} %copy-done.2, f32[128,1024]{1,0:T(8,128)S(1)} %bitcast.8), custom_call_target="tpu_custom_call" | custom-call | tf_op jit(solution)/shard_map/pallas_call | solution.py:129
  27.1 1.4 %collective-permute-start.2 = (bf16[96,256]{1,0:T(8,128)(2,1)S(1)}, bf16[96,256]{1,0:T(8,128)(2,1)S(1)}, u32[]{:S(2)}, u32[]{:S(2)}) collective-permute-start(bf16[96,256]{1,0:T(8,128)(2,1)S(1)} %get-tuple-element.8), channel_id=1, source_target_pairs={{0,12},{2,14},{4,8},{6,10},{8,4},{10,6},{12,0},{14,2},{1,13},{3,15... | collective-permute-start | bytes 147464 | tf_op jit(solution)/shard_map/ppermute | solution.py:141
  28.6 1.2 %collective-permute-start.1 = (bf16[96,256]{1,0:T(8,128)(2,1)S(1)}, bf16[96,256]{1,0:T(8,128)(2,1)S(1)}, u32[]{:S(2)}, u32[]{:S(2)}) collective-permute-start(bf16[96,256]{1,0:T(8,128)(2,1)S(1)} %get-tuple-element.8), channel_id=1, source_target_pairs={{0,8},{2,10},{4,12},{6,14},{8,0},{10,2},{12,4},{14,6},{1,9},{3,11}... | collective-permute-start | bytes 147464 | tf_op jit(solution)/shard_map/ppermute | solution.py:141
  29.8 1.8 %collective-permute-start = (bf16[96,256]{1,0:T(8,128)(2,1)S(1)}, bf16[96,256]{1,0:T(8,128)(2,1)S(1)}, u32[]{:S(2)}, u32[]{:S(2)}) collective-permute-start(bf16[96,256]{1,0:T(8,128)(2,1)S(1)} %get-tuple-element.8), channel_id=1, source_target_pairs={{0,4},{2,6},{4,0},{6,2},{8,12},{10,14},{12,8},{14,10},{1,5},{3,7},... | collective-permute-start | bytes 147464 | tf_op jit(solution)/shard_map/ppermute | solution.py:141
  31.6 1.8 %collective-permute-done.2 = bf16[96,256]{1,0:T(8,128)(2,1)S(1)} collective-permute-done((bf16[96,256]{1,0:T(8,128)(2,1)S(1)}, bf16[96,256]{1,0:T(8,128)(2,1)S(1)}, u32[]{:S(2)}, u32[]{:S(2)}) %collective-permute-start.2) | collective-permute-done | bytes 49184 | tf_op jit(solution)/shard_map/ppermute | solution.py:141
  33.4 1.8 %collective-permute-done.1 = bf16[96,256]{1,0:T(8,128)(2,1)S(1)} collective-permute-done((bf16[96,256]{1,0:T(8,128)(2,1)S(1)}, bf16[96,256]{1,0:T(8,128)(2,1)S(1)}, u32[]{:S(2)}, u32[]{:S(2)}) %collective-permute-start.1) | collective-permute-done | bytes 49184 | tf_op jit(solution)/shard_map/ppermute | solution.py:141
  35.2 0.0 collective-permute-done
  35.2 1.1 %collective-permute-start.3 = (bf16[4,96,256]{2,1,0:T(8,128)(2,1)S(1)}, bf16[4,96,256]{2,1,0:T(8,128)(2,1)S(1)}, u32[]{:S(2)}, u32[]{:S(2)}) collective-permute-start(bf16[4,96,256]{2,1,0:T(8,128)(2,1)S(1)} %pad_maximum_fusion.a_ref), channel_id=1, source_target_pairs={{0,2},{2,0},{4,6},{6,4},{8,10},{10,8},{12,14},{14,12},{1,3},{3,1},... | collective-permute-start | bytes 589832 | tf_op jit(solution)/shard_map/ppermute | solution.py:141
  36.4 0.0 collective-permute-start.4
  36.4 5.5 %collective-permute-done.3.b_ref = bf16[4,96,256]{2,1,0:T(8,128)(2,1)S(1)} collective-permute-done((bf16[4,96,256]{2,1,0:T(8,128)(2,1)S(1)}, bf16[4,96,256]{2,1,0:T(8,128)(2,1)S(1)}, u32[]{:S(2)}, u32[]{:S(2)}) %collective-permute-start.3) | collective-permute-done | bytes 196640 | tf_op jit(solution)/shard_map/ppermute | solution.py:141
  41.9 0.0 collective-permute-start.5
  41.9 0.1 pad_add_fusion.place_ref
  42.0 0.0 collective-permute-done.4.c_ref
  42.0 1.4 %collective-permute-done.5.d_ref = bf16[4,96,256]{2,1,0:T(8,128)(2,1)S(1)} collective-permute-done((bf16[4,96,256]{2,1,0:T(8,128)(2,1)S(1)}, bf16[4,96,256]{2,1,0:T(8,128)(2,1)S(1)}, u32[]{:S(2)}, u32[]{:S(2)}) %collective-permute-start.5) | collective-permute-done | bytes 196640 | tf_op jit(solution)/shard_map/ppermute | solution.py:144
  43.3 6.3 %shard_map.57 = bf16[712,4096]{1,0:T(8,128)(2,1)} custom-call(s32[2]{0:T(128)S(1)} %pad_add_fusion.place_ref, bf16[712,96]{1,0:T(8,128)(2,1)S(1)} %get-tuple-element.7.own_ref, bf16[4,96,256]{2,1,0:T(8,128)(2,1)S(1)} %pad_maximum_fusion.a_ref, bf16[4,96,256]{2,1,0:T(8,128)(2,1)S(1)} %collective-permute-done.3.b_ref, ...), custom_call_target="tpu_custom_call" | custom-call | tf_op jit(solution)/shard_map/pallas_call | solution.py:158
  (1 shorter events, 0.0 us)
Async XLA Ops:
  0.7 1.0 %copy-start = (f32[8,11392]{1,0:T(8,128)S(1)}, f32[8,11392]{1,0:T(8,128)}, u32[]{:S(2)}) copy-start(f32[8,11392]{1,0:T(8,128)} %series_ref.1) | copy-start | bytes 1093636
  2.6 21.9 %all-to-all-start = ((f32[16,8,1024]{2,1,0:T(8,128)}), f32[16,8,1024]{2,1,0:T(8,128)S(1)}, u32[]{:S(2)}, u32[]{:S(2)}) async-start(f32[16,8,1024]{2,1,0:T(8,128)} %shard_map.55), calls=%async_computation | async-start | bytes 1048576 | tf_op jit(solution)/shard_map/all_to_all | solution.py:128
  24.5 0.7 %copy-start.1 = (f32[17]{0:T(128)S(1)}, f32[17]{0:T(128)}, u32[]{:S(2)}) copy-start(f32[17]{0:T(128)} %taps_ref.1) | copy-start | bytes 208
  25.2 0.7 %copy-start.2 = (s32[16]{0:T(128)S(1)}, s32[16]{0:T(128)}, u32[]{:S(2)}) copy-start(s32[16]{0:T(128)} %kept_ref.1) | copy-start | bytes 196
  27.1 6.2 %collective-permute-start.2 = (bf16[96,256]{1,0:T(8,128)(2,1)S(1)}, bf16[96,256]{1,0:T(8,128)(2,1)S(1)}, u32[]{:S(2)}, u32[]{:S(2)}) collective-permute-start(bf16[96,256]{1,0:T(8,128)(2,1)S(1)} %get-tuple-element.8), channel_id=1, source_target_pairs={{0,12},{2,14},{4,8},{6,10},{8,4},{10,6},{12,0},{14,2},{1,13},{3,15... | collective-permute-start | bytes 147464 | tf_op jit(solution)/shard_map/ppermute | solution.py:141
  28.6 6.6 %collective-permute-start.1 = (bf16[96,256]{1,0:T(8,128)(2,1)S(1)}, bf16[96,256]{1,0:T(8,128)(2,1)S(1)}, u32[]{:S(2)}, u32[]{:S(2)}) collective-permute-start(bf16[96,256]{1,0:T(8,128)(2,1)S(1)} %get-tuple-element.8), channel_id=1, source_target_pairs={{0,8},{2,10},{4,12},{6,14},{8,0},{10,2},{12,4},{14,6},{1,9},{3,11}... | collective-permute-start | bytes 147464 | tf_op jit(solution)/shard_map/ppermute | solution.py:141
  29.8 5.4 %collective-permute-start = (bf16[96,256]{1,0:T(8,128)(2,1)S(1)}, bf16[96,256]{1,0:T(8,128)(2,1)S(1)}, u32[]{:S(2)}, u32[]{:S(2)}) collective-permute-start(bf16[96,256]{1,0:T(8,128)(2,1)S(1)} %get-tuple-element.8), channel_id=1, source_target_pairs={{0,4},{2,6},{4,0},{6,2},{8,12},{10,14},{12,8},{14,10},{1,5},{3,7},... | collective-permute-start | bytes 147464 | tf_op jit(solution)/shard_map/ppermute | solution.py:141
  35.2 6.7 %collective-permute-start.3 = (bf16[4,96,256]{2,1,0:T(8,128)(2,1)S(1)}, bf16[4,96,256]{2,1,0:T(8,128)(2,1)S(1)}, u32[]{:S(2)}, u32[]{:S(2)}) collective-permute-start(bf16[4,96,256]{2,1,0:T(8,128)(2,1)S(1)} %pad_maximum_fusion.a_ref), channel_id=1, source_target_pairs={{0,2},{2,0},{4,6},{6,4},{8,10},{10,8},{12,14},{14,12},{1,3},{3,1},... | collective-permute-start | bytes 589832 | tf_op jit(solution)/shard_map/ppermute | solution.py:141
  36.4 5.6 %collective-permute-start.4 = (bf16[4,96,256]{2,1,0:T(8,128)(2,1)S(1)}, bf16[4,96,256]{2,1,0:T(8,128)(2,1)S(1)}, u32[]{:S(2)}, u32[]{:S(2)}) collective-permute-start(bf16[4,96,256]{2,1,0:T(8,128)(2,1)S(1)} %pad_maximum_fusion.a_ref), channel_id=1, source_target_pairs={{0,1},{1,0},{2,3},{3,2},{4,5},{5,4},{6,7},{7,6},{8,9},{9,8},{10,11... | collective-permute-start | bytes 589832 | tf_op jit(solution)/shard_map/ppermute | solution.py:144
  41.9 1.4 %collective-permute-start.5 = (bf16[4,96,256]{2,1,0:T(8,128)(2,1)S(1)}, bf16[4,96,256]{2,1,0:T(8,128)(2,1)S(1)}, u32[]{:S(2)}, u32[]{:S(2)}) collective-permute-start(bf16[4,96,256]{2,1,0:T(8,128)(2,1)S(1)} %collective-permute-done.3.b_ref), channel_id=1, source_target_pairs={{0,1},{1,0},{2,3},{3,2},{4,5},{5,4},{6,7},{7,6},{8,9},{9,8},{10,11... | collective-permute-start | bytes 589832 | tf_op jit(solution)/shard_map/ppermute | solution.py:144

commit v2 on v1

v2 whole, which is shorter than its diff:
```python
import functools

import jax
import jax.numpy as jnp
from jax import lax
from jax.experimental import pallas as pl
from jax.experimental.pallas import tpu as pltpu
from jax.sharding import PartitionSpec as P

B = 4096
LANES = 128
EPSILON = 1e-06
CLIP_LIMIT = 0.999
AXES = ("row", "col")


def round_up(value, unit):
    return (value + unit - 1) // unit * unit


def band_place(device, n_row):
    row, col = device // 2, device % 2
    return (col * 2 + row % 2) * (n_row // 2) + row // 2


def pack_band_kernel(n_row, share, start_ref, series_ref, out_ref, window_ref, band_ref, sem):
    total = series_ref.shape[1]
    start = start_ref[0]
    base = pl.multiple_of(jnp.minimum(start // LANES * LANES, total - B - LANES), LANES)
    rest = start - base
    shift = lax.rem(LANES - rest, LANES)
    load = pltpu.make_async_copy(series_ref.at[:, pl.ds(base, B + LANES)], window_ref, sem)
    load.start()
    lane = lax.broadcasted_iota(jnp.int32, (8, LANES), 1)
    here = lane < LANES - rest
    load.wait()
    before = pltpu.roll(window_ref[:, :LANES], shift, 1)
    for tile in range(B // LANES):
        after = pltpu.roll(window_ref[:, (tile + 1) * LANES : (tile + 2) * LANES], shift, 1)
        band_ref[:, tile * LANES : (tile + 1) * LANES] = jnp.where(here, before, after)
        before = after
    for device in range(2 * n_row):
        place = band_place(device, n_row)
        out_ref[device, :, :share] = band_ref[:, place * share : (place + 1) * share]


def pack_own_kernel(own, taps_ref, count_ref, kept_ref, series_ref, out_ref, matrix_ref):
    kept, frames = matrix_ref.shape
    matrix_ref[...] = filter_matrix(kept, frames, taps_ref, count_ref, kept_ref)
    own_pad = out_ref.shape[2]
    for device in range(out_ref.shape[0]):
        out_ref[device, :, :own] = series_ref[:, device * own : (device + 1) * own]
        if own_pad > own:
            out_ref[device, :, own:] = jnp.zeros((8, own_pad - own), jnp.float32)


def filter_matrix(kept, frames, taps_ref, count_ref, kept_ref):
    n_taps = taps_ref.shape[0]
    reach = n_taps // 2
    shape = (kept, LANES)
    place = lax.broadcasted_iota(jnp.int32, shape, 0)

    def skip(block, carry):
        frame, seen = carry
        seen = seen + kept_ref[block]
        return frame + jnp.where(place >= seen, 8 - kept_ref[block], 0), seen

    frame, _ = lax.fori_loop(0, frames // 8, skip, (place, jnp.int32(0)), unroll=frames <= 128)
    reach_used = count_ref[0]
    tap_sum = jnp.float32(0)
    tap_number = jnp.float32(0)
    for tap in range(n_taps):
        used = abs(tap - reach) <= reach_used
        tap_sum = tap_sum + jnp.where(used, taps_ref[tap], 0.0)
        tap_number = tap_number + jnp.where(used, 1.0, 0.0)
    centre = jnp.full(shape, tap_sum, jnp.float32) / jnp.full(shape, tap_number, jnp.float32)
    pieces = []
    for tile in range(frames // LANES):
        offset = lax.broadcasted_iota(jnp.int32, shape, 1) + tile * LANES - frame
        value = jnp.zeros(shape, jnp.float32)
        for tap in range(n_taps):
            value = jnp.where(offset == tap - reach, taps_ref[tap], value)
        pieces.append(jnp.where(jnp.abs(offset) <= reach_used, value - centre, 0.0))
    return pieces[0] if len(pieces) == 1 else jnp.concatenate(pieces, 1)


def scaled_columns(matrix_ref, raw_ref):
    centered = jnp.dot(
        matrix_ref[...],
        raw_ref[...],
        precision=lax.Precision.HIGHEST,
        preferred_element_type=jnp.float32,
    )
    spread = jnp.sum(centered * centered, axis=0, keepdims=True)
    return centered * lax.rsqrt(spread + EPSILON)


def scale_band_kernel(matrix_ref, raw_ref, band_ref):
    scaled = scaled_columns(matrix_ref, raw_ref)
    band_ref[...] = scaled[:, : band_ref.shape[1]].astype(jnp.bfloat16)


def scale_own_kernel(matrix_ref, raw_ref, own_ref):
    scaled = scaled_columns(matrix_ref, raw_ref)
    own_ref[...] = scaled.T[: own_ref.shape[0]].astype(jnp.bfloat16)


def fisher_kernel(place_ref, own_ref, line_ref, *refs):
    out_ref = refs[-1]
    blocks, _, width = line_ref.shape
    z = place_ref[0] % blocks
    for step in range(blocks):
        correlation = jnp.dot(own_ref[...], line_ref[step], preferred_element_type=jnp.float32)
        clipped = jnp.clip(correlation, -CLIP_LIMIT, CLIP_LIMIT)
        z_value = 0.5 * (jnp.log(1.0 + clipped) - jnp.log(1.0 - clipped))
        where = pl.multiple_of((z ^ step) * width, width)
        out_ref[:, pl.ds(where, width)] = z_value.astype(jnp.bfloat16)


def fisher_quarter(place, own_rows, line, out, k):
    blocks, kept, width = line.shape
    parts = 2 if blocks % 2 == 0 else 1
    step_blocks = blocks // parts
    own = own_rows.shape[0]
    specs = [
        pl.BlockSpec((own, kept), lambda j, p: (0, 0)),
        pl.BlockSpec((step_blocks, kept, width), lambda j, p: (j, 0, 0)),
    ]
    args = [place, own_rows, line]
    aliases = {}
    if out is not None:
        specs.append(pl.BlockSpec(memory_space=pl.ANY))
        args.append(out)
        aliases = {3: 0}
    return pl.pallas_call(
        fisher_kernel,
        out_shape=jax.ShapeDtypeStruct((own, B), jnp.bfloat16),
        grid_spec=pltpu.PrefetchScalarGridSpec(
            num_scalar_prefetch=1,
            grid=(parts,),
            in_specs=specs,
            out_specs=pl.BlockSpec(
                (own, B // 4 // parts),
                lambda j, p: (0, (p[1] ^ k) * parts + ((p[0] // step_blocks) ^ j)),
            ),
        ),
        input_output_aliases=aliases,
        compiler_params=pltpu.CompilerParams(vmem_limit_bytes=48 << 20),
    )(*args)


def body(series, tap_values, tap_count, kept_frames, band_start):
    n_row = lax.axis_size("row")
    n_dev = n_row * lax.axis_size("col")
    frames = 8 * n_dev
    kept = frames * 3 // 4
    own = series.shape[1] // n_dev
    own_pad = round_up(own, LANES)
    share = B // n_dev
    share_pad = round_up(share, LANES)
    n_quarter = n_row // 2
    smem = pl.BlockSpec(memory_space=pltpu.SMEM)
    vmem = pl.BlockSpec(memory_space=pltpu.VMEM)
    params = pltpu.CompilerParams(vmem_limit_bytes=48 << 20)

    packed_band = pl.pallas_call(
        functools.partial(pack_band_kernel, n_row, share),
        out_shape=jax.ShapeDtypeStruct((n_dev, 8, share_pad), jnp.float32),
        in_specs=[smem, pl.BlockSpec(memory_space=pltpu.HBM)],
        out_specs=vmem,
        scratch_shapes=[
            pltpu.VMEM((8, B + LANES), jnp.float32),
            pltpu.VMEM((8, B), jnp.float32),
            pltpu.SemaphoreType.DMA,
        ],
        compiler_params=params,
    )(band_start, series)
    raw_band = lax.all_to_all(packed_band, AXES, 0, 0, tiled=True).reshape(frames, share_pad)
    packed_own, matrix = pl.pallas_call(
        functools.partial(pack_own_kernel, own),
        out_shape=(
            jax.ShapeDtypeStruct((n_dev, 8, own_pad), jnp.float32),
            jax.ShapeDtypeStruct((kept, frames), jnp.float32),
        ),
        in_specs=[smem, smem, smem, vmem],
        out_specs=(vmem, vmem),
        compiler_params=params,
    )(tap_values, tap_count, kept_frames, series)
    raw_own = lax.all_to_all(packed_own, AXES, 0, 0, tiled=True).reshape(frames, own_pad)
    block = pl.pallas_call(
        scale_band_kernel,
        out_shape=jax.ShapeDtypeStruct((kept, share), jnp.bfloat16),
        in_specs=[vmem, vmem],
        out_specs=vmem,
        compiler_params=params,
    )(matrix, raw_band)

    def swap_row(x, bits):
        return lax.ppermute(x, "row", [(i, i ^ bits) for i in range(n_row)])

    def swap_col(x):
        return lax.ppermute(x, "col", [(0, 1), (1, 0)])

    row, col = lax.axis_index("row"), lax.axis_index("col")
    first = row // 2
    line = jnp.stack([block] + [swap_row(block, 2 * step) for step in range(1, n_quarter)])
    if share % LANES:
        line = jnp.take(line, jnp.arange(n_quarter, dtype=jnp.int32) ^ first, axis=0)
        line = line.transpose(1, 0, 2).reshape(1, kept, n_quarter * share)
        first = jnp.zeros_like(first)
    line_y = swap_row(line, 1)
    line_c = swap_col(line)
    line_yc = swap_col(line_y)

    own_rows = pl.pallas_call(
        scale_own_kernel,
        out_shape=jax.ShapeDtypeStruct((own, kept), jnp.bfloat16),
        in_specs=[vmem, vmem],
        out_specs=vmem,
        compiler_params=params,
    )(matrix, raw_own)
    place = jnp.stack([first, col * 2 + row % 2]).astype(jnp.int32)
    out = fisher_quarter(place, own_rows, line, None, 0)
    out = fisher_quarter(place, own_rows, line_c, out, 2)
    out = fisher_quarter(place, own_rows, line_y, out, 1)
    out = fisher_quarter(place, own_rows, line_yc, out, 3)
    return out.T


def solution(mesh):
    placed = (P(("subj", "row", "col"), None), P(), P(), P("subj"), P("subj"))
    return jax.shard_map(
        body, mesh=mesh, in_specs=placed, out_specs=P("subj", ("row", "col")), check_vma=False
    )
```

time: 50 us -> 55.4 us (1.11)
  Pallas kernels: 8.65 us -> 13.9 us
  waiting for transfers between devices: 24.3 us -> 19.3 us
  starting transfers between devices: 13 us -> 16.9 us
  local copies, waits for them, and re-layouts: 2.29 us -> 3.27 us
    all_to_all x1 -> x2, waiting for transfers between devices: 13.8 us -> 3.53 us  [the longest x1 3.53 us: body(): lax.all_to_all(packed_band, AXES, 0, 0, tiled=True)]
    ppermute x4, waiting for transfers between devices: 9.14 us -> 15.8 us  [swap_row(): return lax.ppermute(x, 'row', [(i, i ^ bits) for i in range(n_row)])]
    pallas_call x3 -> x8, Pallas kernels: 8.65 us -> 13.9 us  [the longest x4 10.8 us: fisher_quarter(): pl.pallas_call(fisher_kernel, out_shape=jax.ShapeDtypeStruct((own, B), jn...]
    all_to_all x1 -> x2, starting transfers between devices: 7.39 us -> 11 us  [the longest x1 7.4 us: body(): lax.all_to_all(packed_band, AXES, 0, 0, tiled=True)]
    ppermute x2, waiting for transfers between devices: 1.36 us -> 0.01 us  [swap_col(): return lax.ppermute(x, 'col', [(0, 1), (1, 0)])]
    unnamed x6 -> x8, local copies, waits for them, and re-layouts: 2.29 us -> 3.27 us
  transfers between devices with their start and end apart: 7 -> 8, of which waited for: 5 -> 4; matrix products, arithmetic and copies ran while one was open for 0% -> 0% of each run, Pallas kernels for 0% -> 19%
where the time goes in v2:
time: 55.4 us; the launch traced here: 55 us
  waiting for transfers between devices  19.3 us (35%)
  starting transfers between devices  16.9 us (31%)
  Pallas kernels  13.9 us (25%)
  local copies, waits for them, and re-layouts  3.27 us (6%)
  between operations  1.37 us (2%)
    ppermute x4, waiting for transfers between devices, swap_row(): return lax.ppermute(x, 'row', [(i, i ^ bits) for i in range(n_row)])  15.8 us
    pallas_call x4, Pallas kernels, fisher_quarter(): pl.pallas_call(fisher_kernel, out_shape=jax.ShapeDtypeStruct((own, B), jn...  10.8 us
    all_to_all x1, starting transfers between devices, body(): lax.all_to_all(packed_band, AXES, 0, 0, tiled=True)  7.4 us
    ppermute x4, starting transfers between devices, swap_row(): return lax.ppermute(x, 'row', [(i, i ^ bits) for i in range(n_row)])  5.99 us
    all_to_all x1, starting transfers between devices, body(): lax.all_to_all(packed_own, AXES, 0, 0, tiled=True).reshape(frames, own_pad)  3.55 us
    all_to_all x1, waiting for transfers between devices, body(): lax.all_to_all(packed_band, AXES, 0, 0, tiled=True)  3.53 us
    unnamed x8, local copies, waits for them, and re-layouts  3.27 us
    pallas_call x1, Pallas kernels, body(): pl.pallas_call(functools.partial(pack_own_kernel, own), out_shape=(jax.Sh...  1.46 us
  transfers between devices with their start and end apart: 8, of which 4 were waited for; matrix products, arithmetic and copies ran while one was open for 0% of the time, Pallas kernels for 19%

profile of v2, /device:TPU:0, one launch (start us, length us, event | category | flops | bytes accessed | tf_op | source)
XLA Modules:
  0.0 55.0 jit_solution(10892008914451739475)
XLA Ops:
  0.7 0.0 copy-start
  0.7 1.0 %copy-done = f32[8,11392]{1,0:T(8,128)S(1)} copy-done((f32[8,11392]{1,0:T(8,128)S(1)}, f32[8,11392]{1,0:T(8,128)}, u32[]{:S(2)}) %copy-start) | copy-done | bytes 364568
  1.6 0.9 %shard_map.57 = f32[16,8,256]{2,1,0:T(8,128)} custom-call(s32[1]{0:T(128)S(6)} %copy.13.start_ref, f32[8,11392]{1,0:T(8,128)S(1)} %copy-done), custom_call_target="tpu_custom_call" | custom-call | tf_op jit(solution)/shard_map/pallas_call | solution.py:166
  2.6 7.4 %all-to-all-start.1 = ((f32[16,8,256]{2,1,0:T(8,128)}), f32[16,8,256]{2,1,0:T(8,128)S(1)}, u32[]{:S(2)}, u32[]{:S(2)}) async-start(f32[16,8,256]{2,1,0:T(8,128)} %shard_map.57), calls=%async_computation.1 | async-start | bytes 262144 | tf_op jit(solution)/shard_map/all_to_all | solution.py:178
  10.6 1.0 %copy-done.1 = f32[8,11392]{1,0:T(8,128)S(1)} copy-done((f32[8,11392]{1,0:T(8,128)S(1)}, f32[8,11392]{1,0:T(8,128)}, u32[]{:S(2)}) %copy-start.1) | copy-done | bytes 364568
  11.6 0.7 %copy-done.2 = f32[17]{0:T(128)S(1)} copy-done((f32[17]{0:T(128)S(1)}, f32[17]{0:T(128)}, u32[]{:S(2)}) %copy-start.2) | copy-done | bytes 92
  12.3 0.7 %copy-done.3 = s32[16]{0:T(128)S(1)} copy-done((s32[16]{0:T(128)S(1)}, s32[16]{0:T(128)}, u32[]{:S(2)}) %copy-start.3) | copy-done | bytes 88
  12.9 1.5 %shard_map.55 = (f32[16,8,768]{2,1,0:T(8,128)}, f32[96,128]{1,0:T(8,128)S(1)}) custom-call(f32[17]{0:T(128)S(1)} %copy-done.2, s32[1]{0:T(128)S(6)} %copy.12.count_ref, s32[16]{0:T(128)S(1)} %copy-done.3, f32[8,11392]{1,0:T(8,128)S(1)} %copy-done.1), custom_call_target="tpu_custom_call" | custom-call | tf_op jit(solution)/shard_map/pallas_call | solution.py:179
  14.4 3.5 %all-to-all-done.1 = f32[16,8,256]{2,1,0:T(8,128)S(1)} async-done(((f32[16,8,256]{2,1,0:T(8,128)}), f32[16,8,256]{2,1,0:T(8,128)S(1)}, u32[]{:S(2)}, u32[]{:S(2)}) %all-to-all-start.1) | async-done | bytes 131104 | tf_op jit(solution)/shard_map/all_to_all | solution.py:178
  17.9 3.6 %all-to-all-start = ((f32[16,8,768]{2,1,0:T(8,128)}), f32[16,8,768]{2,1,0:T(8,128)S(1)}, u32[]{:S(2)}, u32[]{:S(2)}) async-start(f32[16,8,768]{2,1,0:T(8,128)} %get-tuple-element.8), calls=%async_computation | async-start | bytes 786432 | tf_op jit(solution)/shard_map/all_to_all | solution.py:189
  21.5 0.2 shard_map.58
  21.7 1.9 %collective-permute-start = (bf16[96,256]{1,0:T(8,128)(2,1)S(1)}, bf16[96,256]{1,0:T(8,128)(2,1)S(1)}, u32[]{:S(2)}, u32[]{:S(2)}) collective-permute-start(bf16[96,256]{1,0:T(8,128)(2,1)S(1)} %shard_map.58), channel_id=1, source_target_pairs={{0,4},{2,6},{4,0},{6,2},{8,12},{10,14},{12,8},{14,10},{1,5},{3,7},... | collective-permute-start | bytes 147464 | tf_op jit(solution)/shard_map/ppermute | solution.py:199
  23.6 2.4 %collective-permute-start.1 = (bf16[96,256]{1,0:T(8,128)(2,1)S(1)}, bf16[96,256]{1,0:T(8,128)(2,1)S(1)}, u32[]{:S(2)}, u32[]{:S(2)}) collective-permute-start(bf16[96,256]{1,0:T(8,128)(2,1)S(1)} %shard_map.58), channel_id=1, source_target_pairs={{0,8},{2,10},{4,12},{6,14},{8,0},{10,2},{12,4},{14,6},{1,9},{3,11}... | collective-permute-start | bytes 147464 | tf_op jit(solution)/shard_map/ppermute | solution.py:199
  26.0 0.1 collective-permute-start.2
  26.2 4.8 %collective-permute-done = bf16[96,256]{1,0:T(8,128)(2,1)S(1)} collective-permute-done((bf16[96,256]{1,0:T(8,128)(2,1)S(1)}, bf16[96,256]{1,0:T(8,128)(2,1)S(1)}, u32[]{:S(2)}, u32[]{:S(2)}) %collective-permute-start) | collective-permute-done | bytes 49184 | tf_op jit(solution)/shard_map/ppermute | solution.py:199
  30.9 6.5 %collective-permute-done.1 = bf16[96,256]{1,0:T(8,128)(2,1)S(1)} collective-permute-done((bf16[96,256]{1,0:T(8,128)(2,1)S(1)}, bf16[96,256]{1,0:T(8,128)(2,1)S(1)}, u32[]{:S(2)}, u32[]{:S(2)}) %collective-permute-start.1) | collective-permute-done | bytes 49184 | tf_op jit(solution)/shard_map/ppermute | solution.py:199
  37.5 1.5 %collective-permute-start.3 = (bf16[4,96,256]{2,1,0:T(8,128)(2,1)S(1)}, bf16[4,96,256]{2,1,0:T(8,128)(2,1)S(1)}, u32[]{:S(2)}, u32[]{:S(2)}) collective-permute-start(bf16[4,96,256]{2,1,0:T(8,128)(2,1)S(1)} %pad_maximum_fusion.line_ref), channel_id=1, source_target_pairs={{0,2},{2,0},{4,6},{6,4},{8,10},{10,8},{12,14},{14,12},{1,3},{3,1},... | collective-permute-start | bytes 589832 | tf_op jit(solution)/shard_map/ppermute | solution.py:199
  39.1 4.5 %collective-permute-done.3.line_ref = bf16[4,96,256]{2,1,0:T(8,128)(2,1)S(1)} collective-permute-done((bf16[4,96,256]{2,1,0:T(8,128)(2,1)S(1)}, bf16[4,96,256]{2,1,0:T(8,128)(2,1)S(1)}, u32[]{:S(2)}, u32[]{:S(2)}) %collective-permute-start.3) | collective-permute-done | bytes 196640 | tf_op jit(solution)/shard_map/ppermute | solution.py:199
  43.5 0.1 pad_add_fusion.place_ref
  43.6 0.5 shard_map.56.own_ref
  44.2 2.7 %shard_map.59.refs_0_ = bf16[712,4096]{1,0:T(8,128)(2,1)} custom-call(s32[2]{0:T(128)S(1)} %pad_add_fusion.place_ref, bf16[712,96]{1,0:T(8,128)(2,1)S(1)} %shard_map.56.own_ref, bf16[4,96,256]{2,1,0:T(8,128)(2,1)S(1)} %pad_maximum_fusion.line_ref), custom_call_target="tpu_custom_call" | custom-call | tf_op jit(solution)/shard_map/pallas_call | solution.py:135
  46.9 2.7 %shard_map.60.refs_0_ = bf16[712,4096]{1,0:T(8,128)(2,1)} custom-call(s32[2]{0:T(128)S(1)} %pad_add_fusion.place_ref, bf16[712,96]{1,0:T(8,128)(2,1)S(1)} %shard_map.56.own_ref, bf16[4,96,256]{2,1,0:T(8,128)(2,1)S(1)} %collective-permute-done.5.line_ref, bf16[712,4096]{1,0:T(8,128)(2,1)} %shard_map.59.refs_0_), custom_call_target="tpu_custom_call", output_to_operand_aliasing={{}: (3, {})} | custom-call | tf_op jit(solution)/shard_map/pallas_call | solution.py:135
  49.6 2.7 %shard_map.61.refs_0_ = bf16[712,4096]{1,0:T(8,128)(2,1)} custom-call(s32[2]{0:T(128)S(1)} %pad_add_fusion.place_ref, bf16[712,96]{1,0:T(8,128)(2,1)S(1)} %shard_map.56.own_ref, bf16[4,96,256]{2,1,0:T(8,128)(2,1)S(1)} %collective-permute-done.3.line_ref, bf16[712,4096]{1,0:T(8,128)(2,1)} %shard_map.60.refs_0_), custom_call_target="tpu_custom_call", output_to_operand_aliasing={{}: (3, {})} | custom-call | tf_op jit(solution)/shard_map/pallas_call | solution.py:135
  52.3 2.7 %shard_map.62 = bf16[712,4096]{1,0:T(8,128)(2,1)} custom-call(s32[2]{0:T(128)S(1)} %pad_add_fusion.place_ref, bf16[712,96]{1,0:T(8,128)(2,1)S(1)} %shard_map.56.own_ref, bf16[4,96,256]{2,1,0:T(8,128)(2,1)S(1)} %collective-permute-done.4.line_ref, bf16[712,4096]{1,0:T(8,128)(2,1)} %shard_map.61.refs_0_), custom_call_target="tpu_custom_call", output_to_operand_aliasing={{}: (3, {})} | custom-call | tf_op jit(solution)/shard_map/pallas_call | solution.py:135
  (10 shorter events, 0.1 us)
Async XLA Ops:
  0.7 1.0 %copy-start = (f32[8,11392]{1,0:T(8,128)S(1)}, f32[8,11392]{1,0:T(8,128)}, u32[]{:S(2)}) copy-start(f32[8,11392]{1,0:T(8,128)} %series_ref.3) | copy-start | bytes 1093636
  2.6 15.3 %all-to-all-start.1 = ((f32[16,8,256]{2,1,0:T(8,128)}), f32[16,8,256]{2,1,0:T(8,128)S(1)}, u32[]{:S(2)}, u32[]{:S(2)}) async-start(f32[16,8,256]{2,1,0:T(8,128)} %shard_map.57), calls=%async_computation.1 | async-start | bytes 262144 | tf_op jit(solution)/shard_map/all_to_all | solution.py:178
  10.6 1.0 %copy-start.1 = (f32[8,11392]{1,0:T(8,128)S(1)}, f32[8,11392]{1,0:T(8,128)}, u32[]{:S(2)}) copy-start(f32[8,11392]{1,0:T(8,128)} %series_ref.3) | copy-start | bytes 1093636
  11.6 0.7 %copy-start.2 = (f32[17]{0:T(128)S(1)}, f32[17]{0:T(128)}, u32[]{:S(2)}) copy-start(f32[17]{0:T(128)} %taps_ref.1) | copy-start | bytes 208
  12.3 0.7 %copy-start.3 = (s32[16]{0:T(128)S(1)}, s32[16]{0:T(128)}, u32[]{:S(2)}) copy-start(s32[16]{0:T(128)} %kept_ref.1) | copy-start | bytes 196
  17.9 25.7 %all-to-all-start = ((f32[16,8,768]{2,1,0:T(8,128)}), f32[16,8,768]{2,1,0:T(8,128)S(1)}, u32[]{:S(2)}, u32[]{:S(2)}) async-start(f32[16,8,768]{2,1,0:T(8,128)} %get-tuple-element.8), calls=%async_computation | async-start | bytes 786432 | tf_op jit(solution)/shard_map/all_to_all | solution.py:189
  21.7 9.2 %collective-permute-start = (bf16[96,256]{1,0:T(8,128)(2,1)S(1)}, bf16[96,256]{1,0:T(8,128)(2,1)S(1)}, u32[]{:S(2)}, u32[]{:S(2)}) collective-permute-start(bf16[96,256]{1,0:T(8,128)(2,1)S(1)} %shard_map.58), channel_id=1, source_target_pairs={{0,4},{2,6},{4,0},{6,2},{8,12},{10,14},{12,8},{14,10},{1,5},{3,7},... | collective-permute-start | bytes 147464 | tf_op jit(solution)/shard_map/ppermute | solution.py:199
  23.6 13.9 %collective-permute-start.1 = (bf16[96,256]{1,0:T(8,128)(2,1)S(1)}, bf16[96,256]{1,0:T(8,128)(2,1)S(1)}, u32[]{:S(2)}, u32[]{:S(2)}) collective-permute-start(bf16[96,256]{1,0:T(8,128)(2,1)S(1)} %shard_map.58), channel_id=1, source_target_pairs={{0,8},{2,10},{4,12},{6,14},{8,0},{10,2},{12,4},{14,6},{1,9},{3,11}... | collective-permute-start | bytes 147464 | tf_op jit(solution)/shard_map/ppermute | solution.py:199
  26.0 11.4 %collective-permute-start.2 = (bf16[96,256]{1,0:T(8,128)(2,1)S(1)}, bf16[96,256]{1,0:T(8,128)(2,1)S(1)}, u32[]{:S(2)}, u32[]{:S(2)}) collective-permute-start(bf16[96,256]{1,0:T(8,128)(2,1)S(1)} %shard_map.58), channel_id=1, source_target_pairs={{0,12},{2,14},{4,8},{6,10},{8,4},{10,6},{12,0},{14,2},{1,13},{3,15... | collective-permute-start | bytes 147464 | tf_op jit(solution)/shard_map/ppermute | solution.py:199
  37.5 6.0 %collective-permute-start.3 = (bf16[4,96,256]{2,1,0:T(8,128)(2,1)S(1)}, bf16[4,96,256]{2,1,0:T(8,128)(2,1)S(1)}, u32[]{:S(2)}, u32[]{:S(2)}) collective-permute-start(bf16[4,96,256]{2,1,0:T(8,128)(2,1)S(1)} %pad_maximum_fusion.line_ref), channel_id=1, source_target_pairs={{0,2},{2,0},{4,6},{6,4},{8,10},{10,8},{12,14},{14,12},{1,3},{3,1},... | collective-permute-start | bytes 589832 | tf_op jit(solution)/shard_map/ppermute | solution.py:199
  39.0 7.8 %collective-permute-start.5 = (bf16[4,96,256]{2,1,0:T(8,128)(2,1)S(1)}, bf16[4,96,256]{2,1,0:T(8,128)(2,1)S(1)}, u32[]{:S(2)}, u32[]{:S(2)}) collective-permute-start(bf16[4,96,256]{2,1,0:T(8,128)(2,1)S(1)} %pad_maximum_fusion.line_ref), channel_id=1, source_target_pairs={{0,1},{1,0},{2,3},{3,2},{4,5},{5,4},{6,7},{7,6},{8,9},{9,8},{10,11... | collective-permute-start | bytes 589832 | tf_op jit(solution)/shard_map/ppermute | solution.py:202
  43.5 8.7 %collective-permute-start.4 = (bf16[4,96,256]{2,1,0:T(8,128)(2,1)S(1)}, bf16[4,96,256]{2,1,0:T(8,128)(2,1)S(1)}, u32[]{:S(2)}, u32[]{:S(2)}) collective-permute-start(bf16[4,96,256]{2,1,0:T(8,128)(2,1)S(1)} %collective-permute-done.3.line_ref), channel_id=1, source_target_pairs={{0,1},{1,0},{2,3},{3,2},{4,5},{5,4},{6,7},{7,6},{8,9},{9,8},{10,11... | collective-permute-start | bytes 589832 | tf_op jit(solution)/shard_map/ppermute | solution.py:202

commit v3 on v1

v3 whole, which is shorter than its diff:
```python
import functools

import jax
import jax.numpy as jnp
from jax import lax
from jax.experimental import pallas as pl
from jax.experimental.pallas import tpu as pltpu
from jax.sharding import PartitionSpec as P

B = 4096
LANES = 128
EPSILON = 1e-06
CLIP_LIMIT = 0.999
HALF_LN2 = 0.34657359027997264
N_LOADS = 4
PACK_VMEM = 62 << 20
AXES = ("row", "col")


def round_up(value, unit):
    return (value + unit - 1) // unit * unit


def band_place(device, n_row):
    row, col = device // 2, device % 2
    return (col * 2 + row % 2) * (n_row // 2) + row // 2


def pack_kernel(n_row, own, share, start_ref, series_ref, out_ref, whole_ref, band_ref, sems):
    total = series_ref.shape[1]
    own_pad = round_up(own, LANES)
    tiles = total // LANES
    cuts = [tiles * i // N_LOADS * LANES for i in range(N_LOADS + 1)]
    loads = [
        pltpu.make_async_copy(
            series_ref.at[:, low:high], whole_ref.at[:, low:high], sems.at[i]
        )
        for i, (low, high) in enumerate(zip(cuts, cuts[1:]))
    ]
    for load in loads:
        load.start()
    loaded = 0
    for device in range(2 * n_row):
        while cuts[loaded] < (device + 1) * own:
            loads[loaded].wait()
            loaded += 1
        out_ref[device, :, :own] = whole_ref[:, device * own : (device + 1) * own]
        if own_pad > own:
            out_ref[device, :, own:own_pad] = jnp.zeros((8, own_pad - own), jnp.float32)
    while loaded < N_LOADS:
        loads[loaded].wait()
        loaded += 1

    start = start_ref[0]
    base = pl.multiple_of(jnp.minimum(start // LANES * LANES, total - B - LANES), LANES)
    rest = start - base
    shift = lax.rem(LANES - rest, LANES)
    lane = lax.broadcasted_iota(jnp.int32, (8, LANES), 1)
    here = lane < LANES - rest
    before = pltpu.roll(whole_ref[:, pl.ds(base, LANES)], shift, 1)
    for tile in range(B // LANES):
        after = pltpu.roll(whole_ref[:, pl.ds(base + (tile + 1) * LANES, LANES)], shift, 1)
        band_ref[:, tile * LANES : (tile + 1) * LANES] = jnp.where(here, before, after)
        before = after
    for device in range(2 * n_row):
        place = band_place(device, n_row)
        out_ref[device, :, own_pad : own_pad + share] = band_ref[
            :, place * share : (place + 1) * share
        ]


def filter_matrix(kept, frames, taps_ref, count_ref, kept_ref):
    n_taps = taps_ref.shape[0]
    reach = n_taps // 2
    shape = (kept, LANES)
    place = lax.broadcasted_iota(jnp.int32, shape, 0)

    def skip(block, carry):
        frame, seen = carry
        seen = seen + kept_ref[block]
        return frame + jnp.where(place >= seen, 8 - kept_ref[block], 0), seen

    frame, _ = lax.fori_loop(0, frames // 8, skip, (place, jnp.int32(0)), unroll=frames <= 128)
    reach_used = count_ref[0]
    tap_sum = jnp.float32(0)
    tap_number = jnp.float32(0)
    for tap in range(n_taps):
        used = abs(tap - reach) <= reach_used
        tap_sum = tap_sum + jnp.where(used, taps_ref[tap], 0.0)
        tap_number = tap_number + jnp.where(used, 1.0, 0.0)
    centre = jnp.full(shape, tap_sum, jnp.float32) / jnp.full(shape, tap_number, jnp.float32)
    pieces = []
    for tile in range(frames // LANES):
        offset = lax.broadcasted_iota(jnp.int32, shape, 1) + tile * LANES - frame
        value = jnp.zeros(shape, jnp.float32)
        for tap in range(n_taps):
            value = jnp.where(offset == tap - reach, taps_ref[tap], value)
        pieces.append(jnp.where(jnp.abs(offset) <= reach_used, value - centre, 0.0))
    return pieces[0] if len(pieces) == 1 else jnp.concatenate(pieces, 1)


def matrix_kernel(taps_ref, count_ref, kept_ref, out_ref):
    kept, frames = out_ref.shape
    out_ref[...] = filter_matrix(kept, frames, taps_ref, count_ref, kept_ref)


def scaled_columns(matrix, raw):
    centered = jnp.dot(
        matrix, raw, precision=lax.Precision.HIGHEST, preferred_element_type=jnp.float32
    )
    spread = jnp.sum(centered * centered, axis=0, keepdims=True)
    return centered * lax.rsqrt(spread + EPSILON)


def scale_band_kernel(first, matrix_ref, raw_ref, band_ref):
    scaled = scaled_columns(matrix_ref[...], raw_ref[:, first:])
    band_ref[...] = scaled[:, : band_ref.shape[1]].astype(jnp.bfloat16)


def scale_own_kernel(end, matrix_ref, raw_ref, own_ref):
    scaled = scaled_columns(matrix_ref[...], raw_ref[:, :end])
    own_ref[...] = scaled.T[: own_ref.shape[0]].astype(jnp.bfloat16)


def fisher_kernel(swaps, place_ref, own_ref, *refs):
    lines = refs[: len(swaps)]
    out_ref, made_ref, sems = refs[-3:]
    blocks, _, width = lines[0].shape
    copies = []
    for swap, line_ref in zip(swaps, lines):
        for step in range(blocks):
            spot = len(copies) * width
            correlation = jnp.dot(own_ref[...], line_ref[step], preferred_element_type=jnp.float32)
            c = jnp.clip(correlation, -CLIP_LIMIT, CLIP_LIMIT)
            z_value = HALF_LN2 * (jnp.log2(1.0 + c) - jnp.log2(1.0 - c))
            made_ref[:, spot : spot + width] = z_value.astype(jnp.bfloat16)
            where = ((place_ref[1] ^ swap) * blocks + (place_ref[0] ^ step)) * width
            copy = pltpu.make_async_copy(
                made_ref.at[:, spot : spot + width],
                out_ref.at[:, pl.ds(pl.multiple_of(where, width), width)],
                sems.at[len(copies)],
            )
            copy.start()
            copies.append(copy)
    for copy in copies:
        copy.wait()


def fisher_part(place, own_rows, lines, swaps, out):
    blocks, _, width = lines[0].shape
    own = own_rows.shape[0]
    vmem = pl.BlockSpec(memory_space=pltpu.VMEM)
    specs = [pl.BlockSpec(memory_space=pltpu.SMEM)] + [vmem] * (1 + len(lines))
    args = [place, own_rows, *lines]
    aliases = {}
    if out is not None:
        specs.append(pl.BlockSpec(memory_space=pltpu.HBM))
        aliases = {len(args): 0}
        args.append(out)
    return pl.pallas_call(
        functools.partial(fisher_kernel, swaps),
        out_shape=jax.ShapeDtypeStruct((own, B), jnp.bfloat16),
        in_specs=specs,
        out_specs=pl.BlockSpec(memory_space=pltpu.HBM),
        scratch_shapes=[
            pltpu.VMEM((own, len(lines) * blocks * width), jnp.bfloat16),
            pltpu.SemaphoreType.DMA((len(lines) * blocks,)),
        ],
        input_output_aliases=aliases,
        compiler_params=pltpu.CompilerParams(vmem_limit_bytes=48 << 20),
    )(*args)


def body(series, tap_values, tap_count, kept_frames, band_start):
    n_row = lax.axis_size("row")
    n_dev = n_row * lax.axis_size("col")
    frames = 8 * n_dev
    kept = frames * 3 // 4
    total = series.shape[1]
    own = total // n_dev
    own_pad = round_up(own, LANES)
    share = B // n_dev
    share_pad = round_up(share, LANES)
    n_quarter = n_row // 2
    smem = pl.BlockSpec(memory_space=pltpu.SMEM)
    vmem = pl.BlockSpec(memory_space=pltpu.VMEM)
    params = pltpu.CompilerParams(vmem_limit_bytes=48 << 20)

    packed = pl.pallas_call(
        functools.partial(pack_kernel, n_row, own, share),
        out_shape=jax.ShapeDtypeStruct((n_dev, 8, own_pad + share_pad), jnp.float32),
        in_specs=[smem, pl.BlockSpec(memory_space=pltpu.HBM)],
        out_specs=vmem,
        scratch_shapes=[
            pltpu.VMEM((8, total), jnp.float32),
            pltpu.VMEM((8, B), jnp.float32),
            pltpu.SemaphoreType.DMA((N_LOADS,)),
        ],
        compiler_params=pltpu.CompilerParams(vmem_limit_bytes=PACK_VMEM),
    )(band_start, series)
    raw = lax.all_to_all(packed, AXES, 0, 0, tiled=True).reshape(frames, own_pad + share_pad)
    matrix = pl.pallas_call(
        matrix_kernel,
        out_shape=jax.ShapeDtypeStruct((kept, frames), jnp.float32),
        in_specs=[smem, smem, smem],
        out_specs=vmem,
        compiler_params=params,
    )(tap_values, tap_count, kept_frames)
    block = pl.pallas_call(
        functools.partial(scale_band_kernel, own_pad),
        out_shape=jax.ShapeDtypeStruct((kept, share), jnp.bfloat16),
        in_specs=[vmem, vmem],
        out_specs=vmem,
        compiler_params=params,
    )(matrix, raw)

    def swap_row(x, bits):
        return lax.ppermute(x, "row", [(i, i ^ bits) for i in range(n_row)])

    def swap_col(x):
        return lax.ppermute(x, "col", [(0, 1), (1, 0)])

    row, col = lax.axis_index("row"), lax.axis_index("col")
    first = row // 2
    own_rows = pl.pallas_call(
        functools.partial(scale_own_kernel, own_pad),
        out_shape=jax.ShapeDtypeStruct((own, kept), jnp.bfloat16),
        in_specs=[vmem, vmem],
        out_specs=vmem,
        compiler_params=params,
    )(matrix, raw)
    parts = [block] + [swap_row(block, 2 * step) for step in range(1, n_quarter)]
    own_rows, *parts = lax.optimization_barrier((own_rows, *parts))
    line = jnp.stack(parts)
    if share % LANES:
        line = jnp.take(line, jnp.arange(n_quarter, dtype=jnp.int32) ^ first, axis=0)
        line = line.transpose(1, 0, 2).reshape(1, kept, n_quarter * share)
        first = jnp.zeros_like(first)
    place = jnp.stack([first, col * 2 + row % 2]).astype(jnp.int32)
    line_y = swap_row(line, 1)
    line_c = swap_col(line)
    out = fisher_part(place, own_rows, [line, line_c], (0, 2), None)
    line_y, out = lax.optimization_barrier((line_y, out))
    line_yc = swap_col(line_y)
    out = fisher_part(place, own_rows, [line_y, line_yc], (1, 3), out)
    return out.T


def solution(mesh):
    placed = (P(("subj", "row", "col"), None), P(), P(), P("subj"), P("subj"))
    return jax.shard_map(
        body, mesh=mesh, in_specs=placed, out_specs=P("subj", ("row", "col")), check_vma=False
    )
```

time: 50 us -> 45.4 us (0.908)
  waiting for transfers between devices: 24.3 us -> 19.1 us
  Pallas kernels: 8.65 us -> 10.2 us
  local copies, waits for them, and re-layouts: 2.29 us -> 1.31 us
    ppermute x4, waiting for transfers between devices: 9.14 us -> 5.66 us  [swap_row(): return lax.ppermute(x, 'row', [(i, i ^ bits) for i in range(n_row)])]
    all_to_all x1, waiting for transfers between devices: 13.8 us -> 11.8 us  [body(): lax.all_to_all(packed, AXES, 0, 0, tiled=True)]
    pallas_call x3 -> x6, Pallas kernels: 8.65 us -> 10.2 us  [the longest x2 6.62 us: fisher_part(): pl.pallas_call(functools.partial(fisher_kernel, swaps), out_shape=jax.Sha...]
    unnamed x6 -> x4, local copies, waits for them, and re-layouts: 2.29 us -> 1.31 us
  transfers between devices with their start and end apart: 7 -> 7, of which waited for: 5 -> 6; matrix products, arithmetic and copies ran while one was open for 0% -> 0% of each run, Pallas kernels for 0% -> 10%
where the time goes in v3:
time: 45.4 us; the launch traced here: 45.2 us
  waiting for transfers between devices  19.1 us (42%)
  starting transfers between devices  13 us (29%)
  Pallas kernels  10.2 us (22%)
  between operations  1.37 us (3%)
  local copies, waits for them, and re-layouts  1.31 us (3%)
    all_to_all x1, waiting for transfers between devices, body(): lax.all_to_all(packed, AXES, 0, 0, tiled=True)  11.8 us
    all_to_all x1, starting transfers between devices, body(): lax.all_to_all(packed, AXES, 0, 0, tiled=True)  7.4 us
    pallas_call x2, Pallas kernels, fisher_part(): pl.pallas_call(functools.partial(fisher_kernel, swaps), out_shape=jax.Sha...  6.62 us
    ppermute x4, waiting for transfers between devices, swap_row(): return lax.ppermute(x, 'row', [(i, i ^ bits) for i in range(n_row)])  5.66 us
    ppermute x4, starting transfers between devices, swap_row(): return lax.ppermute(x, 'row', [(i, i ^ bits) for i in range(n_row)])  5.58 us
    pallas_call x1, Pallas kernels, body(): pl.pallas_call(functools.partial(pack_kernel, n_row, own, share), out_sha...  2.13 us
    ppermute x2, waiting for transfers between devices, swap_col(): return lax.ppermute(x, 'col', [(0, 1), (1, 0)])  1.67 us
    unnamed x4, local copies, waits for them, and re-layouts  1.31 us
  transfers between devices with their start and end apart: 7, of which 6 were waited for; matrix products, arithmetic and copies ran while one was open for 0% of the time, Pallas kernels for 10%

profile of v3, /device:TPU:0, one launch (start us, length us, event | category | flops | bytes accessed | tf_op | source)
XLA Modules:
  0.0 45.2 jit_solution(12009128771394018989)
XLA Ops:
  0.7 2.1 %shard_map.56 = f32[16,8,1024]{2,1,0:T(8,128)} custom-call(s32[1]{0:T(128)S(6)} %copy.9.start_ref, f32[8,11392]{1,0:T(8,128)} %series_ref.1), custom_call_target="tpu_custom_call" | custom-call | tf_op jit(solution)/shard_map/pallas_call | solution.py:189
  2.8 7.4 %all-to-all-start = ((f32[16,8,1024]{2,1,0:T(8,128)}), f32[16,8,1024]{2,1,0:T(8,128)S(1)}, u32[]{:S(2)}, u32[]{:S(2)}) async-start(f32[16,8,1024]{2,1,0:T(8,128)} %shard_map.56), calls=%async_computation | async-start | bytes 1048576 | tf_op jit(solution)/shard_map/all_to_all | solution.py:201
  10.8 0.0 copy-start
  10.9 0.6 %copy-done = f32[17]{0:T(128)S(1)} copy-done((f32[17]{0:T(128)S(1)}, f32[17]{0:T(128)}, u32[]{:S(2)}) %copy-start) | copy-done | bytes 92
  11.5 0.7 %copy-done.1 = s32[16]{0:T(128)S(1)} copy-done((s32[16]{0:T(128)S(1)}, s32[16]{0:T(128)}, u32[]{:S(2)}) %copy-start.1) | copy-done | bytes 88
  12.2 0.7 %shard_map.55.matrix_ref = f32[96,128]{1,0:T(8,128)S(1)} custom-call(f32[17]{0:T(128)S(1)} %copy-done, s32[1]{0:T(128)S(6)} %copy.8.count_ref, s32[16]{0:T(128)S(1)} %copy-done.1), custom_call_target="tpu_custom_call" | custom-call | tf_op jit(solution)/shard_map/pallas_call | solution.py:202
  12.9 11.8 %all-to-all-done = f32[16,8,1024]{2,1,0:T(8,128)S(1)} async-done(((f32[16,8,1024]{2,1,0:T(8,128)}), f32[16,8,1024]{2,1,0:T(8,128)S(1)}, u32[]{:S(2)}, u32[]{:S(2)}) %all-to-all-start) | async-done | bytes 524320 | tf_op jit(solution)/shard_map/all_to_all | solution.py:201
  24.7 0.2 shard_map.58
  24.9 1.4 %collective-permute-start.2 = (bf16[96,256]{1,0:T(8,128)(2,1)S(1)}, bf16[96,256]{1,0:T(8,128)(2,1)S(1)}, u32[]{:S(2)}, u32[]{:S(2)}) collective-permute-start(bf16[96,256]{1,0:T(8,128)(2,1)S(1)} %shard_map.58), channel_id=1, source_target_pairs={{0,12},{2,14},{4,8},{6,10},{8,4},{10,6},{12,0},{14,2},{1,13},{3,15... | collective-permute-start | bytes 147464 | tf_op jit(solution)/shard_map/ppermute | solution.py:218
  26.4 1.2 %collective-permute-start.1 = (bf16[96,256]{1,0:T(8,128)(2,1)S(1)}, bf16[96,256]{1,0:T(8,128)(2,1)S(1)}, u32[]{:S(2)}, u32[]{:S(2)}) collective-permute-start(bf16[96,256]{1,0:T(8,128)(2,1)S(1)} %shard_map.58), channel_id=1, source_target_pairs={{0,8},{2,10},{4,12},{6,14},{8,0},{10,2},{12,4},{14,6},{1,9},{3,11}... | collective-permute-start | bytes 147464 | tf_op jit(solution)/shard_map/ppermute | solution.py:218
  27.6 1.8 %collective-permute-start = (bf16[96,256]{1,0:T(8,128)(2,1)S(1)}, bf16[96,256]{1,0:T(8,128)(2,1)S(1)}, u32[]{:S(2)}, u32[]{:S(2)}) collective-permute-start(bf16[96,256]{1,0:T(8,128)(2,1)S(1)} %shard_map.58), channel_id=1, source_target_pairs={{0,4},{2,6},{4,0},{6,2},{8,12},{10,14},{12,8},{14,10},{1,5},{3,7},... | collective-permute-start | bytes 147464 | tf_op jit(solution)/shard_map/ppermute | solution.py:218
  29.4 0.5 %shard_map.57.own_ref = bf16[712,96]{1,0:T(8,128)(2,1)S(1)} custom-call(f32[96,128]{1,0:T(8,128)S(1)} %shard_map.55.matrix_ref, f32[128,1024]{1,0:T(8,128)S(1)} %bitcast.9), custom_call_target="tpu_custom_call" | custom-call | tf_op jit(solution)/shard_map/pallas_call | solution.py:225
  29.9 1.2 %collective-permute-done.2 = bf16[96,256]{1,0:T(8,128)(2,1)S(1)} collective-permute-done((bf16[96,256]{1,0:T(8,128)(2,1)S(1)}, bf16[96,256]{1,0:T(8,128)(2,1)S(1)}, u32[]{:S(2)}, u32[]{:S(2)}) %collective-permute-start.2) | collective-permute-done | bytes 49184 | tf_op jit(solution)/shard_map/ppermute | solution.py:218
  31.1 1.8 %collective-permute-done.1 = bf16[96,256]{1,0:T(8,128)(2,1)S(1)} collective-permute-done((bf16[96,256]{1,0:T(8,128)(2,1)S(1)}, bf16[96,256]{1,0:T(8,128)(2,1)S(1)}, u32[]{:S(2)}, u32[]{:S(2)}) %collective-permute-start.1) | collective-permute-done | bytes 49184 | tf_op jit(solution)/shard_map/ppermute | solution.py:218
  33.0 0.0 collective-permute-done
  33.0 0.1 collective-permute-start.4
  33.1 1.1 %collective-permute-start.3 = (bf16[4,96,256]{2,1,0:T(8,128)(2,1)S(1)}, bf16[4,96,256]{2,1,0:T(8,128)(2,1)S(1)}, u32[]{:S(2)}, u32[]{:S(2)}) collective-permute-start(bf16[4,96,256]{2,1,0:T(8,128)(2,1)S(1)} %pad_maximum_fusion.refs_0_), channel_id=1, source_target_pairs={{0,2},{2,0},{4,6},{6,4},{8,10},{10,8},{12,14},{14,12},{1,3},{3,1},... | collective-permute-start | bytes 589832 | tf_op jit(solution)/shard_map/ppermute | solution.py:218
  34.2 0.1 pad_add_fusion.place_ref
  34.3 0.2 collective-permute-done.4.refs_1_
  34.5 3.3 %shard_map.59.refs_2_ = bf16[712,4096]{1,0:T(8,128)(2,1)} custom-call(s32[2]{0:T(128)S(1)} %pad_add_fusion.place_ref, bf16[712,96]{1,0:T(8,128)(2,1)S(1)} %shard_map.57.own_ref, bf16[4,96,256]{2,1,0:T(8,128)(2,1)S(1)} %pad_maximum_fusion.refs_0_, bf16[4,96,256]{2,1,0:T(8,128)(2,1)S(1)} %collective-permute-done.4.refs_1_), custom_call_target="tpu_custom_call" | custom-call | tf_op jit(solution)/shard_map/pallas_call | solution.py:160
  37.8 2.6 %collective-permute-done.3.refs_0_ = bf16[4,96,256]{2,1,0:T(8,128)(2,1)S(1)} collective-permute-done((bf16[4,96,256]{2,1,0:T(8,128)(2,1)S(1)}, bf16[4,96,256]{2,1,0:T(8,128)(2,1)S(1)}, u32[]{:S(2)}, u32[]{:S(2)}) %collective-permute-start.3) | collective-permute-done | bytes 196640 | tf_op jit(solution)/shard_map/ppermute | solution.py:218
  40.4 0.0 collective-permute-start.5
  40.4 1.4 %collective-permute-done.5.refs_1_ = bf16[4,96,256]{2,1,0:T(8,128)(2,1)S(1)} collective-permute-done((bf16[4,96,256]{2,1,0:T(8,128)(2,1)S(1)}, bf16[4,96,256]{2,1,0:T(8,128)(2,1)S(1)}, u32[]{:S(2)}, u32[]{:S(2)}) %collective-permute-start.5) | collective-permute-done | bytes 196640 | tf_op jit(solution)/shard_map/ppermute | solution.py:221
  41.8 3.3 %shard_map.60 = bf16[712,4096]{1,0:T(8,128)(2,1)} custom-call(s32[2]{0:T(128)S(1)} %pad_add_fusion.place_ref, bf16[712,96]{1,0:T(8,128)(2,1)S(1)} %shard_map.57.own_ref, bf16[4,96,256]{2,1,0:T(8,128)(2,1)S(1)} %collective-permute-done.3.refs_0_, bf16[4,96,256]{2,1,0:T(8,128)(2,1)S(1)} %collective-permute-done.5.refs_1_, ...), custom_call_target="tpu_custom_call", output_to_operand_aliasing={{}: (4, {})} | custom-call | tf_op jit(solution)/shard_map/pallas_call | solution.py:160
  (2 shorter events, 0.0 us)
Async XLA Ops:
  2.8 21.9 %all-to-all-start = ((f32[16,8,1024]{2,1,0:T(8,128)}), f32[16,8,1024]{2,1,0:T(8,128)S(1)}, u32[]{:S(2)}, u32[]{:S(2)}) async-start(f32[16,8,1024]{2,1,0:T(8,128)} %shard_map.56), calls=%async_computation | async-start | bytes 1048576 | tf_op jit(solution)/shard_map/all_to_all | solution.py:201
  10.8 0.7 %copy-start = (f32[17]{0:T(128)S(1)}, f32[17]{0:T(128)}, u32[]{:S(2)}) copy-start(f32[17]{0:T(128)} %taps_ref.1) | copy-start | bytes 208
  11.5 0.7 %copy-start.1 = (s32[16]{0:T(128)S(1)}, s32[16]{0:T(128)}, u32[]{:S(2)}) copy-start(s32[16]{0:T(128)} %kept_ref.1) | copy-start | bytes 196
  24.9 6.2 %collective-permute-start.2 = (bf16[96,256]{1,0:T(8,128)(2,1)S(1)}, bf16[96,256]{1,0:T(8,128)(2,1)S(1)}, u32[]{:S(2)}, u32[]{:S(2)}) collective-permute-start(bf16[96,256]{1,0:T(8,128)(2,1)S(1)} %shard_map.58), channel_id=1, source_target_pairs={{0,12},{2,14},{4,8},{6,10},{8,4},{10,6},{12,0},{14,2},{1,13},{3,15... | collective-permute-start | bytes 147464 | tf_op jit(solution)/shard_map/ppermute | solution.py:218
  26.4 6.6 %collective-permute-start.1 = (bf16[96,256]{1,0:T(8,128)(2,1)S(1)}, bf16[96,256]{1,0:T(8,128)(2,1)S(1)}, u32[]{:S(2)}, u32[]{:S(2)}) collective-permute-start(bf16[96,256]{1,0:T(8,128)(2,1)S(1)} %shard_map.58), channel_id=1, source_target_pairs={{0,8},{2,10},{4,12},{6,14},{8,0},{10,2},{12,4},{14,6},{1,9},{3,11}... | collective-permute-start | bytes 147464 | tf_op jit(solution)/shard_map/ppermute | solution.py:218
  27.6 5.4 %collective-permute-start = (bf16[96,256]{1,0:T(8,128)(2,1)S(1)}, bf16[96,256]{1,0:T(8,128)(2,1)S(1)}, u32[]{:S(2)}, u32[]{:S(2)}) collective-permute-start(bf16[96,256]{1,0:T(8,128)(2,1)S(1)} %shard_map.58), channel_id=1, source_target_pairs={{0,4},{2,6},{4,0},{6,2},{8,12},{10,14},{12,8},{14,10},{1,5},{3,7},... | collective-permute-start | bytes 147464 | tf_op jit(solution)/shard_map/ppermute | solution.py:218
  33.0 1.5 %collective-permute-start.4 = (bf16[4,96,256]{2,1,0:T(8,128)(2,1)S(1)}, bf16[4,96,256]{2,1,0:T(8,128)(2,1)S(1)}, u32[]{:S(2)}, u32[]{:S(2)}) collective-permute-start(bf16[4,96,256]{2,1,0:T(8,128)(2,1)S(1)} %pad_maximum_fusion.refs_0_), channel_id=1, source_target_pairs={{0,1},{1,0},{2,3},{3,2},{4,5},{5,4},{6,7},{7,6},{8,9},{9,8},{10,11... | collective-permute-start | bytes 589832 | tf_op jit(solution)/shard_map/ppermute | solution.py:221
  33.1 7.3 %collective-permute-start.3 = (bf16[4,96,256]{2,1,0:T(8,128)(2,1)S(1)}, bf16[4,96,256]{2,1,0:T(8,128)(2,1)S(1)}, u32[]{:S(2)}, u32[]{:S(2)}) collective-permute-start(bf16[4,96,256]{2,1,0:T(8,128)(2,1)S(1)} %pad_maximum_fusion.refs_0_), channel_id=1, source_target_pairs={{0,2},{2,0},{4,6},{6,4},{8,10},{10,8},{12,14},{14,12},{1,3},{3,1},... | collective-permute-start | bytes 589832 | tf_op jit(solution)/shard_map/ppermute | solution.py:218
  40.4 1.4 %collective-permute-start.5 = (bf16[4,96,256]{2,1,0:T(8,128)(2,1)S(1)}, bf16[4,96,256]{2,1,0:T(8,128)(2,1)S(1)}, u32[]{:S(2)}, u32[]{:S(2)}) collective-permute-start(bf16[4,96,256]{2,1,0:T(8,128)(2,1)S(1)} %collective-permute-done.3.refs_0_), channel_id=1, source_target_pairs={{0,1},{1,0},{2,3},{3,2},{4,5},{5,4},{6,7},{7,6},{8,9},{9,8},{10,11... | collective-permute-start | bytes 589832 | tf_op jit(solution)/shard_map/ppermute | solution.py:221

commit v4 on v3

--- a/solution.py
+++ b/solution.py
@@ -26,27 +26,36 @@
     return (col * 2 + row % 2) * (n_row // 2) + row // 2
 
 
-def pack_kernel(n_row, own, share, start_ref, series_ref, out_ref, whole_ref, band_ref, sems):
+def pack_kernel(
+    n_row, own, share, start_ref, series_ref, out_ref, whole_ref, own_ref, band_ref, shares_ref, load_sems, sems
+):
     total = series_ref.shape[1]
-    own_pad = round_up(own, LANES)
+    n_dev = 2 * n_row
+    own_pad = own_ref.shape[2]
     tiles = total // LANES
     cuts = [tiles * i // N_LOADS * LANES for i in range(N_LOADS + 1)]
     loads = [
         pltpu.make_async_copy(
-            series_ref.at[:, low:high], whole_ref.at[:, low:high], sems.at[i]
+            series_ref.at[:, low:high], whole_ref.at[:, low:high], load_sems.at[i]
         )
         for i, (low, high) in enumerate(zip(cuts, cuts[1:]))
     ]
     for load in loads:
         load.start()
     loaded = 0
-    for device in range(2 * n_row):
+    stores = []
+    for device in range(n_dev):
         while cuts[loaded] < (device + 1) * own:
             loads[loaded].wait()
             loaded += 1
-        out_ref[device, :, :own] = whole_ref[:, device * own : (device + 1) * own]
+        own_ref[device, :, :own] = whole_ref[:, device * own : (device + 1) * own]
         if own_pad > own:
-            out_ref[device, :, own:own_pad] = jnp.zeros((8, own_pad - own), jnp.float32)
+            own_ref[device, :, own:] = jnp.zeros((8, own_pad - own), jnp.float32)
+        store = pltpu.make_async_copy(
+            own_ref.at[device], out_ref.at[device, :, :own_pad], sems.at[device]
+        )
+        store.start()
+        stores.append(store)
     while loaded < N_LOADS:
         loads[loaded].wait()
         loaded += 1
@@ -62,11 +71,14 @@
         after = pltpu.roll(whole_ref[:, pl.ds(base + (tile + 1) * LANES, LANES)], shift, 1)
         band_ref[:, tile * LANES : (tile + 1) * LANES] = jnp.where(here, before, after)
         before = after
-    for device in range(2 * n_row):
+    for device in range(n_dev):
         place = band_place(device, n_row)
-        out_ref[device, :, own_pad : own_pad + share] = band_ref[
-            :, place * share : (place + 1) * share
-        ]
+        shares_ref[device, :, :share] = band_ref[:, place * share : (place + 1) * share]
+    store = pltpu.make_async_copy(shares_ref, out_ref.at[:, :, own_pad:], sems.at[n_dev])
+    store.start()
+    stores.append(store)
+    for store in stores:
+        store.wait()
 
 
 def filter_matrix(kept, frames, taps_ref, count_ref, kept_ref):
@@ -122,19 +134,19 @@
     own_ref[...] = scaled.T[: own_ref.shape[0]].astype(jnp.bfloat16)
 
 
-def fisher_kernel(swaps, place_ref, own_ref, *refs):
-    lines = refs[: len(swaps)]
+def fisher_kernel(spots, n_blocks, place_ref, own_ref, *refs):
+    pieces = refs[: len(spots)]
     out_ref, made_ref, sems = refs[-3:]
-    blocks, _, width = lines[0].shape
+    width = pieces[0].shape[2]
     copies = []
-    for swap, line_ref in zip(swaps, lines):
-        for step in range(blocks):
+    for (swap, steps), piece_ref in zip(spots, pieces):
+        for at, step in enumerate(steps):
             spot = len(copies) * width
-            correlation = jnp.dot(own_ref[...], line_ref[step], preferred_element_type=jnp.float32)
+            correlation = jnp.dot(own_ref[...], piece_ref[at], preferred_element_type=jnp.float32)
             c = jnp.clip(correlation, -CLIP_LIMIT, CLIP_LIMIT)
             z_value = HALF_LN2 * (jnp.log2(1.0 + c) - jnp.log2(1.0 - c))
             made_ref[:, spot : spot + width] = z_value.astype(jnp.bfloat16)
-            where = ((place_ref[1] ^ swap) * blocks + (place_ref[0] ^ step)) * width
+            where = ((place_ref[1] ^ swap) * n_blocks + (place_ref[0] ^ step)) * width
             copy = pltpu.make_async_copy(
                 made_ref.at[:, spot : spot + width],
                 out_ref.at[:, pl.ds(pl.multiple_of(where, width), width)],
@@ -146,25 +158,27 @@
         copy.wait()
 
 
-def fisher_part(place, own_rows, lines, swaps, out):
-    blocks, _, width = lines[0].shape
+def fisher_part(n_blocks, place, own_rows, pieces, out):
+    spots = [(swap, steps) for swap, steps, _ in pieces]
+    arrays = [array for _, _, array in pieces]
+    count, width = sum(len(steps) for _, steps in spots), arrays[0].shape[2]
     own = own_rows.shape[0]
     vmem = pl.BlockSpec(memory_space=pltpu.VMEM)
-    specs = [pl.BlockSpec(memory_space=pltpu.SMEM)] + [vmem] * (1 + len(lines))
-    args = [place, own_rows, *lines]
+    specs = [pl.BlockSpec(memory_space=pltpu.SMEM)] + [vmem] * (1 + len(arrays))
+    args = [place, own_rows, *arrays]
     aliases = {}
     if out is not None:
         specs.append(pl.BlockSpec(memory_space=pltpu.HBM))
         aliases = {len(args): 0}
         args.append(out)
     return pl.pallas_call(
-        functools.partial(fisher_kernel, swaps),
+        functools.partial(fisher_kernel, spots, n_blocks),
         out_shape=jax.ShapeDtypeStruct((own, B), jnp.bfloat16),
         in_specs=specs,
         out_specs=pl.BlockSpec(memory_space=pltpu.HBM),
         scratch_shapes=[
-            pltpu.VMEM((own, len(lines) * blocks * width), jnp.bfloat16),
-            pltpu.SemaphoreType.DMA((len(lines) * blocks,)),
+            pltpu.VMEM((own, count * width), jnp.bfloat16),
+            pltpu.SemaphoreType.DMA((count,)),
         ],
         input_output_aliases=aliases,
         compiler_params=pltpu.CompilerParams(vmem_limit_bytes=48 << 20),
@@ -186,15 +200,19 @@
     vmem = pl.BlockSpec(memory_space=pltpu.VMEM)
     params = pltpu.CompilerParams(vmem_limit_bytes=48 << 20)
 
+    hbm = pl.BlockSpec(memory_space=pltpu.HBM)
     packed = pl.pallas_call(
         functools.partial(pack_kernel, n_row, own, share),
         out_shape=jax.ShapeDtypeStruct((n_dev, 8, own_pad + share_pad), jnp.float32),
-        in_specs=[smem, pl.BlockSpec(memory_space=pltpu.HBM)],
-        out_specs=vmem,
+        in_specs=[smem, hbm],
+        out_specs=hbm,
         scratch_shapes=[
             pltpu.VMEM((8, total), jnp.float32),
+            pltpu.VMEM((n_dev, 8, own_pad), jnp.float32),
             pltpu.VMEM((8, B), jnp.float32),
+            pltpu.VMEM((n_dev, 8, share_pad), jnp.float32),
             pltpu.SemaphoreType.DMA((N_LOADS,)),
+            pltpu.SemaphoreType.DMA((n_dev + 1,)),
         ],
         compiler_params=pltpu.CompilerParams(vmem_limit_bytes=PACK_VMEM),
     )(band_start, series)
@@ -229,20 +247,35 @@
         out_specs=vmem,
         compiler_params=params,
     )(matrix, raw)
-    parts = [block] + [swap_row(block, 2 * step) for step in range(1, n_quarter)]
-    own_rows, *parts = lax.optimization_barrier((own_rows, *parts))
-    line = jnp.stack(parts)
+    arrived = {step: swap_row(block, 2 * step) for step in reversed(range(1, n_quarter))}
+    arrived[0] = block
     if share % LANES:
+        line = jnp.stack([arrived[step] for step in range(n_quarter)])
         line = jnp.take(line, jnp.arange(n_quarter, dtype=jnp.int32) ^ first, axis=0)
-        line = line.transpose(1, 0, 2).reshape(1, kept, n_quarter * share)
+        near = line.transpose(1, 0, 2).reshape(1, kept, n_quarter * share)
         first = jnp.zeros_like(first)
+        pieces = [((0,), near)]
+        n_blocks = 1
+    else:
+        half = n_quarter // 2
+        pieces = [
+            (steps, jnp.stack([arrived[step] for step in steps]))
+            for steps in (tuple(range(half)), tuple(range(half, n_quarter)))
+        ]
+        n_blocks = n_quarter
     place = jnp.stack([first, col * 2 + row % 2]).astype(jnp.int32)
-    line_y = swap_row(line, 1)
-    line_c = swap_col(line)
-    out = fisher_part(place, own_rows, [line, line_c], (0, 2), None)
-    line_y, out = lax.optimization_barrier((line_y, out))
-    line_yc = swap_col(line_y)
-    out = fisher_part(place, own_rows, [line_y, line_yc], (1, 3), out)
+    near_steps, near = pieces[0]
+    near_y = swap_row(near, 1)
+    fars = [(steps, far, swap_row(far, 1)) for steps, far in pieces[1:]]
+    late = [(2, near_steps, swap_col(near)), (3, near_steps, swap_col(near_y))]
+    late += [(2, steps, swap_col(far)) for steps, far, _ in fars]
+    early = [(0, near_steps, near), (1, near_steps, near_y)]
+    early += [(0, steps, far) for steps, far, _ in fars]
+    out = fisher_part(n_blocks, place, own_rows, early, None)
+    for steps, _, far_y in fars:
+        far_y, out = lax.optimization_barrier((far_y, out))
+        late += [(1, steps, far_y), (3, steps, swap_col(far_y))]
+    out = fisher_part(n_blocks, place, own_rows, late, out)
     return out.T
 
 

time: 45.4 us -> 44.5 us (0.980)
  waiting for transfers between devices: 19.1 us -> 17.2 us
  starting transfers between devices: 13 us -> 14.1 us
    ppermute x4 -> x5, waiting for transfers between devices: 5.66 us -> 4.5 us  [swap_row(): return lax.ppermute(x, 'row', [(i, i ^ bits) for i in range(n_row)])]
    ppermute x2 -> x4, starting transfers between devices: 0.07 us -> 1.14 us  [swap_col(): return lax.ppermute(x, 'col', [(0, 1), (1, 0)])]
    ppermute x2 -> x4, waiting for transfers between devices: 1.67 us -> 0.94 us  [swap_col(): return lax.ppermute(x, 'col', [(0, 1), (1, 0)])]
    ppermute x4 -> x5, starting transfers between devices: 5.58 us -> 5.56 us  [swap_row(): return lax.ppermute(x, 'row', [(i, i ^ bits) for i in range(n_row)])]
  transfers between devices with their start and end apart: 7 -> 10, of which waited for: 6 -> 6; matrix products, arithmetic and copies ran while one was open for 0% -> 0% of each run, Pallas kernels for 10% -> 9%
where the time goes in v4:
time: 44.5 us; the launch traced here: 44.2 us
  waiting for transfers between devices  17.2 us (39%)
  starting transfers between devices  14.1 us (32%)
  Pallas kernels  10.1 us (23%)
  between operations  1.38 us (3%)
  local copies, waits for them, and re-layouts  1.31 us (3%)
    all_to_all x1, waiting for transfers between devices, body(): lax.all_to_all(packed, AXES, 0, 0, tiled=True)  11.8 us
    all_to_all x1, starting transfers between devices, body(): lax.all_to_all(packed, AXES, 0, 0, tiled=True)  7.4 us
    pallas_call x2, Pallas kernels, fisher_part(): pl.pallas_call(functools.partial(fisher_kernel, spots, n_blocks), out_sha...  6.48 us
    ppermute x5, starting transfers between devices, swap_row(): return lax.ppermute(x, 'row', [(i, i ^ bits) for i in range(n_row)])  5.56 us
    ppermute x5, waiting for transfers between devices, swap_row(): return lax.ppermute(x, 'row', [(i, i ^ bits) for i in range(n_row)])  4.5 us
    pallas_call x1, Pallas kernels, body(): pl.pallas_call(functools.partial(pack_kernel, n_row, own, share), out_sha...  2.14 us
    unnamed x4, local copies, waits for them, and re-layouts  1.31 us
    ppermute x4, starting transfers between devices, swap_col(): return lax.ppermute(x, 'col', [(0, 1), (1, 0)])  1.14 us
  transfers between devices with their start and end apart: 10, of which 6 were waited for; matrix products, arithmetic and copies ran while one was open for 0% of the time, Pallas kernels for 9%

profile of v4, /device:TPU:0, one launch (start us, length us, event | category | flops | bytes accessed | tf_op | source)
XLA Modules:
  0.0 44.2 jit_solution(13453073960121997301)
XLA Ops:
  0.7 2.1 %shard_map.56 = f32[16,8,1024]{2,1,0:T(8,128)} custom-call(s32[1]{0:T(128)S(6)} %copy.9.start_ref, f32[8,11392]{1,0:T(8,128)} %series_ref.1), custom_call_target="tpu_custom_call" | custom-call | tf_op jit(solution)/shard_map/pallas_call | solution.py:204
  2.8 7.4 %all-to-all-start = ((f32[16,8,1024]{2,1,0:T(8,128)}), f32[16,8,1024]{2,1,0:T(8,128)S(1)}, u32[]{:S(2)}, u32[]{:S(2)}) async-start(f32[16,8,1024]{2,1,0:T(8,128)} %shard_map.56), calls=%async_computation | async-start | bytes 1048576 | tf_op jit(solution)/shard_map/all_to_all | solution.py:219
  10.9 0.6 %copy-done = f32[17]{0:T(128)S(1)} copy-done((f32[17]{0:T(128)S(1)}, f32[17]{0:T(128)}, u32[]{:S(2)}) %copy-start) | copy-done | bytes 92
  11.5 0.7 %copy-done.1 = s32[16]{0:T(128)S(1)} copy-done((s32[16]{0:T(128)S(1)}, s32[16]{0:T(128)}, u32[]{:S(2)}) %copy-start.1) | copy-done | bytes 88
  12.2 0.7 %shard_map.55.matrix_ref = f32[96,128]{1,0:T(8,128)S(1)} custom-call(f32[17]{0:T(128)S(1)} %copy-done, s32[1]{0:T(128)S(6)} %copy.8.count_ref, s32[16]{0:T(128)S(1)} %copy-done.1), custom_call_target="tpu_custom_call" | custom-call | tf_op jit(solution)/shard_map/pallas_call | solution.py:220
  12.9 11.8 %all-to-all-done = f32[16,8,1024]{2,1,0:T(8,128)S(1)} async-done(((f32[16,8,1024]{2,1,0:T(8,128)}), f32[16,8,1024]{2,1,0:T(8,128)S(1)}, u32[]{:S(2)}, u32[]{:S(2)}) %all-to-all-start) | async-done | bytes 524320 | tf_op jit(solution)/shard_map/all_to_all | solution.py:219
  24.7 0.2 shard_map.58
  24.9 1.2 %collective-permute-start = (bf16[96,256]{1,0:T(8,128)(2,1)S(1)}, bf16[96,256]{1,0:T(8,128)(2,1)S(1)}, u32[]{:S(2)}, u32[]{:S(2)}) collective-permute-start(bf16[96,256]{1,0:T(8,128)(2,1)S(1)} %shard_map.58), channel_id=1, source_target_pairs={{0,4},{2,6},{4,0},{6,2},{8,12},{10,14},{12,8},{14,10},{1,5},{3,7},... | collective-permute-start | bytes 147464 | tf_op jit(solution)/shard_map/ppermute | solution.py:236
  26.1 2.6 %collective-permute-start.5 = (bf16[96,256]{1,0:T(8,128)(2,1)S(1)}, bf16[96,256]{1,0:T(8,128)(2,1)S(1)}, u32[]{:S(2)}, u32[]{:S(2)}) collective-permute-start(bf16[96,256]{1,0:T(8,128)(2,1)S(1)} %shard_map.58), channel_id=1, source_target_pairs={{0,12},{2,14},{4,8},{6,10},{8,4},{10,6},{12,0},{14,2},{1,13},{3,15... | collective-permute-start | bytes 147464 | tf_op jit(solution)/shard_map/ppermute | solution.py:236
  28.7 0.4 collective-permute-done
  29.1 0.8 %collective-permute-start.2 = (bf16[2,96,256]{2,1,0:T(8,128)(2,1)S(1)}, bf16[2,96,256]{2,1,0:T(8,128)(2,1)S(1)}, u32[]{:S(2)}, u32[]{:S(2)}) collective-permute-start(bf16[2,96,256]{2,1,0:T(8,128)(2,1)S(1)} %pad_maximum_fusion.refs_0_), channel_id=1, source_target_pairs={{0,2},{2,0},{4,6},{6,4},{8,10},{10,8},{12,14},{14,12},{1,3},{3,1},... | collective-permute-start | bytes 294920 | tf_op jit(solution)/shard_map/ppermute | solution.py:236
  29.9 2.6 %collective-permute-done.5 = bf16[96,256]{1,0:T(8,128)(2,1)S(1)} collective-permute-done((bf16[96,256]{1,0:T(8,128)(2,1)S(1)}, bf16[96,256]{1,0:T(8,128)(2,1)S(1)}, u32[]{:S(2)}, u32[]{:S(2)}) %collective-permute-start.5) | collective-permute-done | bytes 49184 | tf_op jit(solution)/shard_map/ppermute | solution.py:236
  32.5 1.5 %collective-permute-done.4 = bf16[96,256]{1,0:T(8,128)(2,1)S(1)} collective-permute-done((bf16[96,256]{1,0:T(8,128)(2,1)S(1)}, bf16[96,256]{1,0:T(8,128)(2,1)S(1)}, u32[]{:S(2)}, u32[]{:S(2)}) %collective-permute-start.4) | collective-permute-done | bytes 49184 | tf_op jit(solution)/shard_map/ppermute | solution.py:236
  34.0 1.0 %collective-permute-start.7 = (bf16[2,96,256]{2,1,0:T(8,128)(2,1)S(1)}, bf16[2,96,256]{2,1,0:T(8,128)(2,1)S(1)}, u32[]{:S(2)}, u32[]{:S(2)}) collective-permute-start(bf16[2,96,256]{2,1,0:T(8,128)(2,1)S(1)} %pad_maximum_fusion.1.refs_2_), channel_id=1, source_target_pairs={{0,2},{2,0},{4,6},{6,4},{8,10},{10,8},{12,14},{14,12},{1,3},{3,1},... | collective-permute-start | bytes 294920 | tf_op jit(solution)/shard_map/ppermute | solution.py:236
  35.0 0.1 pad_add_fusion.place_ref
  35.1 0.5 %shard_map.57.own_ref = bf16[712,96]{1,0:T(8,128)(2,1)S(1)} custom-call(f32[96,128]{1,0:T(8,128)S(1)} %shard_map.55.matrix_ref, f32[128,1024]{1,0:T(8,128)S(1)} %bitcast.9), custom_call_target="tpu_custom_call" | custom-call | tf_op jit(solution)/shard_map/pallas_call | solution.py:243
  35.6 0.1 collective-permute-start.1
  35.7 0.5 %collective-permute-start.6 = (bf16[2,96,256]{2,1,0:T(8,128)(2,1)S(1)}, bf16[2,96,256]{2,1,0:T(8,128)(2,1)S(1)}, u32[]{:S(2)}, u32[]{:S(2)}) collective-permute-start(bf16[2,96,256]{2,1,0:T(8,128)(2,1)S(1)} %pad_maximum_fusion.1.refs_2_), channel_id=1, source_target_pairs={{0,1},{1,0},{2,3},{3,2},{4,5},{5,4},{6,7},{7,6},{8,9},{9,8},{10,11... | collective-permute-start | bytes 294920 | tf_op jit(solution)/shard_map/ppermute | solution.py:239
  36.2 2.8 %shard_map.59.refs_5_ = bf16[712,4096]{1,0:T(8,128)(2,1)} custom-call(s32[2]{0:T(128)S(1)} %pad_add_fusion.place_ref, bf16[712,96]{1,0:T(8,128)(2,1)S(1)} %shard_map.57.own_ref, bf16[2,96,256]{2,1,0:T(8,128)(2,1)S(1)} %pad_maximum_fusion.refs_0_, bf16[2,96,256]{2,1,0:T(8,128)(2,1)S(1)} %collective-permute-done.2.refs_1_, ...), custom_call_target="tpu_custom_call" | custom-call | tf_op jit(solution)/shard_map/pallas_call | solution.py:174
  39.0 0.2 collective-permute-start.3
  39.2 0.4 collective-permute-start.8
  39.6 0.8 %collective-permute-done.3.refs_1_ = bf16[2,96,256]{2,1,0:T(8,128)(2,1)S(1)} collective-permute-done((bf16[2,96,256]{2,1,0:T(8,128)(2,1)S(1)}, bf16[2,96,256]{2,1,0:T(8,128)(2,1)S(1)}, u32[]{:S(2)}, u32[]{:S(2)}) %collective-permute-start.3) | collective-permute-done | bytes 98336 | tf_op jit(solution)/shard_map/ppermute | solution.py:239
  40.4 0.2 collective-permute-done.8.refs_4_
  40.5 3.7 %shard_map.60 = bf16[712,4096]{1,0:T(8,128)(2,1)} custom-call(s32[2]{0:T(128)S(1)} %pad_add_fusion.place_ref, bf16[712,96]{1,0:T(8,128)(2,1)S(1)} %shard_map.57.own_ref, bf16[2,96,256]{2,1,0:T(8,128)(2,1)S(1)} %collective-permute-done.1.refs_0_, bf16[2,96,256]{2,1,0:T(8,128)(2,1)S(1)} %collective-permute-done.3.refs_1_, ...), custom_call_target="tpu_custom_call", output_to_operand_aliasing={{}: (7, {})} | custom-call | tf_op jit(solution)/shard_map/pallas_call | solution.py:174
  (9 shorter events, 0.0 us)
Async XLA Ops:
  2.8 21.9 %all-to-all-start = ((f32[16,8,1024]{2,1,0:T(8,128)}), f32[16,8,1024]{2,1,0:T(8,128)S(1)}, u32[]{:S(2)}, u32[]{:S(2)}) async-start(f32[16,8,1024]{2,1,0:T(8,128)} %shard_map.56), calls=%async_computation | async-start | bytes 1048576 | tf_op jit(solution)/shard_map/all_to_all | solution.py:219
  10.9 0.7 %copy-start = (f32[17]{0:T(128)S(1)}, f32[17]{0:T(128)}, u32[]{:S(2)}) copy-start(f32[17]{0:T(128)} %taps_ref.1) | copy-start | bytes 208
  11.5 0.7 %copy-start.1 = (s32[16]{0:T(128)S(1)}, s32[16]{0:T(128)}, u32[]{:S(2)}) copy-start(s32[16]{0:T(128)} %kept_ref.1) | copy-start | bytes 196
  24.9 4.2 %collective-permute-start = (bf16[96,256]{1,0:T(8,128)(2,1)S(1)}, bf16[96,256]{1,0:T(8,128)(2,1)S(1)}, u32[]{:S(2)}, u32[]{:S(2)}) collective-permute-start(bf16[96,256]{1,0:T(8,128)(2,1)S(1)} %shard_map.58), channel_id=1, source_target_pairs={{0,4},{2,6},{4,0},{6,2},{8,12},{10,14},{12,8},{14,10},{1,5},{3,7},... | collective-permute-start | bytes 147464 | tf_op jit(solution)/shard_map/ppermute | solution.py:236
  26.1 6.4 %collective-permute-start.5 = (bf16[96,256]{1,0:T(8,128)(2,1)S(1)}, bf16[96,256]{1,0:T(8,128)(2,1)S(1)}, u32[]{:S(2)}, u32[]{:S(2)}) collective-permute-start(bf16[96,256]{1,0:T(8,128)(2,1)S(1)} %shard_map.58), channel_id=1, source_target_pairs={{0,12},{2,14},{4,8},{6,10},{8,4},{10,6},{12,0},{14,2},{1,13},{3,15... | collective-permute-start | bytes 147464 | tf_op jit(solution)/shard_map/ppermute | solution.py:236
  28.7 5.3 %collective-permute-start.4 = (bf16[96,256]{1,0:T(8,128)(2,1)S(1)}, bf16[96,256]{1,0:T(8,128)(2,1)S(1)}, u32[]{:S(2)}, u32[]{:S(2)}) collective-permute-start(bf16[96,256]{1,0:T(8,128)(2,1)S(1)} %shard_map.58), channel_id=1, source_target_pairs={{0,8},{2,10},{4,12},{6,14},{8,0},{10,2},{12,4},{14,6},{1,9},{3,11}... | collective-permute-start | bytes 147464 | tf_op jit(solution)/shard_map/ppermute | solution.py:236
  29.1 7.1 %collective-permute-start.2 = (bf16[2,96,256]{2,1,0:T(8,128)(2,1)S(1)}, bf16[2,96,256]{2,1,0:T(8,128)(2,1)S(1)}, u32[]{:S(2)}, u32[]{:S(2)}) collective-permute-start(bf16[2,96,256]{2,1,0:T(8,128)(2,1)S(1)} %pad_maximum_fusion.refs_0_), channel_id=1, source_target_pairs={{0,2},{2,0},{4,6},{6,4},{8,10},{10,8},{12,14},{14,12},{1,3},{3,1},... | collective-permute-start | bytes 294920 | tf_op jit(solution)/shard_map/ppermute | solution.py:236
  34.0 5.0 %collective-permute-start.7 = (bf16[2,96,256]{2,1,0:T(8,128)(2,1)S(1)}, bf16[2,96,256]{2,1,0:T(8,128)(2,1)S(1)}, u32[]{:S(2)}, u32[]{:S(2)}) collective-permute-start(bf16[2,96,256]{2,1,0:T(8,128)(2,1)S(1)} %pad_maximum_fusion.1.refs_2_), channel_id=1, source_target_pairs={{0,2},{2,0},{4,6},{6,4},{8,10},{10,8},{12,14},{14,12},{1,3},{3,1},... | collective-permute-start | bytes 294920 | tf_op jit(solution)/shard_map/ppermute | solution.py:236
  35.6 4.0 %collective-permute-start.1 = (bf16[2,96,256]{2,1,0:T(8,128)(2,1)S(1)}, bf16[2,96,256]{2,1,0:T(8,128)(2,1)S(1)}, u32[]{:S(2)}, u32[]{:S(2)}) collective-permute-start(bf16[2,96,256]{2,1,0:T(8,128)(2,1)S(1)} %pad_maximum_fusion.refs_0_), channel_id=1, source_target_pairs={{0,1},{1,0},{2,3},{3,2},{4,5},{5,4},{6,7},{7,6},{8,9},{9,8},{10,11... | collective-permute-start | bytes 294920 | tf_op jit(solution)/shard_map/ppermute | solution.py:239
  35.7 3.9 %collective-permute-start.6 = (bf16[2,96,256]{2,1,0:T(8,128)(2,1)S(1)}, bf16[2,96,256]{2,1,0:T(8,128)(2,1)S(1)}, u32[]{:S(2)}, u32[]{:S(2)}) collective-permute-start(bf16[2,96,256]{2,1,0:T(8,128)(2,1)S(1)} %pad_maximum_fusion.1.refs_2_), channel_id=1, source_target_pairs={{0,1},{1,0},{2,3},{3,2},{4,5},{5,4},{6,7},{7,6},{8,9},{9,8},{10,11... | collective-permute-start | bytes 294920 | tf_op jit(solution)/shard_map/ppermute | solution.py:239
  39.0 1.4 %collective-permute-start.3 = (bf16[2,96,256]{2,1,0:T(8,128)(2,1)S(1)}, bf16[2,96,256]{2,1,0:T(8,128)(2,1)S(1)}, u32[]{:S(2)}, u32[]{:S(2)}) collective-permute-start(bf16[2,96,256]{2,1,0:T(8,128)(2,1)S(1)} %collective-permute-done.2.refs_1_), channel_id=1, source_target_pairs={{0,1},{1,0},{2,3},{3,2},{4,5},{5,4},{6,7},{7,6},{8,9},{9,8},{10,11... | collective-permute-start | bytes 294920 | tf_op jit(solution)/shard_map/ppermute | solution.py:239
  39.2 1.4 %collective-permute-start.8 = (bf16[2,96,256]{2,1,0:T(8,128)(2,1)S(1)}, bf16[2,96,256]{2,1,0:T(8,128)(2,1)S(1)}, u32[]{:S(2)}, u32[]{:S(2)}) collective-permute-start(bf16[2,96,256]{2,1,0:T(8,128)(2,1)S(1)} %collective-permute-done.7.refs_3_), channel_id=1, source_target_pairs={{0,1},{1,0},{2,3},{3,2},{4,5},{5,4},{6,7},{7,6},{8,9},{9,8},{10,11... | collective-permute-start | bytes 294920 | tf_op jit(solution)/shard_map/ppermute | solution.py:239

commit v5 on v4

v5 whole, which is shorter than its diff:
```python
import functools

import jax
import jax.numpy as jnp
from jax import lax
from jax.experimental import pallas as pl
from jax.experimental.pallas import tpu as pltpu
from jax.sharding import PartitionSpec as P

B = 4096
LANES = 128
EPSILON = 1e-06
CLIP_LIMIT = 0.999
HALF_LN2 = 0.34657359027997264
N_LOADS = 4
GROUP = 8
PACK_VMEM = 62 << 20
AXES = ("row", "col")


def round_up(value, unit):
    return (value + unit - 1) // unit * unit


def band_place(device):
    row, col = device // 2, device % 2
    return col * 4 + row % 4


def pack_kernel(
    own, start_ref, series_ref, out_ref, whole_ref, own_ref, band_ref, load_sems, own_sems, band_sems
):
    total = series_ref.shape[1]
    n_dev, _, own_pad = own_ref.shape
    share = B // GROUP
    tiles = total // LANES
    cuts = [tiles * i // N_LOADS * LANES for i in range(N_LOADS + 1)]
    loads = [
        pltpu.make_async_copy(
            series_ref.at[:, low:high], whole_ref.at[:, low:high], load_sems.at[i]
        )
        for i, (low, high) in enumerate(zip(cuts, cuts[1:]))
    ]
    for load in loads:
        load.start()
    loaded = 0
    stores = []
    for device in range(n_dev):
        while cuts[loaded] < (device + 1) * own:
            loads[loaded].wait()
            loaded += 1
        own_ref[device, :, :own] = whole_ref[:, device * own : (device + 1) * own]
        if own_pad > own:
            own_ref[device, :, own:] = jnp.zeros((8, own_pad - own), jnp.float32)
        store = pltpu.make_async_copy(
            own_ref.at[device], out_ref.at[device, :, :own_pad], own_sems.at[device]
        )
        store.start()
        stores.append(store)
    while loaded < N_LOADS:
        loads[loaded].wait()
        loaded += 1

    start = start_ref[0]
    base = pl.multiple_of(jnp.minimum(start // LANES * LANES, total - B - LANES), LANES)
    rest = start - base
    shift = lax.rem(LANES - rest, LANES)
    lane = lax.broadcasted_iota(jnp.int32, (8, LANES), 1)
    here = lane < LANES - rest
    before = pltpu.roll(whole_ref[:, pl.ds(base, LANES)], shift, 1)
    for tile in range(B // LANES):
        after = pltpu.roll(whole_ref[:, pl.ds(base + (tile + 1) * LANES, LANES)], shift, 1)
        band_ref[:, tile * LANES : (tile + 1) * LANES] = jnp.where(here, before, after)
        before = after
    for device in range(n_dev):
        place = band_place(device)
        store = pltpu.make_async_copy(
            band_ref.at[:, place * share : (place + 1) * share],
            out_ref.at[device, :, own_pad:],
            band_sems.at[device],
        )
        store.start()
        stores.append(store)
    for store in stores:
        store.wait()


def filter_matrix(kept, frames, taps_ref, count_ref, kept_ref):
    n_taps = taps_ref.shape[0]
    reach = n_taps // 2
    shape = (kept, LANES)
    place = lax.broadcasted_iota(jnp.int32, shape, 0)

    def skip(block, carry):
        frame, seen = carry
        seen = seen + kept_ref[block]
        return frame + jnp.where(place >= seen, 8 - kept_ref[block], 0), seen

    frame, _ = lax.fori_loop(0, frames // 8, skip, (place, jnp.int32(0)), unroll=frames <= 128)
    reach_used = count_ref[0]
    tap_sum = jnp.float32(0)
    tap_number = jnp.float32(0)
    for tap in range(n_taps):
        used = abs(tap - reach) <= reach_used
        tap_sum = tap_sum + jnp.where(used, taps_ref[tap], 0.0)
        tap_number = tap_number + jnp.where(used, 1.0, 0.0)
    centre = jnp.full(shape, tap_sum, jnp.float32) / jnp.full(shape, tap_number, jnp.float32)
    pieces = []
    for tile in range(frames // LANES):
        offset = lax.broadcasted_iota(jnp.int32, shape, 1) + tile * LANES - frame
        value = jnp.zeros(shape, jnp.float32)
        for tap in range(n_taps):
            value = jnp.where(offset == tap - reach, taps_ref[tap], value)
        pieces.append(jnp.where(jnp.abs(offset) <= reach_used, value - centre, 0.0))
    return pieces[0] if len(pieces) == 1 else jnp.concatenate(pieces, 1)


def matrix_kernel(taps_ref, count_ref, kept_ref, out_ref):
    kept, frames = out_ref.shape
    out_ref[...] = filter_matrix(kept, frames, taps_ref, count_ref, kept_ref)


def scaled_columns(matrix, raw):
    centered = jnp.dot(
        matrix, raw, precision=lax.Precision.HIGHEST, preferred_element_type=jnp.float32
    )
    spread = jnp.sum(centered * centered, axis=0, keepdims=True)
    return centered * lax.rsqrt(spread + EPSILON)


def scale_band_kernel(first, matrix_ref, raw_ref, band_ref):
    scaled = scaled_columns(matrix_ref[...], raw_ref[:, first:])
    band_ref[...] = scaled[:, : band_ref.shape[1]].astype(jnp.bfloat16)


def scale_own_kernel(end, matrix_ref, raw_ref, own_ref):
    scaled = scaled_columns(matrix_ref[...], raw_ref[:, :end])
    own_ref[...] = scaled.T[: own_ref.shape[0]].astype(jnp.bfloat16)


def fisher_kernel(flips, place_ref, own_ref, *refs):
    pieces = refs[: len(flips)]
    out_ref, made_ref, sems = refs[-3:]
    share = pieces[0].shape[1]
    half = share // 2
    copies = []
    for at, (flip, piece_ref) in enumerate(zip(flips, pieces)):
        for low in (0, half):
            correlation = jnp.dot(
                own_ref[...], piece_ref[:, low : low + half], preferred_element_type=jnp.float32
            )
            c = jnp.clip(correlation, -CLIP_LIMIT, CLIP_LIMIT)
            z_value = HALF_LN2 * (jnp.log2(1.0 + c) - jnp.log2(1.0 - c))
            made_ref[:, at * share + low : at * share + low + half] = z_value.astype(jnp.bfloat16)
        where = pl.multiple_of((place_ref[0] ^ flip) * share, share)
        copy = pltpu.make_async_copy(
            made_ref.at[:, at * share : (at + 1) * share],
            out_ref.at[:, pl.ds(where, share)],
            sems.at[at],
        )
        copy.start()
        copies.append(copy)
    for copy in copies:
        copy.wait()


def fisher_part(place, own_rows, pieces, out):
    flips = [flip for flip, _ in pieces]
    arrays = [array for _, array in pieces]
    own = own_rows.shape[0]
    vmem = pl.BlockSpec(memory_space=pltpu.VMEM)
    specs = [pl.BlockSpec(memory_space=pltpu.SMEM)] + [vmem] * (1 + len(arrays))
    args = [place, own_rows, *arrays]
    aliases = {}
    if out is not None:
        specs.append(pl.BlockSpec(memory_space=pltpu.HBM))
        aliases = {len(args): 0}
        args.append(out)
    return pl.pallas_call(
        functools.partial(fisher_kernel, flips),
        out_shape=jax.ShapeDtypeStruct((own, B), jnp.bfloat16),
        in_specs=specs,
        out_specs=pl.BlockSpec(memory_space=pltpu.HBM),
        scratch_shapes=[
            pltpu.VMEM((own, len(arrays) * arrays[0].shape[1]), jnp.bfloat16),
            pltpu.SemaphoreType.DMA((len(arrays),)),
        ],
        input_output_aliases=aliases,
        compiler_params=pltpu.CompilerParams(vmem_limit_bytes=48 << 20),
    )(*args)


def body(series, tap_values, tap_count, kept_frames, band_start):
    n_row = lax.axis_size("row")
    n_dev = n_row * lax.axis_size("col")
    frames = 8 * n_dev
    kept = frames * 3 // 4
    total = series.shape[1]
    own = total // n_dev
    own_pad = round_up(own, LANES)
    share = B // GROUP
    smem = pl.BlockSpec(memory_space=pltpu.SMEM)
    vmem = pl.BlockSpec(memory_space=pltpu.VMEM)
    hbm = pl.BlockSpec(memory_space=pltpu.HBM)
    params = pltpu.CompilerParams(vmem_limit_bytes=48 << 20)

    packed = pl.pallas_call(
        functools.partial(pack_kernel, own),
        out_shape=jax.ShapeDtypeStruct((n_dev, 8, own_pad + share), jnp.float32),
        in_specs=[smem, hbm],
        out_specs=hbm,
        scratch_shapes=[
            pltpu.VMEM((8, total), jnp.float32),
            pltpu.VMEM((n_dev, 8, own_pad), jnp.float32),
            pltpu.VMEM((8, B), jnp.float32),
            pltpu.SemaphoreType.DMA((N_LOADS,)),
            pltpu.SemaphoreType.DMA((n_dev,)),
            pltpu.SemaphoreType.DMA((n_dev,)),
        ],
        compiler_params=pltpu.CompilerParams(vmem_limit_bytes=PACK_VMEM),
    )(band_start, series)
    raw = lax.all_to_all(packed, AXES, 0, 0, tiled=True).reshape(frames, own_pad + share)
    matrix = pl.pallas_call(
        matrix_kernel,
        out_shape=jax.ShapeDtypeStruct((kept, frames), jnp.float32),
        in_specs=[smem, smem, smem],
        out_specs=vmem,
        compiler_params=params,
    )(tap_values, tap_count, kept_frames)
    block = pl.pallas_call(
        functools.partial(scale_band_kernel, own_pad),
        out_shape=jax.ShapeDtypeStruct((kept, share), jnp.bfloat16),
        in_specs=[vmem, vmem],
        out_specs=vmem,
        compiler_params=params,
    )(matrix, raw)
    own_rows = pl.pallas_call(
        functools.partial(scale_own_kernel, own_pad),
        out_shape=jax.ShapeDtypeStruct((own, kept), jnp.bfloat16),
        in_specs=[vmem, vmem],
        out_specs=vmem,
        compiler_params=params,
    )(matrix, raw)

    def swap_row(x, bits):
        return lax.ppermute(x, "row", [(i, i ^ bits) for i in range(n_row)])

    def swap_col(x):
        return lax.ppermute(x, "col", [(0, 1), (1, 0)])

    place = (lax.axis_index("col") * 4 + lax.axis_index("row") % 4).astype(jnp.int32).reshape(1)
    near = swap_row(block, 2)
    side = swap_row(block, 1)
    across = swap_row(block, 3)
    early = [(0, block), (4, swap_col(block)), (2, near)]
    out = fisher_part(place, own_rows, early, None)
    side, across, out = lax.optimization_barrier((side, across, out))
    late = [(6, swap_col(near)), (1, side), (3, across), (5, swap_col(side)), (7, swap_col(across))]
    out = fisher_part(place, own_rows, late, out)
    return out.T


def solution(mesh):
    placed = (P(("subj", "row", "col"), None), P(), P(), P("subj"), P("subj"))
    return jax.shard_map(
        body, mesh=mesh, in_specs=placed, out_specs=P("subj", ("row", "col")), check_vma=False
    )
```

time: 44.5 us -> 42 us (0.944)
  starting transfers between devices: 14.1 us -> 11.8 us
  Pallas kernels: 10.1 us -> 9.02 us
  waiting for transfers between devices: 17.2 us -> 18.2 us
    all_to_all x1, waiting for transfers between devices: 11.8 us -> 13.9 us  [body(): lax.all_to_all(packed, AXES, 0, 0, tiled=True)]
    ppermute x5 -> x3, starting transfers between devices: 5.56 us -> 3.75 us  [swap_row(): return lax.ppermute(x, 'row', [(i, i ^ bits) for i in range(n_row)])]
    ppermute x5 -> x3, waiting for transfers between devices: 4.5 us -> 3 us  [swap_row(): return lax.ppermute(x, 'row', [(i, i ^ bits) for i in range(n_row)])]
    pallas_call x3, Pallas kernels: 8.63 us -> 7.44 us  [the longest x2 5.13 us: fisher_part(): pl.pallas_call(functools.partial(fisher_kernel, flips), out_shape=jax.Sha...]
    ppermute x4, starting transfers between devices: 1.14 us -> 0.66 us  [swap_col(): return lax.ppermute(x, 'col', [(0, 1), (1, 0)])]
  transfers between devices with their start and end apart: 10 -> 8, of which waited for: 6 -> 6; matrix products, arithmetic and copies ran while one was open for 0% -> 0% of each run, Pallas kernels for 9% -> 8%
where the time goes in v5:
time: 42 us; the launch traced here: 41.7 us
  waiting for transfers between devices  18.2 us (43%)
  starting transfers between devices  11.8 us (28%)
  Pallas kernels  9.02 us (21%)
  between operations  1.37 us (3%)
  local copies, waits for them, and re-layouts  1.31 us (3%)
    all_to_all x1, waiting for transfers between devices, body(): lax.all_to_all(packed, AXES, 0, 0, tiled=True)  13.9 us
    all_to_all x1, starting transfers between devices, body(): lax.all_to_all(packed, AXES, 0, 0, tiled=True)  7.4 us
    pallas_call x2, Pallas kernels, fisher_part(): pl.pallas_call(functools.partial(fisher_kernel, flips), out_shape=jax.Sha...  5.13 us
    ppermute x3, starting transfers between devices, swap_row(): return lax.ppermute(x, 'row', [(i, i ^ bits) for i in range(n_row)])  3.75 us
    ppermute x3, waiting for transfers between devices, swap_row(): return lax.ppermute(x, 'row', [(i, i ^ bits) for i in range(n_row)])  3 us
    pallas_call x1, Pallas kernels, body(): pl.pallas_call(functools.partial(pack_kernel, own), out_shape=jax.ShapeDt...  2.31 us
    unnamed x4, local copies, waits for them, and re-layouts  1.31 us
    ppermute x4, waiting for transfers between devices, swap_col(): return lax.ppermute(x, 'col', [(0, 1), (1, 0)])  1.3 us
  transfers between devices with their start and end apart: 8, of which 6 were waited for; matrix products, arithmetic and copies ran while one was open for 0% of the time, Pallas kernels for 8%

profile of v5, /device:TPU:0, one launch (start us, length us, event | category | flops | bytes accessed | tf_op | source)
XLA Modules:
  0.0 41.7 jit_solution(1977850869381378818)
XLA Ops:
  0.7 2.3 %shard_map.56 = f32[16,8,1280]{2,1,0:T(8,128)} custom-call(s32[1]{0:T(128)S(6)} %copy.9.start_ref, f32[8,11392]{1,0:T(8,128)} %series_ref.1), custom_call_target="tpu_custom_call" | custom-call | tf_op jit(solution)/shard_map/pallas_call | solution.py:207
  3.0 7.4 %all-to-all-start = ((f32[16,8,1280]{2,1,0:T(8,128)}), f32[16,8,1280]{2,1,0:T(8,128)S(1)}, u32[]{:S(2)}, u32[]{:S(2)}) async-start(f32[16,8,1280]{2,1,0:T(8,128)} %shard_map.56), calls=%async_computation | async-start | bytes 1310720 | tf_op jit(solution)/shard_map/all_to_all | solution.py:222
  11.0 0.0 copy-start
  11.0 0.6 %copy-done = f32[17]{0:T(128)S(1)} copy-done((f32[17]{0:T(128)S(1)}, f32[17]{0:T(128)}, u32[]{:S(2)}) %copy-start) | copy-done | bytes 92
  11.7 0.7 %copy-done.1 = s32[16]{0:T(128)S(1)} copy-done((s32[16]{0:T(128)S(1)}, s32[16]{0:T(128)}, u32[]{:S(2)}) %copy-start.1) | copy-done | bytes 88
  12.3 0.7 %shard_map.55.matrix_ref = f32[96,128]{1,0:T(8,128)S(1)} custom-call(f32[17]{0:T(128)S(1)} %copy-done, s32[1]{0:T(128)S(6)} %copy.8.count_ref, s32[16]{0:T(128)S(1)} %copy-done.1), custom_call_target="tpu_custom_call" | custom-call | tf_op jit(solution)/shard_map/pallas_call | solution.py:223
  13.1 13.9 %all-to-all-done = f32[16,8,1280]{2,1,0:T(8,128)S(1)} async-done(((f32[16,8,1280]{2,1,0:T(8,128)}), f32[16,8,1280]{2,1,0:T(8,128)S(1)}, u32[]{:S(2)}, u32[]{:S(2)}) %all-to-all-start) | async-done | bytes 655392 | tf_op jit(solution)/shard_map/all_to_all | solution.py:222
  27.0 0.3 shard_map.58.refs_0_
  27.3 0.1 collective-permute-start.4
  27.5 2.3 %collective-permute-start = (bf16[96,512]{1,0:T(8,128)(2,1)S(1)}, bf16[96,512]{1,0:T(8,128)(2,1)S(1)}, u32[]{:S(2)}, u32[]{:S(2)}) collective-permute-start(bf16[96,512]{1,0:T(8,128)(2,1)S(1)} %shard_map.58.refs_0_), channel_id=1, source_target_pairs={{0,4},{2,6},{4,0},{6,2},{8,12},{10,14},{12,8},{14,10},{1,5},{3,7},... | collective-permute-start | bytes 294920 | tf_op jit(solution)/shard_map/ppermute | solution.py:246
  29.8 0.6 %collective-permute-start.3 = (bf16[96,512]{1,0:T(8,128)(2,1)S(1)}, bf16[96,512]{1,0:T(8,128)(2,1)S(1)}, u32[]{:S(2)}, u32[]{:S(2)}) collective-permute-start(bf16[96,512]{1,0:T(8,128)(2,1)S(1)} %shard_map.58.refs_0_), channel_id=1, source_target_pairs={{0,6},{2,4},{4,2},{6,0},{8,14},{10,12},{12,10},{14,8},{1,7},{3,5},... | collective-permute-start | bytes 294920 | tf_op jit(solution)/shard_map/ppermute | solution.py:246
  30.4 0.8 %collective-permute-start.2 = (bf16[96,512]{1,0:T(8,128)(2,1)S(1)}, bf16[96,512]{1,0:T(8,128)(2,1)S(1)}, u32[]{:S(2)}, u32[]{:S(2)}) collective-permute-start(bf16[96,512]{1,0:T(8,128)(2,1)S(1)} %shard_map.58.refs_0_), channel_id=1, source_target_pairs={{0,2},{2,0},{4,6},{6,4},{8,10},{10,8},{12,14},{14,12},{1,3},{3,1},... | collective-permute-start | bytes 294920 | tf_op jit(solution)/shard_map/ppermute | solution.py:246
  31.2 0.5 %shard_map.57.own_ref = bf16[712,96]{1,0:T(8,128)(2,1)S(1)} custom-call(f32[96,128]{1,0:T(8,128)S(1)} %shard_map.55.matrix_ref, f32[128,1280]{1,0:T(8,128)S(1)} %bitcast.4), custom_call_target="tpu_custom_call" | custom-call | tf_op jit(solution)/shard_map/pallas_call | solution.py:237
  31.7 0.0 collective-permute-done.4.refs_1_
  31.8 1.2 %collective-permute-done.refs_2_ = bf16[96,512]{1,0:T(8,128)(2,1)S(1)} collective-permute-done((bf16[96,512]{1,0:T(8,128)(2,1)S(1)}, bf16[96,512]{1,0:T(8,128)(2,1)S(1)}, u32[]{:S(2)}, u32[]{:S(2)}) %collective-permute-start) | collective-permute-done | bytes 98336 | tf_op jit(solution)/shard_map/ppermute | solution.py:246
  32.9 2.2 %shard_map.59.refs_5_ = bf16[712,4096]{1,0:T(8,128)(2,1)} custom-call(s32[1]{0:T(128)} %bitcast.place_ref, bf16[712,96]{1,0:T(8,128)(2,1)S(1)} %shard_map.57.own_ref, bf16[96,512]{1,0:T(8,128)(2,1)S(1)} %shard_map.58.refs_0_, bf16[96,512]{1,0:T(8,128)(2,1)S(1)} %collective-permute-done.4.refs_1_, bf16[96,512]{1,0:T(8,128)(2,1)S(1)} %collective-permute-done.refs_2_), custom_call_target="tpu_custom_call" | custom-call | tf_op jit(solution)/shard_map/pallas_call | solution.py:179
  35.1 0.5 %collective-permute-done.3.refs_2_ = bf16[96,512]{1,0:T(8,128)(2,1)S(1)} collective-permute-done((bf16[96,512]{1,0:T(8,128)(2,1)S(1)}, bf16[96,512]{1,0:T(8,128)(2,1)S(1)}, u32[]{:S(2)}, u32[]{:S(2)}) %collective-permute-start.3) | collective-permute-done | bytes 98336 | tf_op jit(solution)/shard_map/ppermute | solution.py:246
  35.6 1.4 %collective-permute-done.2.refs_1_ = bf16[96,512]{1,0:T(8,128)(2,1)S(1)} collective-permute-done((bf16[96,512]{1,0:T(8,128)(2,1)S(1)}, bf16[96,512]{1,0:T(8,128)(2,1)S(1)}, u32[]{:S(2)}, u32[]{:S(2)}) %collective-permute-start.2) | collective-permute-done | bytes 98336 | tf_op jit(solution)/shard_map/ppermute | solution.py:246
  36.9 0.0 collective-permute-start.5
  36.9 0.5 %collective-permute-start.1 = (bf16[96,512]{1,0:T(8,128)(2,1)S(1)}, bf16[96,512]{1,0:T(8,128)(2,1)S(1)}, u32[]{:S(2)}, u32[]{:S(2)}) collective-permute-start(bf16[96,512]{1,0:T(8,128)(2,1)S(1)} %collective-permute-done.refs_2_), channel_id=1, source_target_pairs={{0,1},{1,0},{2,3},{3,2},{4,5},{5,4},{6,7},{7,6},{8,9},{9,8},{10,11... | collective-permute-start | bytes 294920 | tf_op jit(solution)/shard_map/ppermute | solution.py:249
  37.4 0.0 collective-permute-start.6
  37.4 0.9 %collective-permute-done.1.refs_0_ = bf16[96,512]{1,0:T(8,128)(2,1)S(1)} collective-permute-done((bf16[96,512]{1,0:T(8,128)(2,1)S(1)}, bf16[96,512]{1,0:T(8,128)(2,1)S(1)}, u32[]{:S(2)}, u32[]{:S(2)}) %collective-permute-start.1) | collective-permute-done | bytes 98336 | tf_op jit(solution)/shard_map/ppermute | solution.py:249
  38.4 0.4 collective-permute-done.6.refs_4_
  38.7 3.0 %shard_map.60 = bf16[712,4096]{1,0:T(8,128)(2,1)} custom-call(s32[1]{0:T(128)} %bitcast.place_ref, bf16[712,96]{1,0:T(8,128)(2,1)S(1)} %shard_map.57.own_ref, bf16[96,512]{1,0:T(8,128)(2,1)S(1)} %collective-permute-done.1.refs_0_, bf16[96,512]{1,0:T(8,128)(2,1)S(1)} %collective-permute-done.2.refs_1_, ...), custom_call_target="tpu_custom_call", output_to_operand_aliasing={{}: (7, {})} | custom-call | tf_op jit(solution)/shard_map/pallas_call | solution.py:179
  (2 shorter events, 0.0 us)
Async XLA Ops:
  3.0 24.0 %all-to-all-start = ((f32[16,8,1280]{2,1,0:T(8,128)}), f32[16,8,1280]{2,1,0:T(8,128)S(1)}, u32[]{:S(2)}, u32[]{:S(2)}) async-start(f32[16,8,1280]{2,1,0:T(8,128)} %shard_map.56), calls=%async_computation | async-start | bytes 1310720 | tf_op jit(solution)/shard_map/all_to_all | solution.py:222
  11.0 0.7 %copy-start = (f32[17]{0:T(128)S(1)}, f32[17]{0:T(128)}, u32[]{:S(2)}) copy-start(f32[17]{0:T(128)} %taps_ref.1) | copy-start | bytes 208
  11.7 0.7 %copy-start.1 = (s32[16]{0:T(128)S(1)}, s32[16]{0:T(128)}, u32[]{:S(2)}) copy-start(s32[16]{0:T(128)} %kept_ref.1) | copy-start | bytes 196
  27.3 4.4 %collective-permute-start.4 = (bf16[96,512]{1,0:T(8,128)(2,1)S(1)}, bf16[96,512]{1,0:T(8,128)(2,1)S(1)}, u32[]{:S(2)}, u32[]{:S(2)}) collective-permute-start(bf16[96,512]{1,0:T(8,128)(2,1)S(1)} %shard_map.58.refs_0_), channel_id=1, source_target_pairs={{0,1},{1,0},{2,3},{3,2},{4,5},{5,4},{6,7},{7,6},{8,9},{9,8},{10,11... | collective-permute-start | bytes 294920 | tf_op jit(solution)/shard_map/ppermute | solution.py:249
  27.5 5.5 %collective-permute-start = (bf16[96,512]{1,0:T(8,128)(2,1)S(1)}, bf16[96,512]{1,0:T(8,128)(2,1)S(1)}, u32[]{:S(2)}, u32[]{:S(2)}) collective-permute-start(bf16[96,512]{1,0:T(8,128)(2,1)S(1)} %shard_map.58.refs_0_), channel_id=1, source_target_pairs={{0,4},{2,6},{4,0},{6,2},{8,12},{10,14},{12,8},{14,10},{1,5},{3,7},... | collective-permute-start | bytes 294920 | tf_op jit(solution)/shard_map/ppermute | solution.py:246
  29.8 5.8 %collective-permute-start.3 = (bf16[96,512]{1,0:T(8,128)(2,1)S(1)}, bf16[96,512]{1,0:T(8,128)(2,1)S(1)}, u32[]{:S(2)}, u32[]{:S(2)}) collective-permute-start(bf16[96,512]{1,0:T(8,128)(2,1)S(1)} %shard_map.58.refs_0_), channel_id=1, source_target_pairs={{0,6},{2,4},{4,2},{6,0},{8,14},{10,12},{12,10},{14,8},{1,7},{3,5},... | collective-permute-start | bytes 294920 | tf_op jit(solution)/shard_map/ppermute | solution.py:246
  30.4 6.6 %collective-permute-start.2 = (bf16[96,512]{1,0:T(8,128)(2,1)S(1)}, bf16[96,512]{1,0:T(8,128)(2,1)S(1)}, u32[]{:S(2)}, u32[]{:S(2)}) collective-permute-start(bf16[96,512]{1,0:T(8,128)(2,1)S(1)} %shard_map.58.refs_0_), channel_id=1, source_target_pairs={{0,2},{2,0},{4,6},{6,4},{8,10},{10,8},{12,14},{14,12},{1,3},{3,1},... | collective-permute-start | bytes 294920 | tf_op jit(solution)/shard_map/ppermute | solution.py:246
  36.9 1.5 %collective-permute-start.5 = (bf16[96,512]{1,0:T(8,128)(2,1)S(1)}, bf16[96,512]{1,0:T(8,128)(2,1)S(1)}, u32[]{:S(2)}, u32[]{:S(2)}) collective-permute-start(bf16[96,512]{1,0:T(8,128)(2,1)S(1)} %collective-permute-done.2.refs_1_), channel_id=1, source_target_pairs={{0,1},{1,0},{2,3},{3,2},{4,5},{5,4},{6,7},{7,6},{8,9},{9,8},{10,11... | collective-permute-start | bytes 294920 | tf_op jit(solution)/shard_map/ppermute | solution.py:249
  36.9 1.5 %collective-permute-start.1 = (bf16[96,512]{1,0:T(8,128)(2,1)S(1)}, bf16[96,512]{1,0:T(8,128)(2,1)S(1)}, u32[]{:S(2)}, u32[]{:S(2)}) collective-permute-start(bf16[96,512]{1,0:T(8,128)(2,1)S(1)} %collective-permute-done.refs_2_), channel_id=1, source_target_pairs={{0,1},{1,0},{2,3},{3,2},{4,5},{5,4},{6,7},{7,6},{8,9},{9,8},{10,11... | collective-permute-start | bytes 294920 | tf_op jit(solution)/shard_map/ppermute | solution.py:249
  37.4 1.3 %collective-permute-start.6 = (bf16[96,512]{1,0:T(8,128)(2,1)S(1)}, bf16[96,512]{1,0:T(8,128)(2,1)S(1)}, u32[]{:S(2)}, u32[]{:S(2)}) collective-permute-start(bf16[96,512]{1,0:T(8,128)(2,1)S(1)} %collective-permute-done.3.refs_2_), channel_id=1, source_target_pairs={{0,1},{1,0},{2,3},{3,2},{4,5},{5,4},{6,7},{7,6},{8,9},{9,8},{10,11... | collective-permute-start | bytes 294920 | tf_op jit(solution)/shard_map/ppermute | solution.py:249

commit v6 on v5

v6 whole, which is shorter than its diff:
```python
import functools

import jax
import jax.numpy as jnp
import numpy as np
from jax import lax
from jax.experimental import pallas as pl
from jax.experimental.pallas import tpu as pltpu
from jax.sharding import PartitionSpec as P

B = 4096
LANES = 128
EPSILON = 1e-06
CLIP_LIMIT = 0.999
HALF_LN2 = 0.34657359027997264
GROUP = 8
AXES = ("row", "col")


def round_up(value, unit):
    return (value + unit - 1) // unit * unit


def band_place(device):
    row, col = device // 2, device % 2
    return col * 4 + row % 4


def shift_band(start_ref, series_ref, band_ref):
    total = series_ref.shape[1]
    start = start_ref[0]
    base = pl.multiple_of(jnp.minimum(start // LANES * LANES, total - B - LANES), LANES)
    rest = start - base
    shift = lax.rem(LANES - rest, LANES)
    lane = lax.broadcasted_iota(jnp.int32, (8, LANES), 1)
    here = lane < LANES - rest
    before = pltpu.roll(series_ref[:, pl.ds(base, LANES)], shift, 1)
    for tile in range(B // LANES):
        after = pltpu.roll(series_ref[:, pl.ds(base + (tile + 1) * LANES, LANES)], shift, 1)
        band_ref[:, tile * LANES : (tile + 1) * LANES] = jnp.where(here, before, after)
        before = after


def own_columns(device, own, own_pad, series_ref):
    columns = series_ref[:, device * own : (device + 1) * own]
    if own_pad > own:
        columns = jnp.concatenate([columns, jnp.zeros((8, own_pad - own), jnp.float32)], 1)
    return columns


def pack_all_kernel(own, start_ref, series_ref, out_ref, band_ref):
    share = B // GROUP
    own_pad = out_ref.shape[2] - share
    shift_band(start_ref, series_ref, band_ref)
    for device in range(out_ref.shape[0]):
        out_ref[device, :, :own_pad] = own_columns(device, own, own_pad, series_ref)
        place = band_place(device)
        out_ref[device, :, own_pad:] = band_ref[:, place * share : (place + 1) * share]


def pack_kernel(own, start_ref, series_ref, straight_ref, cross_ref, band_ref):
    share = B // GROUP
    own_pad = straight_ref.shape[2] - share
    first_core = lax.axis_index("col") == 0
    shift_band(start_ref, series_ref, band_ref)
    for row in range(straight_ref.shape[0]):
        slabs = []
        for device in (2 * row, 2 * row + 1):
            place = band_place(device)
            slabs.append(
                (
                    own_columns(device, own, own_pad, series_ref),
                    band_ref[:, place * share : (place + 1) * share],
                )
            )
        for (low, high), zero, one in zip(((0, own_pad), (own_pad, own_pad + share)), *slabs):
            straight_ref[row, :, low:high] = jnp.where(first_core, zero, one)
            cross_ref[row, :, low:high] = jnp.where(first_core, one, zero)


def merge_kernel(straight_ref, crossed_ref, *out_refs):
    row = lax.axis_index("row")
    for mask, out_ref in enumerate(out_refs):
        out_ref[:8] = straight_ref[row ^ mask]
        out_ref[8:] = crossed_ref[row ^ mask]


def filter_matrix(kept, frames, turn, taps_ref, count_ref, kept_ref):
    n_taps = taps_ref.shape[0]
    reach = n_taps // 2
    shape = (kept, LANES)
    place = lax.broadcasted_iota(jnp.int32, shape, 0)

    def skip(block, carry):
        frame, seen = carry
        seen = seen + kept_ref[block]
        return frame + jnp.where(place >= seen, 8 - kept_ref[block], 0), seen

    frame, _ = lax.fori_loop(0, frames // 8, skip, (place, jnp.int32(0)), unroll=frames <= 128)
    reach_used = count_ref[0]
    tap_sum = jnp.float32(0)
    tap_number = jnp.float32(0)
    for tap in range(n_taps):
        used = abs(tap - reach) <= reach_used
        tap_sum = tap_sum + jnp.where(used, taps_ref[tap], 0.0)
        tap_number = tap_number + jnp.where(used, 1.0, 0.0)
    centre = jnp.full(shape, tap_sum, jnp.float32) / jnp.full(shape, tap_number, jnp.float32)
    pieces = []
    for tile in range(frames // LANES):
        offset = ((lax.broadcasted_iota(jnp.int32, shape, 1) + tile * LANES) ^ turn) - frame
        value = jnp.zeros(shape, jnp.float32)
        for tap in range(n_taps):
            value = jnp.where(offset == tap - reach, taps_ref[tap], value)
        pieces.append(jnp.where(jnp.abs(offset) <= reach_used, value - centre, 0.0))
    return pieces[0] if len(pieces) == 1 else jnp.concatenate(pieces, 1)


def matrix_kernel(relative, taps_ref, count_ref, kept_ref, out_ref):
    kept, frames = out_ref.shape
    turn = 8 * (2 * lax.axis_index("row") + lax.axis_index("col")) if relative else 0
    out_ref[...] = filter_matrix(kept, frames, turn, taps_ref, count_ref, kept_ref)


def scaled_columns(matrix, raw):
    centered = jnp.dot(
        matrix, raw, precision=lax.Precision.HIGHEST, preferred_element_type=jnp.float32
    )
    spread = jnp.sum(centered * centered, axis=0, keepdims=True)
    return centered * lax.rsqrt(spread + EPSILON)


def scale_band_kernel(masks, first, matrix_ref, *refs):
    *raw_refs, band_ref = refs
    raw = jnp.concatenate([raw_refs[i][:, first:] for i in np.argsort(masks)], 0)
    band_ref[...] = scaled_columns(matrix_ref[...], raw).astype(jnp.bfloat16)


def scale_own_kernel(masks, end, matrix_ref, *refs):
    *raw_refs, own_ref = refs
    raw = jnp.concatenate([raw_refs[i][:, :end] for i in np.argsort(masks)], 0)
    scaled = scaled_columns(matrix_ref[...], raw)
    own_ref[...] = scaled.T[: own_ref.shape[0]].astype(jnp.bfloat16)


def fisher_kernel(flips, own_ref, *refs):
    pieces = refs[: len(flips)]
    out_ref, made_ref, sems = refs[-3:]
    share = pieces[0].shape[1]
    half = share // 2
    place = lax.axis_index("col") * 4 + lax.axis_index("row") % 4
    copies = []
    for at, (flip, piece_ref) in enumerate(zip(flips, pieces)):
        for low in (0, half):
            correlation = jnp.dot(
                own_ref[...], piece_ref[:, low : low + half], preferred_element_type=jnp.float32
            )
            c = jnp.clip(correlation, -CLIP_LIMIT, CLIP_LIMIT)
            z_value = HALF_LN2 * (jnp.log2(1.0 + c) - jnp.log2(1.0 - c))
            made_ref[:, at * share + low : at * share + low + half] = z_value.astype(jnp.bfloat16)
        where = pl.multiple_of((place ^ flip) * share, share)
        copy = pltpu.make_async_copy(
            made_ref.at[:, at * share : (at + 1) * share],
            out_ref.at[:, pl.ds(where, share)],
            sems.at[at],
        )
        copy.start()
        copies.append(copy)
    for copy in copies:
        copy.wait()


def fisher_part(own_rows, pieces, out):
    flips = [flip for flip, _ in pieces]
    arrays = [array for _, array in pieces]
    own = own_rows.shape[0]
    vmem = pl.BlockSpec(memory_space=pltpu.VMEM)
    specs = [vmem] * (1 + len(arrays))
    args = [own_rows, *arrays]
    aliases = {}
    if out is not None:
        specs.append(pl.BlockSpec(memory_space=pltpu.HBM))
        aliases = {len(args): 0}
        args.append(out)
    return pl.pallas_call(
        functools.partial(fisher_kernel, flips),
        out_shape=jax.ShapeDtypeStruct((own, B), jnp.bfloat16),
        in_specs=specs,
        out_specs=pl.BlockSpec(memory_space=pltpu.HBM),
        scratch_shapes=[
            pltpu.VMEM((own, len(arrays) * arrays[0].shape[1]), jnp.bfloat16),
            pltpu.SemaphoreType.DMA((len(arrays),)),
        ],
        input_output_aliases=aliases,
        compiler_params=pltpu.CompilerParams(vmem_limit_bytes=48 << 20),
    )(*args)


def body(series, tap_values, tap_count, kept_frames, band_start):
    n_row = lax.axis_size("row")
    n_dev = n_row * lax.axis_size("col")
    frames = 8 * n_dev
    kept = frames * 3 // 4
    total = series.shape[1]
    own = total // n_dev
    own_pad = round_up(own, LANES)
    share = B // GROUP
    smem = pl.BlockSpec(memory_space=pltpu.SMEM)
    vmem = pl.BlockSpec(memory_space=pltpu.VMEM)
    params = pltpu.CompilerParams(vmem_limit_bytes=24 << 20)
    width = own_pad + share

    def swap_row(x, bits):
        return lax.ppermute(x, "row", [(i, i ^ bits) for i in range(n_row)])

    def swap_col(x):
        return lax.ppermute(x, "col", [(0, 1), (1, 0)])

    relative = n_row <= 8
    matrix = pl.pallas_call(
        functools.partial(matrix_kernel, relative),
        out_shape=jax.ShapeDtypeStruct((kept, frames), jnp.float32),
        in_specs=[smem, smem, smem],
        out_specs=vmem,
        compiler_params=params,
    )(tap_values, tap_count, kept_frames)
    if relative:
        slabs = jax.ShapeDtypeStruct((n_row, 8, width), jnp.float32)
        straight, cross = pl.pallas_call(
            functools.partial(pack_kernel, own),
            out_shape=(slabs, slabs),
            in_specs=[smem, vmem],
            out_specs=(vmem, vmem),
            scratch_shapes=[pltpu.VMEM((8, B), jnp.float32)],
            compiler_params=params,
        )(band_start, series)
        raws = list(pl.pallas_call(
            merge_kernel,
            out_shape=[jax.ShapeDtypeStruct((16, width), jnp.float32)] * n_row,
            in_specs=[vmem, vmem],
            out_specs=[vmem] * n_row,
            compiler_params=params,
        )(straight, swap_col(cross)))
        masks = [*range(n_row // 2, n_row), *range(n_row // 2)]
        raws = [swap_row(raws[mask], mask) if mask else raws[0] for mask in masks]
    else:
        packed = pl.pallas_call(
            functools.partial(pack_all_kernel, own),
            out_shape=jax.ShapeDtypeStruct((n_dev, 8, width), jnp.float32),
            in_specs=[smem, vmem],
            out_specs=vmem,
            scratch_shapes=[pltpu.VMEM((8, B), jnp.float32)],
            compiler_params=params,
        )(band_start, series)
        masks = [0]
        raws = [lax.all_to_all(packed, AXES, 0, 0, tiled=True).reshape(frames, width)]
    block = pl.pallas_call(
        functools.partial(scale_band_kernel, masks, own_pad),
        out_shape=jax.ShapeDtypeStruct((kept, share), jnp.bfloat16),
        in_specs=[vmem] * (1 + len(raws)),
        out_specs=vmem,
        compiler_params=params,
    )(matrix, *raws)
    own_rows = pl.pallas_call(
        functools.partial(scale_own_kernel, masks, own_pad),
        out_shape=jax.ShapeDtypeStruct((own, kept), jnp.bfloat16),
        in_specs=[vmem] * (1 + len(raws)),
        out_specs=vmem,
        compiler_params=params,
    )(matrix, *raws)

    near = swap_row(block, 2)
    side = swap_row(block, 1)
    across = swap_row(block, 3)
    out = fisher_part(own_rows, [(0, block), (4, swap_col(block))], None)
    near, out = lax.optimization_barrier((near, out))
    out = fisher_part(own_rows, [(2, near), (1, side), (6, swap_col(near))], out)
    across, out = lax.optimization_barrier((across, out))
    late = [(5, swap_col(side)), (3, across), (7, swap_col(across))]
    out = fisher_part(own_rows, late, out)
    return out.T


def solution(mesh):
    placed = (P(("subj", "row", "col"), None), P(), P(), P("subj"), P("subj"))
    return jax.shard_map(
        body, mesh=mesh, in_specs=placed, out_specs=P("subj", ("row", "col")), check_vma=False
    )
```

time: 42 us -> 41.6 us (level)
  waiting for transfers between devices: 18.2 us -> 12.5 us
  starting transfers between devices: 11.8 us -> 17.2 us
  Pallas kernels: 9.02 us -> 7.98 us
  local copies, waits for them, and re-layouts: 1.31 us -> 2.28 us
    all_to_all x1 -> x0, waiting for transfers between devices: 13.9 us -> none  [body(): lax.all_to_all(packed, AXES, 0, 0, tiled=True)]
    ppermute x3 -> x10, starting transfers between devices: 3.75 us -> 16.5 us  [swap_row(): return lax.ppermute(x, 'row', [(i, i ^ bits) for i in range(n_row)])]
    all_to_all x1 -> x0, starting transfers between devices: 7.4 us -> none  [body(): lax.all_to_all(packed, AXES, 0, 0, tiled=True)]
    ppermute x3 -> x10, waiting for transfers between devices: 3 us -> 9.66 us  [swap_row(): return lax.ppermute(x, 'row', [(i, i ^ bits) for i in range(n_row)])]
    pallas_call x4 -> x5, Pallas kernels: 3.89 us -> 1.83 us  [the longest x1 0.72 us: body(): pl.pallas_call(functools.partial(matrix_kernel, relative), out_shape=jax....]
    ppermute x4 -> x5, waiting for transfers between devices: 1.3 us -> 2.87 us  [swap_col(): return lax.ppermute(x, 'col', [(0, 1), (1, 0)])]
    pallas_call x2 -> x3, Pallas kernels: 5.13 us -> 6.15 us  [fisher_part(): pl.pallas_call(functools.partial(fisher_kernel, flips), out_shape=jax.Sha...]
    unnamed x4 -> x6, local copies, waits for them, and re-layouts: 1.31 us -> 2.28 us
  transfers between devices with their start and end apart: 8 -> 15, of which waited for: 6 -> 7; matrix products, arithmetic and copies ran while one was open for 0% -> 0% of each run, Pallas kernels for 8% -> 13%
where the time goes in v6:
time: 41.6 us; the launch traced here: 41.4 us
  starting transfers between devices  17.2 us (41%)
  waiting for transfers between devices  12.5 us (30%)
  Pallas kernels  7.98 us (19%)
  local copies, waits for them, and re-layouts  2.28 us (5%)
  between operations  1.43 us (3%)
    ppermute x10, starting transfers between devices, swap_row(): return lax.ppermute(x, 'row', [(i, i ^ bits) for i in range(n_row)])  16.5 us
    ppermute x10, waiting for transfers between devices, swap_row(): return lax.ppermute(x, 'row', [(i, i ^ bits) for i in range(n_row)])  9.66 us
    pallas_call x3, Pallas kernels, fisher_part(): pl.pallas_call(functools.partial(fisher_kernel, flips), out_shape=jax.Sha...  6.15 us
    ppermute x5, waiting for transfers between devices, swap_col(): return lax.ppermute(x, 'col', [(0, 1), (1, 0)])  2.87 us
    unnamed x6, local copies, waits for them, and re-layouts  2.28 us
  transfers between devices with their start and end apart: 15, of which 7 were waited for; matrix products, arithmetic and copies ran while one was open for 0% of the time, Pallas kernels for 13%

profile of v6, /device:TPU:0, one launch (start us, length us, event | category | flops | bytes accessed | tf_op | source)
XLA Modules:
  0.0 41.4 jit_solution(17544713848916537633)
XLA Ops:
  0.7 1.0 %copy-done = f32[8,11392]{1,0:T(8,128)S(1)} copy-done((f32[8,11392]{1,0:T(8,128)S(1)}, f32[8,11392]{1,0:T(8,128)}, u32[]{:S(2)}) %copy-start) | copy-done | bytes 364568
  1.9 0.5 %collective-permute-start = (f32[8,8,1280]{2,1,0:T(8,128)S(1)}, f32[8,8,1280]{2,1,0:T(8,128)S(1)}, u32[]{:S(2)}, u32[]{:S(2)}) collective-permute-start(f32[8,8,1280]{2,1,0:T(8,128)S(1)} %get-tuple-element.20), channel_id=1, source_target_pairs={{0,1},{1,0},{2,3},{3,2},{4,5},{5,4},{6,7},{7,6},{8,9},{9,8},{10,11... | collective-permute-start | bytes 983048 | tf_op jit(solution)/shard_map/ppermute | solution.py:216
  2.4 1.3 %collective-permute-done.crossed_ref = f32[8,8,1280]{2,1,0:T(8,128)S(1)} collective-permute-done((f32[8,8,1280]{2,1,0:T(8,128)S(1)}, f32[8,8,1280]{2,1,0:T(8,128)S(1)}, u32[]{:S(2)}, u32[]{:S(2)}) %collective-permute-start) | collective-permute-done | bytes 327712 | tf_op jit(solution)/shard_map/ppermute | solution.py:216
  3.7 4.0 %collective-permute-start.1 = (f32[16,1280]{1,0:T(8,128)S(1)}, f32[16,1280]{1,0:T(8,128)S(1)}, u32[]{:S(2)}, u32[]{:S(2)}) collective-permute-start(f32[16,1280]{1,0:T(8,128)S(1)} %get-tuple-element.21), channel_id=1, source_target_pairs={{0,8},{2,10},{4,12},{6,14},{8,0},{10,2},{12,4},{14,6},{1,9},{3,11}... | collective-permute-start | bytes 245768 | tf_op jit(solution)/shard_map/ppermute | solution.py:213
  7.7 1.3 %collective-permute-start.2 = (f32[16,1280]{1,0:T(8,128)S(1)}, f32[16,1280]{1,0:T(8,128)S(1)}, u32[]{:S(2)}, u32[]{:S(2)}) collective-permute-start(f32[16,1280]{1,0:T(8,128)S(1)} %get-tuple-element.22), channel_id=1, source_target_pairs={{0,10},{2,8},{4,14},{6,12},{8,2},{10,0},{12,6},{14,4},{1,11},{3,9}... | collective-permute-start | bytes 245768 | tf_op jit(solution)/shard_map/ppermute | solution.py:213
  9.0 3.6 %collective-permute-start.3 = (f32[16,1280]{1,0:T(8,128)S(1)}, f32[16,1280]{1,0:T(8,128)S(1)}, u32[]{:S(2)}, u32[]{:S(2)}) collective-permute-start(f32[16,1280]{1,0:T(8,128)S(1)} %get-tuple-element.23), channel_id=1, source_target_pairs={{0,12},{2,14},{4,8},{6,10},{8,4},{10,6},{12,0},{14,2},{1,13},{3,15... | collective-permute-start | bytes 245768 | tf_op jit(solution)/shard_map/ppermute | solution.py:213
  12.6 1.7 %collective-permute-start.5 = (f32[16,1280]{1,0:T(8,128)S(1)}, f32[16,1280]{1,0:T(8,128)S(1)}, u32[]{:S(2)}, u32[]{:S(2)}) collective-permute-start(f32[16,1280]{1,0:T(8,128)S(1)} %get-tuple-element.26), channel_id=1, source_target_pairs={{0,2},{2,0},{4,6},{6,4},{8,10},{10,8},{12,14},{14,12},{1,3},{3,1},... | collective-permute-start | bytes 245768 | tf_op jit(solution)/shard_map/ppermute | solution.py:213
  14.3 4.0 %collective-permute-start.6 = (f32[16,1280]{1,0:T(8,128)S(1)}, f32[16,1280]{1,0:T(8,128)S(1)}, u32[]{:S(2)}, u32[]{:S(2)}) collective-permute-start(f32[16,1280]{1,0:T(8,128)S(1)} %get-tuple-element.27), channel_id=1, source_target_pairs={{0,4},{2,6},{4,0},{6,2},{8,12},{10,14},{12,8},{14,10},{1,5},{3,7},... | collective-permute-start | bytes 245768 | tf_op jit(solution)/shard_map/ppermute | solution.py:213
  18.3 2.6 %collective-permute-done.2.refs_1_ = f32[16,1280]{1,0:T(8,128)S(1)} collective-permute-done((f32[16,1280]{1,0:T(8,128)S(1)}, f32[16,1280]{1,0:T(8,128)S(1)}, u32[]{:S(2)}, u32[]{:S(2)}) %collective-permute-start.2) | collective-permute-done | bytes 81952 | tf_op jit(solution)/shard_map/ppermute | solution.py:213
  21.6 0.6 %copy-done.1 = f32[17]{0:T(128)S(1)} copy-done((f32[17]{0:T(128)S(1)}, f32[17]{0:T(128)}, u32[]{:S(2)}) %copy-start.1) | copy-done | bytes 92
  22.3 0.7 %copy-done.2 = s32[16]{0:T(128)S(1)} copy-done((s32[16]{0:T(128)S(1)}, s32[16]{0:T(128)}, u32[]{:S(2)}) %copy-start.2) | copy-done | bytes 88
  22.9 0.7 %shard_map.55.matrix_ref = f32[96,128]{1,0:T(8,128)S(1)} custom-call(f32[17]{0:T(128)S(1)} %copy-done.1, s32[1]{0:T(128)S(6)} %copy.10.count_ref, s32[16]{0:T(128)S(1)} %copy-done.2), custom_call_target="tpu_custom_call" | custom-call | tf_op jit(solution)/shard_map/pallas_call | solution.py:219
  23.7 2.5 %collective-permute-done.7.refs_7_ = f32[16,1280]{1,0:T(8,128)S(1)} collective-permute-done((f32[16,1280]{1,0:T(8,128)S(1)}, f32[16,1280]{1,0:T(8,128)S(1)}, u32[]{:S(2)}, u32[]{:S(2)}) %collective-permute-start.7) | collective-permute-done | bytes 81952 | tf_op jit(solution)/shard_map/ppermute | solution.py:213
  26.2 0.3 shard_map.59.refs_0_
  26.7 0.9 %collective-permute-start.8 = (bf16[96,512]{1,0:T(8,128)(2,1)S(1)}, bf16[96,512]{1,0:T(8,128)(2,1)S(1)}, u32[]{:S(2)}, u32[]{:S(2)}) collective-permute-start(bf16[96,512]{1,0:T(8,128)(2,1)S(1)} %shard_map.59.refs_0_), channel_id=1, source_target_pairs={{0,2},{2,0},{4,6},{6,4},{8,10},{10,8},{12,14},{14,12},{1,3},{3,1},... | collective-permute-start | bytes 294920 | tf_op jit(solution)/shard_map/ppermute | solution.py:213
  27.6 0.5 %shard_map.58.own_ref = bf16[712,96]{1,0:T(8,128)(2,1)S(1)} custom-call(f32[96,128]{1,0:T(8,128)S(1)} %shard_map.55.matrix_ref, f32[16,1280]{1,0:T(8,128)S(1)} %collective-permute-done.1.refs_0_, f32[16,1280]{1,0:T(8,128)S(1)} %collective-permute-done.2.refs_1_, f32[16,1280]{1,0:T(8,128)S(1)} %collective-permute-done.3.refs_2_, ...), custom_call_target="tpu_custom_call" | custom-call | tf_op jit(solution)/shard_map/pallas_call | solution.py:263
  28.1 1.8 %shard_map.60.refs_3_ = bf16[712,4096]{1,0:T(8,128)(2,1)} custom-call(bf16[712,96]{1,0:T(8,128)(2,1)S(1)} %shard_map.58.own_ref, bf16[96,512]{1,0:T(8,128)(2,1)S(1)} %shard_map.59.refs_0_, bf16[96,512]{1,0:T(8,128)(2,1)S(1)} %collective-permute-done.12.refs_1_), custom_call_target="tpu_custom_call" | custom-call | tf_op jit(solution)/shard_map/pallas_call | solution.py:184
  29.9 1.9 %collective-permute-done.11.refs_0_ = bf16[96,512]{1,0:T(8,128)(2,1)S(1)} collective-permute-done((bf16[96,512]{1,0:T(8,128)(2,1)S(1)}, bf16[96,512]{1,0:T(8,128)(2,1)S(1)}, u32[]{:S(2)}, u32[]{:S(2)}) %collective-permute-start.11) | collective-permute-done | bytes 98336 | tf_op jit(solution)/shard_map/ppermute | solution.py:213
  31.9 0.8 %collective-permute-start.10 = (bf16[96,512]{1,0:T(8,128)(2,1)S(1)}, bf16[96,512]{1,0:T(8,128)(2,1)S(1)}, u32[]{:S(2)}, u32[]{:S(2)}) collective-permute-start(bf16[96,512]{1,0:T(8,128)(2,1)S(1)} %shard_map.59.refs_0_), channel_id=1, source_target_pairs={{0,6},{2,4},{4,2},{6,0},{8,14},{10,12},{12,10},{14,8},{1,7},{3,5},... | collective-permute-start | bytes 294920 | tf_op jit(solution)/shard_map/ppermute | solution.py:213
  32.8 0.3 collective-permute-done.13.refs_2_
  33.2 2.2 %shard_map.61.refs_3_ = bf16[712,4096]{1,0:T(8,128)(2,1)} custom-call(bf16[712,96]{1,0:T(8,128)(2,1)S(1)} %shard_map.58.own_ref, bf16[96,512]{1,0:T(8,128)(2,1)S(1)} %collective-permute-done.11.refs_0_, bf16[96,512]{1,0:T(8,128)(2,1)S(1)} %collective-permute-done.8.refs_1_, ...), custom_call_target="tpu_custom_call", output_to_operand_aliasing={{}: (4, {})} | custom-call | tf_op jit(solution)/shard_map/pallas_call | solution.py:184
  35.3 2.6 %collective-permute-done.10.refs_1_ = bf16[96,512]{1,0:T(8,128)(2,1)S(1)} collective-permute-done((bf16[96,512]{1,0:T(8,128)(2,1)S(1)}, bf16[96,512]{1,0:T(8,128)(2,1)S(1)}, u32[]{:S(2)}, u32[]{:S(2)}) %collective-permute-start.10) | collective-permute-done | bytes 98336 | tf_op jit(solution)/shard_map/ppermute | solution.py:213
  38.0 1.3 %collective-permute-done.14.refs_2_ = bf16[96,512]{1,0:T(8,128)(2,1)S(1)} collective-permute-done((bf16[96,512]{1,0:T(8,128)(2,1)S(1)}, bf16[96,512]{1,0:T(8,128)(2,1)S(1)}, u32[]{:S(2)}, u32[]{:S(2)}) %collective-permute-start.14) | collective-permute-done | bytes 98336 | tf_op jit(solution)/shard_map/ppermute | solution.py:216
  39.3 2.2 %shard_map.62 = bf16[712,4096]{1,0:T(8,128)(2,1)} custom-call(bf16[712,96]{1,0:T(8,128)(2,1)S(1)} %shard_map.58.own_ref, bf16[96,512]{1,0:T(8,128)(2,1)S(1)} %collective-permute-done.9.refs_0_, bf16[96,512]{1,0:T(8,128)(2,1)S(1)} %collective-permute-done.10.refs_1_, ...), custom_call_target="tpu_custom_call", output_to_operand_aliasing={{}: (4, {})} | custom-call | tf_op jit(solution)/shard_map/pallas_call | solution.py:184
  (20 shorter events, 0.7 us)
Async XLA Ops:
  0.7 1.0 %copy-start = (f32[8,11392]{1,0:T(8,128)S(1)}, f32[8,11392]{1,0:T(8,128)}, u32[]{:S(2)}) copy-start(f32[8,11392]{1,0:T(8,128)} %series_ref.1) | copy-start | bytes 1093636
  1.9 1.8 %collective-permute-start = (f32[8,8,1280]{2,1,0:T(8,128)S(1)}, f32[8,8,1280]{2,1,0:T(8,128)S(1)}, u32[]{:S(2)}, u32[]{:S(2)}) collective-permute-start(f32[8,8,1280]{2,1,0:T(8,128)S(1)} %get-tuple-element.20), channel_id=1, source_target_pairs={{0,1},{1,0},{2,3},{3,2},{4,5},{5,4},{6,7},{7,6},{8,9},{9,8},{10,11... | collective-permute-start | bytes 983048 | tf_op jit(solution)/shard_map/ppermute | solution.py:216
  3.7 10.6 %collective-permute-start.1 = (f32[16,1280]{1,0:T(8,128)S(1)}, f32[16,1280]{1,0:T(8,128)S(1)}, u32[]{:S(2)}, u32[]{:S(2)}) collective-permute-start(f32[16,1280]{1,0:T(8,128)S(1)} %get-tuple-element.21), channel_id=1, source_target_pairs={{0,8},{2,10},{4,12},{6,14},{8,0},{10,2},{12,4},{14,6},{1,9},{3,11}... | collective-permute-start | bytes 245768 | tf_op jit(solution)/shard_map/ppermute | solution.py:213
  7.7 13.2 %collective-permute-start.2 = (f32[16,1280]{1,0:T(8,128)S(1)}, f32[16,1280]{1,0:T(8,128)S(1)}, u32[]{:S(2)}, u32[]{:S(2)}) collective-permute-start(f32[16,1280]{1,0:T(8,128)S(1)} %get-tuple-element.22), channel_id=1, source_target_pairs={{0,10},{2,8},{4,14},{6,12},{8,2},{10,0},{12,6},{14,4},{1,11},{3,9}... | collective-permute-start | bytes 245768 | tf_op jit(solution)/shard_map/ppermute | solution.py:213
  9.0 14.7 %collective-permute-start.3 = (f32[16,1280]{1,0:T(8,128)S(1)}, f32[16,1280]{1,0:T(8,128)S(1)}, u32[]{:S(2)}, u32[]{:S(2)}) collective-permute-start(f32[16,1280]{1,0:T(8,128)S(1)} %get-tuple-element.23), channel_id=1, source_target_pairs={{0,12},{2,14},{4,8},{6,10},{8,4},{10,6},{12,0},{14,2},{1,13},{3,15... | collective-permute-start | bytes 245768 | tf_op jit(solution)/shard_map/ppermute | solution.py:213
  12.6 11.1 %collective-permute-start.4 = (f32[16,1280]{1,0:T(8,128)S(1)}, f32[16,1280]{1,0:T(8,128)S(1)}, u32[]{:S(2)}, u32[]{:S(2)}) collective-permute-start(f32[16,1280]{1,0:T(8,128)S(1)} %get-tuple-element.24), channel_id=1, source_target_pairs={{0,14},{2,12},{4,10},{6,8},{8,6},{10,4},{12,2},{14,0},{1,15},{3,13... | collective-permute-start | bytes 245768 | tf_op jit(solution)/shard_map/ppermute | solution.py:213
  12.6 11.1 %collective-permute-start.5 = (f32[16,1280]{1,0:T(8,128)S(1)}, f32[16,1280]{1,0:T(8,128)S(1)}, u32[]{:S(2)}, u32[]{:S(2)}) collective-permute-start(f32[16,1280]{1,0:T(8,128)S(1)} %get-tuple-element.26), channel_id=1, source_target_pairs={{0,2},{2,0},{4,6},{6,4},{8,10},{10,8},{12,14},{14,12},{1,3},{3,1},... | collective-permute-start | bytes 245768 | tf_op jit(solution)/shard_map/ppermute | solution.py:213
  14.3 9.4 %collective-permute-start.6 = (f32[16,1280]{1,0:T(8,128)S(1)}, f32[16,1280]{1,0:T(8,128)S(1)}, u32[]{:S(2)}, u32[]{:S(2)}) collective-permute-start(f32[16,1280]{1,0:T(8,128)S(1)} %get-tuple-element.27), channel_id=1, source_target_pairs={{0,4},{2,6},{4,0},{6,2},{8,12},{10,14},{12,8},{14,10},{1,5},{3,7},... | collective-permute-start | bytes 245768 | tf_op jit(solution)/shard_map/ppermute | solution.py:213
  20.9 5.3 %collective-permute-start.7 = (f32[16,1280]{1,0:T(8,128)S(1)}, f32[16,1280]{1,0:T(8,128)S(1)}, u32[]{:S(2)}, u32[]{:S(2)}) collective-permute-start(f32[16,1280]{1,0:T(8,128)S(1)} %get-tuple-element.28), channel_id=1, source_target_pairs={{0,6},{2,4},{4,2},{6,0},{8,14},{10,12},{12,10},{14,8},{1,7},{3,5},... | collective-permute-start | bytes 245768 | tf_op jit(solution)/shard_map/ppermute | solution.py:213
  21.6 0.7 %copy-start.1 = (f32[17]{0:T(128)S(1)}, f32[17]{0:T(128)}, u32[]{:S(2)}) copy-start(f32[17]{0:T(128)} %taps_ref.1) | copy-start | bytes 208
  22.3 0.7 %copy-start.2 = (s32[16]{0:T(128)S(1)}, s32[16]{0:T(128)}, u32[]{:S(2)}) copy-start(s32[16]{0:T(128)} %kept_ref.1) | copy-start | bytes 196
  26.6 1.6 %collective-permute-start.12 = (bf16[96,512]{1,0:T(8,128)(2,1)S(1)}, bf16[96,512]{1,0:T(8,128)(2,1)S(1)}, u32[]{:S(2)}, u32[]{:S(2)}) collective-permute-start(bf16[96,512]{1,0:T(8,128)(2,1)S(1)} %shard_map.59.refs_0_), channel_id=1, source_target_pairs={{0,1},{1,0},{2,3},{3,2},{4,5},{5,4},{6,7},{7,6},{8,9},{9,8},{10,11... | collective-permute-start | bytes 294920 | tf_op jit(solution)/shard_map/ppermute | solution.py:216
  26.6 5.2 %collective-permute-start.11 = (bf16[96,512]{1,0:T(8,128)(2,1)S(1)}, bf16[96,512]{1,0:T(8,128)(2,1)S(1)}, u32[]{:S(2)}, u32[]{:S(2)}) collective-permute-start(bf16[96,512]{1,0:T(8,128)(2,1)S(1)} %shard_map.59.refs_0_), channel_id=1, source_target_pairs={{0,4},{2,6},{4,0},{6,2},{8,12},{10,14},{12,8},{14,10},{1,5},{3,7},... | collective-permute-start | bytes 294920 | tf_op jit(solution)/shard_map/ppermute | solution.py:213
  26.7 6.0 %collective-permute-start.8 = (bf16[96,512]{1,0:T(8,128)(2,1)S(1)}, bf16[96,512]{1,0:T(8,128)(2,1)S(1)}, u32[]{:S(2)}, u32[]{:S(2)}) collective-permute-start(bf16[96,512]{1,0:T(8,128)(2,1)S(1)} %shard_map.59.refs_0_), channel_id=1, source_target_pairs={{0,2},{2,0},{4,6},{6,4},{8,10},{10,8},{12,14},{14,12},{1,3},{3,1},... | collective-permute-start | bytes 294920 | tf_op jit(solution)/shard_map/ppermute | solution.py:213
  31.9 1.3 %collective-permute-start.13 = (bf16[96,512]{1,0:T(8,128)(2,1)S(1)}, bf16[96,512]{1,0:T(8,128)(2,1)S(1)}, u32[]{:S(2)}, u32[]{:S(2)}) collective-permute-start(bf16[96,512]{1,0:T(8,128)(2,1)S(1)} %collective-permute-done.11.refs_0_), channel_id=1, source_target_pairs={{0,1},{1,0},{2,3},{3,2},{4,5},{5,4},{6,7},{7,6},{8,9},{9,8},{10,11... | collective-permute-start | bytes 294920 | tf_op jit(solution)/shard_map/ppermute | solution.py:216
  31.9 6.1 %collective-permute-start.10 = (bf16[96,512]{1,0:T(8,128)(2,1)S(1)}, bf16[96,512]{1,0:T(8,128)(2,1)S(1)}, u32[]{:S(2)}, u32[]{:S(2)}) collective-permute-start(bf16[96,512]{1,0:T(8,128)(2,1)S(1)} %shard_map.59.refs_0_), channel_id=1, source_target_pairs={{0,6},{2,4},{4,2},{6,0},{8,14},{10,12},{12,10},{14,8},{1,7},{3,5},... | collective-permute-start | bytes 294920 | tf_op jit(solution)/shard_map/ppermute | solution.py:213
  32.7 5.3 %collective-permute-start.9 = (bf16[96,512]{1,0:T(8,128)(2,1)S(1)}, bf16[96,512]{1,0:T(8,128)(2,1)S(1)}, u32[]{:S(2)}, u32[]{:S(2)}) collective-permute-start(bf16[96,512]{1,0:T(8,128)(2,1)S(1)} %collective-permute-done.8.refs_1_), channel_id=1, source_target_pairs={{0,1},{1,0},{2,3},{3,2},{4,5},{5,4},{6,7},{7,6},{8,9},{9,8},{10,11... | collective-permute-start | bytes 294920 | tf_op jit(solution)/shard_map/ppermute | solution.py:216
  38.0 1.3 %collective-permute-start.14 = (bf16[96,512]{1,0:T(8,128)(2,1)S(1)}, bf16[96,512]{1,0:T(8,128)(2,1)S(1)}, u32[]{:S(2)}, u32[]{:S(2)}) collective-permute-start(bf16[96,512]{1,0:T(8,128)(2,1)S(1)} %collective-permute-done.10.refs_1_), channel_id=1, source_target_pairs={{0,1},{1,0},{2,3},{3,2},{4,5},{5,4},{6,7},{7,6},{8,9},{9,8},{10,11... | collective-permute-start | bytes 294920 | tf_op jit(solution)/shard_map/ppermute | solution.py:216

commit v7 on v6

--- a/solution.py
+++ b/solution.py
@@ -240,8 +240,13 @@
             out_specs=[vmem] * n_row,
             compiler_params=params,
         )(straight, swap_col(cross)))
-        masks = [*range(n_row // 2, n_row), *range(n_row // 2)]
-        raws = [swap_row(raws[mask], mask) if mask else raws[0] for mask in masks]
+        arrived = [raws[0]]
+        for mask in range(1, n_row):
+            if mask == n_row // 2 - 1:
+                raws[mask], *arrived = lax.optimization_barrier((raws[mask], *arrived))
+            arrived.append(swap_row(raws[mask], mask))
+        masks = [*range(1, n_row), 0]
+        raws = [arrived[mask] for mask in masks]
     else:
         packed = pl.pallas_call(
             functools.partial(pack_all_kernel, own),
@@ -271,11 +276,10 @@
     near = swap_row(block, 2)
     side = swap_row(block, 1)
     across = swap_row(block, 3)
-    out = fisher_part(own_rows, [(0, block), (4, swap_col(block))], None)
-    near, out = lax.optimization_barrier((near, out))
-    out = fisher_part(own_rows, [(2, near), (1, side), (6, swap_col(near))], out)
-    across, out = lax.optimization_barrier((across, out))
-    late = [(5, swap_col(side)), (3, across), (7, swap_col(across))]
+    early = [(0, block), (4, swap_col(block)), (2, near)]
+    out = fisher_part(own_rows, early, None)
+    side, across, out = lax.optimization_barrier((side, across, out))
+    late = [(6, swap_col(near)), (1, side), (3, across), (5, swap_col(side)), (7, swap_col(across))]
     out = fisher_part(own_rows, late, out)
     return out.T
 

time: 41.6 us -> 39.3 us (0.945)
  waiting for transfers between devices: 12.5 us -> 11.2 us
  Pallas kernels: 7.98 us -> 6.98 us
    ppermute x10, waiting for transfers between devices: 9.66 us -> 8.64 us  [swap_row(): return lax.ppermute(x, 'row', [(i, i ^ bits) for i in range(n_row)])]
    pallas_call x3 -> x2, Pallas kernels: 6.15 us -> 5.14 us  [fisher_part(): pl.pallas_call(functools.partial(fisher_kernel, flips), out_shape=jax.Sha...]
  transfers between devices with their start and end apart: 15 -> 15, of which waited for: 7 -> 9; matrix products, arithmetic and copies ran while one was open for 0% -> 0% of each run, Pallas kernels for 13% -> 9%
where the time goes in v7:
time: 39.3 us; the launch traced here: 39.1 us
  starting transfers between devices  17.3 us (44%)
  waiting for transfers between devices  11.2 us (28%)
  Pallas kernels  6.98 us (18%)
  local copies, waits for them, and re-layouts  2.28 us (6%)
  between operations  1.38 us (4%)
    ppermute x10, starting transfers between devices, swap_row(): return lax.ppermute(x, 'row', [(i, i ^ bits) for i in range(n_row)])  16.1 us
    ppermute x10, waiting for transfers between devices, swap_row(): return lax.ppermute(x, 'row', [(i, i ^ bits) for i in range(n_row)])  8.64 us
    pallas_call x2, Pallas kernels, fisher_part(): pl.pallas_call(functools.partial(fisher_kernel, flips), out_shape=jax.Sha...  5.14 us
    ppermute x5, waiting for transfers between devices, swap_col(): return lax.ppermute(x, 'col', [(0, 1), (1, 0)])  2.56 us
    unnamed x6, local copies, waits for them, and re-layouts  2.28 us
    ppermute x5, starting transfers between devices, swap_col(): return lax.ppermute(x, 'col', [(0, 1), (1, 0)])  1.12 us
  transfers between devices with their start and end apart: 15, of which 9 were waited for; matrix products, arithmetic and copies ran while one was open for 0% of the time, Pallas kernels for 9%

profile of v7, /device:TPU:0, one launch (start us, length us, event | category | flops | bytes accessed | tf_op | source)
XLA Modules:
  0.0 39.1 jit_solution(3615454353385213425)
XLA Ops:
  0.7 1.0 %copy-done = f32[8,11392]{1,0:T(8,128)S(1)} copy-done((f32[8,11392]{1,0:T(8,128)S(1)}, f32[8,11392]{1,0:T(8,128)}, u32[]{:S(2)}) %copy-start) | copy-done | bytes 364568
  1.9 0.5 %collective-permute-start = (f32[8,8,1280]{2,1,0:T(8,128)S(1)}, f32[8,8,1280]{2,1,0:T(8,128)S(1)}, u32[]{:S(2)}, u32[]{:S(2)}) collective-permute-start(f32[8,8,1280]{2,1,0:T(8,128)S(1)} %get-tuple-element.23), channel_id=1, source_target_pairs={{0,1},{1,0},{2,3},{3,2},{4,5},{5,4},{6,7},{7,6},{8,9},{9,8},{10,11... | collective-permute-start | bytes 983048 | tf_op jit(solution)/shard_map/ppermute | solution.py:216
  2.4 1.3 %collective-permute-done.crossed_ref = f32[8,8,1280]{2,1,0:T(8,128)S(1)} collective-permute-done((f32[8,8,1280]{2,1,0:T(8,128)S(1)}, f32[8,8,1280]{2,1,0:T(8,128)S(1)}, u32[]{:S(2)}, u32[]{:S(2)}) %collective-permute-start) | collective-permute-done | bytes 327712 | tf_op jit(solution)/shard_map/ppermute | solution.py:216
  3.7 3.0 %collective-permute-start.1 = (f32[16,1280]{1,0:T(8,128)S(1)}, f32[16,1280]{1,0:T(8,128)S(1)}, u32[]{:S(2)}, u32[]{:S(2)}) collective-permute-start(f32[16,1280]{1,0:T(8,128)S(1)} %get-tuple-element.26), channel_id=1, source_target_pairs={{0,2},{2,0},{4,6},{6,4},{8,10},{10,8},{12,14},{14,12},{1,3},{3,1},... | collective-permute-start | bytes 245768 | tf_op jit(solution)/shard_map/ppermute | solution.py:213
  6.6 1.6 %collective-permute-start.2 = (f32[16,1280]{1,0:T(8,128)S(1)}, f32[16,1280]{1,0:T(8,128)S(1)}, u32[]{:S(2)}, u32[]{:S(2)}) collective-permute-start(f32[16,1280]{1,0:T(8,128)S(1)} %get-tuple-element.27), channel_id=1, source_target_pairs={{0,4},{2,6},{4,0},{6,2},{8,12},{10,14},{12,8},{14,10},{1,5},{3,7},... | collective-permute-start | bytes 245768 | tf_op jit(solution)/shard_map/ppermute | solution.py:213
  8.2 2.6 %collective-permute-start.4 = (f32[16,1280]{1,0:T(8,128)S(1)}, f32[16,1280]{1,0:T(8,128)S(1)}, u32[]{:S(2)}, u32[]{:S(2)}) collective-permute-start(f32[16,1280]{1,0:T(8,128)S(1)} %get-tuple-element.31), channel_id=1, source_target_pairs={{0,8},{2,10},{4,12},{6,14},{8,0},{10,2},{12,4},{14,6},{1,9},{3,11}... | collective-permute-start | bytes 245768 | tf_op jit(solution)/shard_map/ppermute | solution.py:213
  11.1 2.5 %collective-permute-start.6 = (f32[16,1280]{1,0:T(8,128)S(1)}, f32[16,1280]{1,0:T(8,128)S(1)}, u32[]{:S(2)}, u32[]{:S(2)}) collective-permute-start(f32[16,1280]{1,0:T(8,128)S(1)} %get-tuple-element.33), channel_id=1, source_target_pairs={{0,12},{2,14},{4,8},{6,10},{8,4},{10,6},{12,0},{14,2},{1,13},{3,15... | collective-permute-start | bytes 245768 | tf_op jit(solution)/shard_map/ppermute | solution.py:213
  13.6 2.3 %collective-permute-start.7 = (f32[16,1280]{1,0:T(8,128)S(1)}, f32[16,1280]{1,0:T(8,128)S(1)}, u32[]{:S(2)}, u32[]{:S(2)}) collective-permute-start(f32[16,1280]{1,0:T(8,128)S(1)} %get-tuple-element.34), channel_id=1, source_target_pairs={{0,14},{2,12},{4,10},{6,8},{8,6},{10,4},{12,2},{14,0},{1,15},{3,13... | collective-permute-start | bytes 245768 | tf_op jit(solution)/shard_map/ppermute | solution.py:213
  16.5 0.6 %copy-done.1 = f32[17]{0:T(128)S(1)} copy-done((f32[17]{0:T(128)S(1)}, f32[17]{0:T(128)}, u32[]{:S(2)}) %copy-start.1) | copy-done | bytes 92
  17.2 0.7 %copy-done.2 = s32[16]{0:T(128)S(1)} copy-done((s32[16]{0:T(128)S(1)}, s32[16]{0:T(128)}, u32[]{:S(2)}) %copy-start.2) | copy-done | bytes 88
  17.8 0.7 %shard_map.55.matrix_ref = f32[96,128]{1,0:T(8,128)S(1)} custom-call(f32[17]{0:T(128)S(1)} %copy-done.1, s32[1]{0:T(128)S(6)} %copy.8.count_ref, s32[16]{0:T(128)S(1)} %copy-done.2), custom_call_target="tpu_custom_call" | custom-call | tf_op jit(solution)/shard_map/pallas_call | solution.py:219
  18.6 1.2 %collective-permute-done.4.refs_3_ = f32[16,1280]{1,0:T(8,128)S(1)} collective-permute-done((f32[16,1280]{1,0:T(8,128)S(1)}, f32[16,1280]{1,0:T(8,128)S(1)}, u32[]{:S(2)}, u32[]{:S(2)}) %collective-permute-start.4) | collective-permute-done | bytes 81952 | tf_op jit(solution)/shard_map/ppermute | solution.py:213
  19.8 2.2 %collective-permute-done.5.refs_4_ = f32[16,1280]{1,0:T(8,128)S(1)} collective-permute-done((f32[16,1280]{1,0:T(8,128)S(1)}, f32[16,1280]{1,0:T(8,128)S(1)}, u32[]{:S(2)}, u32[]{:S(2)}) %collective-permute-start.5) | collective-permute-done | bytes 81952 | tf_op jit(solution)/shard_map/ppermute | solution.py:213
  22.0 1.6 %collective-permute-done.3.refs_2_ = f32[16,1280]{1,0:T(8,128)S(1)} collective-permute-done((f32[16,1280]{1,0:T(8,128)S(1)}, f32[16,1280]{1,0:T(8,128)S(1)}, u32[]{:S(2)}, u32[]{:S(2)}) %collective-permute-start.3) | collective-permute-done | bytes 81952 | tf_op jit(solution)/shard_map/ppermute | solution.py:213
  24.0 2.4 %collective-permute-start.8 = (bf16[96,512]{1,0:T(8,128)(2,1)S(1)}, bf16[96,512]{1,0:T(8,128)(2,1)S(1)}, u32[]{:S(2)}, u32[]{:S(2)}) collective-permute-start(bf16[96,512]{1,0:T(8,128)(2,1)S(1)} %shard_map.59.refs_0_), channel_id=1, source_target_pairs={{0,4},{2,6},{4,0},{6,2},{8,12},{10,14},{12,8},{14,10},{1,5},{3,7},... | collective-permute-start | bytes 294920 | tf_op jit(solution)/shard_map/ppermute | solution.py:213
  26.4 1.0 %collective-permute-start.11 = (bf16[96,512]{1,0:T(8,128)(2,1)S(1)}, bf16[96,512]{1,0:T(8,128)(2,1)S(1)}, u32[]{:S(2)}, u32[]{:S(2)}) collective-permute-start(bf16[96,512]{1,0:T(8,128)(2,1)S(1)} %shard_map.59.refs_0_), channel_id=1, source_target_pairs={{0,6},{2,4},{4,2},{6,0},{8,14},{10,12},{12,10},{14,8},{1,7},{3,5},... | collective-permute-start | bytes 294920 | tf_op jit(solution)/shard_map/ppermute | solution.py:213
  27.4 0.5 %collective-permute-start.10 = (bf16[96,512]{1,0:T(8,128)(2,1)S(1)}, bf16[96,512]{1,0:T(8,128)(2,1)S(1)}, u32[]{:S(2)}, u32[]{:S(2)}) collective-permute-start(bf16[96,512]{1,0:T(8,128)(2,1)S(1)} %shard_map.59.refs_0_), channel_id=1, source_target_pairs={{0,2},{2,0},{4,6},{6,4},{8,10},{10,8},{12,14},{14,12},{1,3},{3,1},... | collective-permute-start | bytes 294920 | tf_op jit(solution)/shard_map/ppermute | solution.py:213
  28.0 0.5 %shard_map.58.own_ref = bf16[712,96]{1,0:T(8,128)(2,1)S(1)} custom-call(f32[96,128]{1,0:T(8,128)S(1)} %shard_map.55.matrix_ref, f32[16,1280]{1,0:T(8,128)S(1)} %collective-permute-done.1.refs_0_, f32[16,1280]{1,0:T(8,128)S(1)} %collective-permute-done.2.refs_1_, f32[16,1280]{1,0:T(8,128)S(1)} %collective-permute-done.3.refs_2_, ...), custom_call_target="tpu_custom_call" | custom-call | tf_op jit(solution)/shard_map/pallas_call | solution.py:268
  28.5 1.3 %collective-permute-done.8.refs_2_ = bf16[96,512]{1,0:T(8,128)(2,1)S(1)} collective-permute-done((bf16[96,512]{1,0:T(8,128)(2,1)S(1)}, bf16[96,512]{1,0:T(8,128)(2,1)S(1)}, u32[]{:S(2)}, u32[]{:S(2)}) %collective-permute-start.8) | collective-permute-done | bytes 98336 | tf_op jit(solution)/shard_map/ppermute | solution.py:213
  29.8 2.2 %shard_map.60.refs_5_ = bf16[712,4096]{1,0:T(8,128)(2,1)} custom-call(bf16[712,96]{1,0:T(8,128)(2,1)S(1)} %shard_map.58.own_ref, bf16[96,512]{1,0:T(8,128)(2,1)S(1)} %shard_map.59.refs_0_, bf16[96,512]{1,0:T(8,128)(2,1)S(1)} %collective-permute-done.12.refs_1_, bf16[96,512]{1,0:T(8,128)(2,1)S(1)} %collective-permute-done.8.refs_2_), custom_call_target="tpu_custom_call" | custom-call | tf_op jit(solution)/shard_map/pallas_call | solution.py:184
  32.0 1.0 %collective-permute-done.11.refs_2_ = bf16[96,512]{1,0:T(8,128)(2,1)S(1)} collective-permute-done((bf16[96,512]{1,0:T(8,128)(2,1)S(1)}, bf16[96,512]{1,0:T(8,128)(2,1)S(1)}, u32[]{:S(2)}, u32[]{:S(2)}) %collective-permute-start.11) | collective-permute-done | bytes 98336 | tf_op jit(solution)/shard_map/ppermute | solution.py:213
  33.0 1.4 %collective-permute-done.10.refs_1_ = bf16[96,512]{1,0:T(8,128)(2,1)S(1)} collective-permute-done((bf16[96,512]{1,0:T(8,128)(2,1)S(1)}, bf16[96,512]{1,0:T(8,128)(2,1)S(1)}, u32[]{:S(2)}, u32[]{:S(2)}) %collective-permute-start.10) | collective-permute-done | bytes 98336 | tf_op jit(solution)/shard_map/ppermute | solution.py:213
  34.8 0.9 %collective-permute-done.9.refs_0_ = bf16[96,512]{1,0:T(8,128)(2,1)S(1)} collective-permute-done((bf16[96,512]{1,0:T(8,128)(2,1)S(1)}, bf16[96,512]{1,0:T(8,128)(2,1)S(1)}, u32[]{:S(2)}, u32[]{:S(2)}) %collective-permute-start.9) | collective-permute-done | bytes 98336 | tf_op jit(solution)/shard_map/ppermute | solution.py:216
  36.1 3.0 %shard_map.61 = bf16[712,4096]{1,0:T(8,128)(2,1)} custom-call(bf16[712,96]{1,0:T(8,128)(2,1)S(1)} %shard_map.58.own_ref, bf16[96,512]{1,0:T(8,128)(2,1)S(1)} %collective-permute-done.9.refs_0_, bf16[96,512]{1,0:T(8,128)(2,1)S(1)} %collective-permute-done.10.refs_1_, ...), custom_call_target="tpu_custom_call", output_to_operand_aliasing={{}: (6, {})} | custom-call | tf_op jit(solution)/shard_map/pallas_call | solution.py:184
  (19 shorter events, 1.8 us)
Async XLA Ops:
  0.7 1.0 %copy-start = (f32[8,11392]{1,0:T(8,128)S(1)}, f32[8,11392]{1,0:T(8,128)}, u32[]{:S(2)}) copy-start(f32[8,11392]{1,0:T(8,128)} %series_ref.1) | copy-start | bytes 1093636
  1.9 1.8 %collective-permute-start = (f32[8,8,1280]{2,1,0:T(8,128)S(1)}, f32[8,8,1280]{2,1,0:T(8,128)S(1)}, u32[]{:S(2)}, u32[]{:S(2)}) collective-permute-start(f32[8,8,1280]{2,1,0:T(8,128)S(1)} %get-tuple-element.23), channel_id=1, source_target_pairs={{0,1},{1,0},{2,3},{3,2},{4,5},{5,4},{6,7},{7,6},{8,9},{9,8},{10,11... | collective-permute-start | bytes 983048 | tf_op jit(solution)/shard_map/ppermute | solution.py:216
  3.7 9.9 %collective-permute-start.1 = (f32[16,1280]{1,0:T(8,128)S(1)}, f32[16,1280]{1,0:T(8,128)S(1)}, u32[]{:S(2)}, u32[]{:S(2)}) collective-permute-start(f32[16,1280]{1,0:T(8,128)S(1)} %get-tuple-element.26), channel_id=1, source_target_pairs={{0,2},{2,0},{4,6},{6,4},{8,10},{10,8},{12,14},{14,12},{1,3},{3,1},... | collective-permute-start | bytes 245768 | tf_op jit(solution)/shard_map/ppermute | solution.py:213
  6.6 9.2 %collective-permute-start.2 = (f32[16,1280]{1,0:T(8,128)S(1)}, f32[16,1280]{1,0:T(8,128)S(1)}, u32[]{:S(2)}, u32[]{:S(2)}) collective-permute-start(f32[16,1280]{1,0:T(8,128)S(1)} %get-tuple-element.27), channel_id=1, source_target_pairs={{0,4},{2,6},{4,0},{6,2},{8,12},{10,14},{12,8},{14,10},{1,5},{3,7},... | collective-permute-start | bytes 245768 | tf_op jit(solution)/shard_map/ppermute | solution.py:213
  8.2 11.6 %collective-permute-start.4 = (f32[16,1280]{1,0:T(8,128)S(1)}, f32[16,1280]{1,0:T(8,128)S(1)}, u32[]{:S(2)}, u32[]{:S(2)}) collective-permute-start(f32[16,1280]{1,0:T(8,128)S(1)} %get-tuple-element.31), channel_id=1, source_target_pairs={{0,8},{2,10},{4,12},{6,14},{8,0},{10,2},{12,4},{14,6},{1,9},{3,11}... | collective-permute-start | bytes 245768 | tf_op jit(solution)/shard_map/ppermute | solution.py:213
  10.8 11.2 %collective-permute-start.5 = (f32[16,1280]{1,0:T(8,128)S(1)}, f32[16,1280]{1,0:T(8,128)S(1)}, u32[]{:S(2)}, u32[]{:S(2)}) collective-permute-start(f32[16,1280]{1,0:T(8,128)S(1)} %get-tuple-element.32), channel_id=1, source_target_pairs={{0,10},{2,8},{4,14},{6,12},{8,2},{10,0},{12,6},{14,4},{1,11},{3,9}... | collective-permute-start | bytes 245768 | tf_op jit(solution)/shard_map/ppermute | solution.py:213
  11.1 10.9 %collective-permute-start.6 = (f32[16,1280]{1,0:T(8,128)S(1)}, f32[16,1280]{1,0:T(8,128)S(1)}, u32[]{:S(2)}, u32[]{:S(2)}) collective-permute-start(f32[16,1280]{1,0:T(8,128)S(1)} %get-tuple-element.33), channel_id=1, source_target_pairs={{0,12},{2,14},{4,8},{6,10},{8,4},{10,6},{12,0},{14,2},{1,13},{3,15... | collective-permute-start | bytes 245768 | tf_op jit(solution)/shard_map/ppermute | solution.py:213
  13.6 8.5 %collective-permute-start.7 = (f32[16,1280]{1,0:T(8,128)S(1)}, f32[16,1280]{1,0:T(8,128)S(1)}, u32[]{:S(2)}, u32[]{:S(2)}) collective-permute-start(f32[16,1280]{1,0:T(8,128)S(1)} %get-tuple-element.34), channel_id=1, source_target_pairs={{0,14},{2,12},{4,10},{6,8},{8,6},{10,4},{12,2},{14,0},{1,15},{3,13... | collective-permute-start | bytes 245768 | tf_op jit(solution)/shard_map/ppermute | solution.py:213
  15.9 7.7 %collective-permute-start.3 = (f32[16,1280]{1,0:T(8,128)S(1)}, f32[16,1280]{1,0:T(8,128)S(1)}, u32[]{:S(2)}, u32[]{:S(2)}) collective-permute-start(f32[16,1280]{1,0:T(8,128)S(1)} %get-tuple-element.30), channel_id=1, source_target_pairs={{0,6},{2,4},{4,2},{6,0},{8,14},{10,12},{12,10},{14,8},{1,7},{3,5},... | collective-permute-start | bytes 245768 | tf_op jit(solution)/shard_map/ppermute | solution.py:213
  16.5 0.7 %copy-start.1 = (f32[17]{0:T(128)S(1)}, f32[17]{0:T(128)}, u32[]{:S(2)}) copy-start(f32[17]{0:T(128)} %taps_ref.1) | copy-start | bytes 208
  17.2 0.7 %copy-start.2 = (s32[16]{0:T(128)S(1)}, s32[16]{0:T(128)}, u32[]{:S(2)}) copy-start(s32[16]{0:T(128)} %kept_ref.1) | copy-start | bytes 196
  23.9 4.6 %collective-permute-start.12 = (bf16[96,512]{1,0:T(8,128)(2,1)S(1)}, bf16[96,512]{1,0:T(8,128)(2,1)S(1)}, u32[]{:S(2)}, u32[]{:S(2)}) collective-permute-start(bf16[96,512]{1,0:T(8,128)(2,1)S(1)} %shard_map.59.refs_0_), channel_id=1, source_target_pairs={{0,1},{1,0},{2,3},{3,2},{4,5},{5,4},{6,7},{7,6},{8,9},{9,8},{10,11... | collective-permute-start | bytes 294920 | tf_op jit(solution)/shard_map/ppermute | solution.py:216
  24.0 5.8 %collective-permute-start.8 = (bf16[96,512]{1,0:T(8,128)(2,1)S(1)}, bf16[96,512]{1,0:T(8,128)(2,1)S(1)}, u32[]{:S(2)}, u32[]{:S(2)}) collective-permute-start(bf16[96,512]{1,0:T(8,128)(2,1)S(1)} %shard_map.59.refs_0_), channel_id=1, source_target_pairs={{0,4},{2,6},{4,0},{6,2},{8,12},{10,14},{12,8},{14,10},{1,5},{3,7},... | collective-permute-start | bytes 294920 | tf_op jit(solution)/shard_map/ppermute | solution.py:213
  26.4 6.6 %collective-permute-start.11 = (bf16[96,512]{1,0:T(8,128)(2,1)S(1)}, bf16[96,512]{1,0:T(8,128)(2,1)S(1)}, u32[]{:S(2)}, u32[]{:S(2)}) collective-permute-start(bf16[96,512]{1,0:T(8,128)(2,1)S(1)} %shard_map.59.refs_0_), channel_id=1, source_target_pairs={{0,6},{2,4},{4,2},{6,0},{8,14},{10,12},{12,10},{14,8},{1,7},{3,5},... | collective-permute-start | bytes 294920 | tf_op jit(solution)/shard_map/ppermute | solution.py:213
  27.4 6.9 %collective-permute-start.10 = (bf16[96,512]{1,0:T(8,128)(2,1)S(1)}, bf16[96,512]{1,0:T(8,128)(2,1)S(1)}, u32[]{:S(2)}, u32[]{:S(2)}) collective-permute-start(bf16[96,512]{1,0:T(8,128)(2,1)S(1)} %shard_map.59.refs_0_), channel_id=1, source_target_pairs={{0,2},{2,0},{4,6},{6,4},{8,10},{10,8},{12,14},{14,12},{1,3},{3,1},... | collective-permute-start | bytes 294920 | tf_op jit(solution)/shard_map/ppermute | solution.py:213
  34.3 1.5 %collective-permute-start.13 = (bf16[96,512]{1,0:T(8,128)(2,1)S(1)}, bf16[96,512]{1,0:T(8,128)(2,1)S(1)}, u32[]{:S(2)}, u32[]{:S(2)}) collective-permute-start(bf16[96,512]{1,0:T(8,128)(2,1)S(1)} %collective-permute-done.10.refs_1_), channel_id=1, source_target_pairs={{0,1},{1,0},{2,3},{3,2},{4,5},{5,4},{6,7},{7,6},{8,9},{9,8},{10,11... | collective-permute-start | bytes 294920 | tf_op jit(solution)/shard_map/ppermute | solution.py:216
  34.3 1.5 %collective-permute-start.9 = (bf16[96,512]{1,0:T(8,128)(2,1)S(1)}, bf16[96,512]{1,0:T(8,128)(2,1)S(1)}, u32[]{:S(2)}, u32[]{:S(2)}) collective-permute-start(bf16[96,512]{1,0:T(8,128)(2,1)S(1)} %collective-permute-done.8.refs_2_), channel_id=1, source_target_pairs={{0,1},{1,0},{2,3},{3,2},{4,5},{5,4},{6,7},{7,6},{8,9},{9,8},{10,11... | collective-permute-start | bytes 294920 | tf_op jit(solution)/shard_map/ppermute | solution.py:216
  34.8 1.3 %collective-permute-start.14 = (bf16[96,512]{1,0:T(8,128)(2,1)S(1)}, bf16[96,512]{1,0:T(8,128)(2,1)S(1)}, u32[]{:S(2)}, u32[]{:S(2)}) collective-permute-start(bf16[96,512]{1,0:T(8,128)(2,1)S(1)} %collective-permute-done.11.refs_2_), channel_id=1, source_target_pairs={{0,1},{1,0},{2,3},{3,2},{4,5},{5,4},{6,7},{7,6},{8,9},{9,8},{10,11... | collective-permute-start | bytes 294920 | tf_op jit(solution)/shard_map/ppermute | solution.py:216

commit v8 on v6

--- a/solution.py
+++ b/solution.py
@@ -2,7 +2,6 @@
 
 import jax
 import jax.numpy as jnp
-import numpy as np
 from jax import lax
 from jax.experimental import pallas as pl
 from jax.experimental.pallas import tpu as pltpu
@@ -28,7 +27,7 @@
 
 def shift_band(start_ref, series_ref, band_ref):
     total = series_ref.shape[1]
-    start = start_ref[0]
+    start = jnp.max(start_ref[...])
     base = pl.multiple_of(jnp.minimum(start // LANES * LANES, total - B - LANES), LANES)
     rest = start - base
     shift = lax.rem(LANES - rest, LANES)
@@ -78,11 +77,25 @@
             cross_ref[row, :, low:high] = jnp.where(first_core, one, zero)
 
 
-def merge_kernel(straight_ref, crossed_ref, *out_refs):
+def merge_kernel(straight_ref, crossed_ref, own_ref, y_ref, z_ref, *far_refs):
     row = lax.axis_index("row")
-    for mask, out_ref in enumerate(out_refs):
-        out_ref[:8] = straight_ref[row ^ mask]
-        out_ref[8:] = crossed_ref[row ^ mask]
+    spots = [(own_ref, 0), (y_ref, 0), (z_ref, 0), (z_ref, 16), *((ref, 0) for ref in far_refs)]
+    for mask, (out_ref, at) in enumerate(spots):
+        out_ref[at : at + 8] = straight_ref[row ^ mask]
+        out_ref[at + 8 : at + 16] = crossed_ref[row ^ mask]
+
+
+def relay_kernel(y_ref, z_ref, out_ref):
+    out_ref[:16] = y_ref[:16]
+    out_ref[16:] = z_ref[16:]
+
+
+def frames_of(refs, low, high):
+    if len(refs) == 1:
+        return refs[0][:, low:high]
+    *far_refs, y_ref, z_ref, own_ref = refs
+    near = [own_ref[...], y_ref[:16], z_ref[:16], y_ref[16:]]
+    return jnp.concatenate([part[:, low:high] for part in near + [ref[...] for ref in far_refs]], 0)
 
 
 def filter_matrix(kept, frames, turn, taps_ref, count_ref, kept_ref):
@@ -129,15 +142,15 @@
     return centered * lax.rsqrt(spread + EPSILON)
 
 
-def scale_band_kernel(masks, first, matrix_ref, *refs):
+def scale_band_kernel(first, matrix_ref, *refs):
     *raw_refs, band_ref = refs
-    raw = jnp.concatenate([raw_refs[i][:, first:] for i in np.argsort(masks)], 0)
+    raw = frames_of(raw_refs, first, first + band_ref.shape[1])
     band_ref[...] = scaled_columns(matrix_ref[...], raw).astype(jnp.bfloat16)
 
 
-def scale_own_kernel(masks, end, matrix_ref, *refs):
+def scale_own_kernel(end, matrix_ref, *refs):
     *raw_refs, own_ref = refs
-    raw = jnp.concatenate([raw_refs[i][:, :end] for i in np.argsort(masks)], 0)
+    raw = frames_of(raw_refs, 0, end)
     scaled = scaled_columns(matrix_ref[...], raw)
     own_ref[...] = scaled.T[: own_ref.shape[0]].astype(jnp.bfloat16)
 
@@ -215,12 +228,13 @@
     def swap_col(x):
         return lax.ppermute(x, "col", [(0, 1), (1, 0)])
 
-    relative = n_row <= 8
+    relative = n_row == 8
     matrix = pl.pallas_call(
         functools.partial(matrix_kernel, relative),
         out_shape=jax.ShapeDtypeStruct((kept, frames), jnp.float32),
         in_specs=[smem, smem, smem],
         out_specs=vmem,
+        cost_estimate=pl.CostEstimate(flops=10**10, transcendentals=0, bytes_accessed=10**8),
         compiler_params=params,
     )(tap_values, tap_count, kept_frames)
     if relative:
@@ -228,54 +242,62 @@
         straight, cross = pl.pallas_call(
             functools.partial(pack_kernel, own),
             out_shape=(slabs, slabs),
-            in_specs=[smem, vmem],
+            in_specs=[vmem, vmem],
             out_specs=(vmem, vmem),
             scratch_shapes=[pltpu.VMEM((8, B), jnp.float32)],
             compiler_params=params,
-        )(band_start, series)
-        raws = list(pl.pallas_call(
+        )(band_start.reshape(1, 1), series)
+        one, two = (jax.ShapeDtypeStruct((16 * count, width), jnp.float32) for count in (1, 2))
+        own_raw, y_raw, z_raw, *far_raws = pl.pallas_call(
             merge_kernel,
-            out_shape=[jax.ShapeDtypeStruct((16, width), jnp.float32)] * n_row,
+            out_shape=[one, two, two] + [one] * (n_row - 4),
             in_specs=[vmem, vmem],
-            out_specs=[vmem] * n_row,
+            out_specs=[vmem] * (n_row - 1),
             compiler_params=params,
-        )(straight, swap_col(cross)))
-        masks = [*range(n_row // 2, n_row), *range(n_row // 2)]
-        raws = [swap_row(raws[mask], mask) if mask else raws[0] for mask in masks]
+        )(straight, swap_col(cross))
+        raws = [swap_row(raw, mask) for mask, raw in enumerate(far_raws, 4)]
+        z_raw = swap_row(z_raw, 2)
+        y_raw = pl.pallas_call(
+            relay_kernel,
+            out_shape=two,
+            in_specs=[vmem, vmem],
+            out_specs=vmem,
+            input_output_aliases={0: 0},
+            compiler_params=params,
+        )(y_raw, z_raw)
+        raws += [swap_row(y_raw, 1), z_raw, own_raw]
     else:
         packed = pl.pallas_call(
             functools.partial(pack_all_kernel, own),
             out_shape=jax.ShapeDtypeStruct((n_dev, 8, width), jnp.float32),
-            in_specs=[smem, vmem],
+            in_specs=[vmem, vmem],
             out_specs=vmem,
             scratch_shapes=[pltpu.VMEM((8, B), jnp.float32)],
             compiler_params=params,
-        )(band_start, series)
-        masks = [0]
+        )(band_start.reshape(1, 1), series)
         raws = [lax.all_to_all(packed, AXES, 0, 0, tiled=True).reshape(frames, width)]
     block = pl.pallas_call(
-        functools.partial(scale_band_kernel, masks, own_pad),
+        functools.partial(scale_band_kernel, own_pad),
         out_shape=jax.ShapeDtypeStruct((kept, share), jnp.bfloat16),
         in_specs=[vmem] * (1 + len(raws)),
         out_specs=vmem,
         compiler_params=params,
     )(matrix, *raws)
     own_rows = pl.pallas_call(
-        functools.partial(scale_own_kernel, masks, own_pad),
+        functools.partial(scale_own_kernel, own_pad),
         out_shape=jax.ShapeDtypeStruct((own, kept), jnp.bfloat16),
         in_specs=[vmem] * (1 + len(raws)),
         out_specs=vmem,
         compiler_params=params,
     )(matrix, *raws)
 
+    across = swap_row(block, 3)
     near = swap_row(block, 2)
     side = swap_row(block, 1)
-    across = swap_row(block, 3)
     out = fisher_part(own_rows, [(0, block), (4, swap_col(block))], None)
-    near, out = lax.optimization_barrier((near, out))
-    out = fisher_part(own_rows, [(2, near), (1, side), (6, swap_col(near))], out)
     across, out = lax.optimization_barrier((across, out))
-    late = [(5, swap_col(side)), (3, across), (7, swap_col(across))]
+    late = [(2, near), (1, side), (3, across)]
+    late += [(6, swap_col(near)), (5, swap_col(side)), (7, swap_col(across))]
     out = fisher_part(own_rows, late, out)
     return out.T
 

time: 41.6 us -> 38.4 us (0.923)
  waiting for transfers between devices: 12.5 us -> 9.28 us
  starting transfers between devices: 17.2 us -> 18.3 us
  Pallas kernels: 7.98 us -> 7.03 us
    ppermute x10 -> x9, waiting for transfers between devices: 9.66 us -> 6.85 us  [swap_row(): return lax.ppermute(x, 'row', [(i, i ^ bits) for i in range(n_row)])]
    pallas_call x3 -> x2, Pallas kernels: 6.15 us -> 5.14 us  [fisher_part(): pl.pallas_call(functools.partial(fisher_kernel, flips), out_shape=jax.Sha...]
    ppermute x10 -> x9, starting transfers between devices: 16.5 us -> 17.2 us  [swap_row(): return lax.ppermute(x, 'row', [(i, i ^ bits) for i in range(n_row)])]
    ppermute x5, waiting for transfers between devices: 2.87 us -> 2.43 us  [swap_col(): return lax.ppermute(x, 'col', [(0, 1), (1, 0)])]
    pallas_call x3 -> x4, Pallas kernels: 0.9 us -> 0.93 us  [the longest x1 0.53 us: body(): pl.pallas_call(functools.partial(scale_own_kernel, own_pad), out_shape=ja...]
  transfers between devices with their start and end apart: 15 -> 14, of which waited for: 7 -> 8; matrix products, arithmetic and copies ran while one was open for 0% -> 0% of each run, Pallas kernels for 13% -> 8%
where the time goes in v8:
time: 38.4 us; the launch traced here: 38.2 us
  starting transfers between devices  18.3 us (48%)
  waiting for transfers between devices  9.28 us (24%)
  Pallas kernels  7.03 us (18%)
  local copies, waits for them, and re-layouts  2.29 us (6%)
  between operations  1.39 us (4%)
    ppermute x9, starting transfers between devices, swap_row(): return lax.ppermute(x, 'row', [(i, i ^ bits) for i in range(n_row)])  17.2 us
    ppermute x9, waiting for transfers between devices, swap_row(): return lax.ppermute(x, 'row', [(i, i ^ bits) for i in range(n_row)])  6.85 us
    pallas_call x2, Pallas kernels, fisher_part(): pl.pallas_call(functools.partial(fisher_kernel, flips), out_shape=jax.Sha...  5.14 us
    ppermute x5, waiting for transfers between devices, swap_col(): return lax.ppermute(x, 'col', [(0, 1), (1, 0)])  2.43 us
    unnamed x6, local copies, waits for them, and re-layouts  2.29 us
    ppermute x5, starting transfers between devices, swap_col(): return lax.ppermute(x, 'col', [(0, 1), (1, 0)])  1.1 us
  transfers between devices with their start and end apart: 14, of which 8 were waited for; matrix products, arithmetic and copies ran while one was open for 0% of the time, Pallas kernels for 8%

profile of v8, /device:TPU:0, one launch (start us, length us, event | category | flops | bytes accessed | tf_op | source)
XLA Modules:
  0.0 38.2 jit_solution(15686774388178895728)
XLA Ops:
  0.7 1.0 %copy-done = f32[8,11392]{1,0:T(8,128)S(1)} copy-done((f32[8,11392]{1,0:T(8,128)S(1)}, f32[8,11392]{1,0:T(8,128)}, u32[]{:S(2)}) %copy-start) | copy-done | bytes 364568
  1.6 0.2 shard_map.56
  1.9 0.5 %collective-permute-start = (f32[8,8,1280]{2,1,0:T(8,128)S(1)}, f32[8,8,1280]{2,1,0:T(8,128)S(1)}, u32[]{:S(2)}, u32[]{:S(2)}) collective-permute-start(f32[8,8,1280]{2,1,0:T(8,128)S(1)} %get-tuple-element.17), channel_id=1, source_target_pairs={{0,1},{1,0},{2,3},{3,2},{4,5},{5,4},{6,7},{7,6},{8,9},{9,8},{10,11... | collective-permute-start | bytes 983048 | tf_op jit(solution)/shard_map/ppermute | solution.py:229
  2.4 1.3 %collective-permute-done.crossed_ref = f32[8,8,1280]{2,1,0:T(8,128)S(1)} collective-permute-done((f32[8,8,1280]{2,1,0:T(8,128)S(1)}, f32[8,8,1280]{2,1,0:T(8,128)S(1)}, u32[]{:S(2)}, u32[]{:S(2)}) %collective-permute-start) | collective-permute-done | bytes 327712 | tf_op jit(solution)/shard_map/ppermute | solution.py:229
  3.7 3.0 %collective-permute-start.5 = (f32[32,1280]{1,0:T(8,128)S(1)}, f32[32,1280]{1,0:T(8,128)S(1)}, u32[]{:S(2)}, u32[]{:S(2)}) collective-permute-start(f32[32,1280]{1,0:T(8,128)S(1)} %get-tuple-element.23), channel_id=1, source_target_pairs={{0,4},{2,6},{4,0},{6,2},{8,12},{10,14},{12,8},{14,10},{1,5},{3,7},... | collective-permute-start | bytes 491528 | tf_op jit(solution)/shard_map/ppermute | solution.py:226
  7.4 2.7 %collective-permute-start.1 = (f32[16,1280]{1,0:T(8,128)S(1)}, f32[16,1280]{1,0:T(8,128)S(1)}, u32[]{:S(2)}, u32[]{:S(2)}) collective-permute-start(f32[16,1280]{1,0:T(8,128)S(1)} %get-tuple-element.18), channel_id=1, source_target_pairs={{0,8},{2,10},{4,12},{6,14},{8,0},{10,2},{12,4},{14,6},{1,9},{3,11}... | collective-permute-start | bytes 245768 | tf_op jit(solution)/shard_map/ppermute | solution.py:226
  10.0 1.3 %collective-permute-start.2 = (f32[16,1280]{1,0:T(8,128)S(1)}, f32[16,1280]{1,0:T(8,128)S(1)}, u32[]{:S(2)}, u32[]{:S(2)}) collective-permute-start(f32[16,1280]{1,0:T(8,128)S(1)} %get-tuple-element.19), channel_id=1, source_target_pairs={{0,10},{2,8},{4,14},{6,12},{8,2},{10,0},{12,6},{14,4},{1,11},{3,9}... | collective-permute-start | bytes 245768 | tf_op jit(solution)/shard_map/ppermute | solution.py:226
  11.3 2.5 %collective-permute-start.3 = (f32[16,1280]{1,0:T(8,128)S(1)}, f32[16,1280]{1,0:T(8,128)S(1)}, u32[]{:S(2)}, u32[]{:S(2)}) collective-permute-start(f32[16,1280]{1,0:T(8,128)S(1)} %get-tuple-element.20), channel_id=1, source_target_pairs={{0,12},{2,14},{4,8},{6,10},{8,4},{10,6},{12,0},{14,2},{1,13},{3,15... | collective-permute-start | bytes 245768 | tf_op jit(solution)/shard_map/ppermute | solution.py:226
  13.8 1.3 %collective-permute-start.4 = (f32[16,1280]{1,0:T(8,128)S(1)}, f32[16,1280]{1,0:T(8,128)S(1)}, u32[]{:S(2)}, u32[]{:S(2)}) collective-permute-start(f32[16,1280]{1,0:T(8,128)S(1)} %get-tuple-element.21), channel_id=1, source_target_pairs={{0,14},{2,12},{4,10},{6,8},{8,6},{10,4},{12,2},{14,0},{1,15},{3,13... | collective-permute-start | bytes 245768 | tf_op jit(solution)/shard_map/ppermute | solution.py:226
  15.1 1.6 %collective-permute-start.6 = (f32[32,1280]{1,0:T(8,128)S(1)}, f32[32,1280]{1,0:T(8,128)S(1)}, u32[]{:S(2)}, u32[]{:S(2)}) collective-permute-start(f32[32,1280]{1,0:T(8,128)S(1)} %shard_map.58), channel_id=1, source_target_pairs={{0,2},{2,0},{4,6},{6,4},{8,10},{10,8},{12,14},{14,12},{1,3},{3,1},... | collective-permute-start | bytes 491528 | tf_op jit(solution)/shard_map/ppermute | solution.py:226
  16.7 0.7 %copy-done.1 = f32[17]{0:T(128)S(1)} copy-done((f32[17]{0:T(128)S(1)}, f32[17]{0:T(128)}, u32[]{:S(2)}) %copy-start.1) | copy-done | bytes 92
  17.4 0.7 %copy-done.2 = s32[16]{0:T(128)S(1)} copy-done((s32[16]{0:T(128)S(1)}, s32[16]{0:T(128)}, u32[]{:S(2)}) %copy-start.2) | copy-done | bytes 88
  18.0 0.7 %shard_map.55.matrix_ref = f32[96,128]{1,0:T(8,128)S(1)} custom-call(f32[17]{0:T(128)S(1)} %copy-done.1, s32[1]{0:T(128)S(6)} %copy.10.count_ref, s32[16]{0:T(128)S(1)} %copy-done.2), custom_call_target="tpu_custom_call" | custom-call | flops 10000000000 | bytes 100000000 | tf_op jit(solution)/shard_map/pallas_call | solution.py:232
  18.8 4.5 %collective-permute-done.2.refs_1_ = f32[16,1280]{1,0:T(8,128)S(1)} collective-permute-done((f32[16,1280]{1,0:T(8,128)S(1)}, f32[16,1280]{1,0:T(8,128)S(1)}, u32[]{:S(2)}, u32[]{:S(2)}) %collective-permute-start.2) | collective-permute-done | bytes 81952 | tf_op jit(solution)/shard_map/ppermute | solution.py:226
  23.3 0.3 shard_map.60.refs_0_
  23.7 3.8 %collective-permute-start.9 = (bf16[96,512]{1,0:T(8,128)(2,1)S(1)}, bf16[96,512]{1,0:T(8,128)(2,1)S(1)}, u32[]{:S(2)}, u32[]{:S(2)}) collective-permute-start(bf16[96,512]{1,0:T(8,128)(2,1)S(1)} %shard_map.60.refs_0_), channel_id=1, source_target_pairs={{0,6},{2,4},{4,2},{6,0},{8,14},{10,12},{12,10},{14,8},{1,7},{3,5},... | collective-permute-start | bytes 294920 | tf_op jit(solution)/shard_map/ppermute | solution.py:226
  27.6 1.0 %collective-permute-start.8 = (bf16[96,512]{1,0:T(8,128)(2,1)S(1)}, bf16[96,512]{1,0:T(8,128)(2,1)S(1)}, u32[]{:S(2)}, u32[]{:S(2)}) collective-permute-start(bf16[96,512]{1,0:T(8,128)(2,1)S(1)} %shard_map.60.refs_0_), channel_id=1, source_target_pairs={{0,2},{2,0},{4,6},{6,4},{8,10},{10,8},{12,14},{14,12},{1,3},{3,1},... | collective-permute-start | bytes 294920 | tf_op jit(solution)/shard_map/ppermute | solution.py:226
  28.6 0.5 %shard_map.59.own_ref = bf16[712,96]{1,0:T(8,128)(2,1)S(1)} custom-call(f32[96,128]{1,0:T(8,128)S(1)} %shard_map.55.matrix_ref, f32[16,1280]{1,0:T(8,128)S(1)} %collective-permute-done.1.refs_0_, f32[16,1280]{1,0:T(8,128)S(1)} %collective-permute-done.2.refs_1_, f32[16,1280]{1,0:T(8,128)S(1)} %collective-permute-done.3.refs_2_, ...), custom_call_target="tpu_custom_call" | custom-call | tf_op jit(solution)/shard_map/pallas_call | solution.py:286
  29.1 1.8 %shard_map.61.refs_6_ = bf16[712,4096]{1,0:T(8,128)(2,1)} custom-call(bf16[712,96]{1,0:T(8,128)(2,1)S(1)} %shard_map.59.own_ref, bf16[96,512]{1,0:T(8,128)(2,1)S(1)} %shard_map.60.refs_0_, bf16[96,512]{1,0:T(8,128)(2,1)S(1)} %collective-permute-done.10.refs_1_), custom_call_target="tpu_custom_call" | custom-call | tf_op jit(solution)/shard_map/pallas_call | solution.py:197
  31.0 2.0 %collective-permute-done.8.refs_1_ = bf16[96,512]{1,0:T(8,128)(2,1)S(1)} collective-permute-done((bf16[96,512]{1,0:T(8,128)(2,1)S(1)}, bf16[96,512]{1,0:T(8,128)(2,1)S(1)}, u32[]{:S(2)}, u32[]{:S(2)}) %collective-permute-start.8) | collective-permute-done | bytes 98336 | tf_op jit(solution)/shard_map/ppermute | solution.py:226
  33.2 0.4 collective-permute-start.11
  33.7 0.7 %collective-permute-done.12.refs_4_ = bf16[96,512]{1,0:T(8,128)(2,1)S(1)} collective-permute-done((bf16[96,512]{1,0:T(8,128)(2,1)S(1)}, bf16[96,512]{1,0:T(8,128)(2,1)S(1)}, u32[]{:S(2)}, u32[]{:S(2)}) %collective-permute-start.12) | collective-permute-done | bytes 98336 | tf_op jit(solution)/shard_map/ppermute | solution.py:229
  34.5 0.4 collective-permute-done.13.refs_5_
  34.9 3.4 %shard_map.62 = bf16[712,4096]{1,0:T(8,128)(2,1)} custom-call(bf16[712,96]{1,0:T(8,128)(2,1)S(1)} %shard_map.59.own_ref, bf16[96,512]{1,0:T(8,128)(2,1)S(1)} %collective-permute-done.7.refs_0_, bf16[96,512]{1,0:T(8,128)(2,1)S(1)} %collective-permute-done.8.refs_1_, ...), custom_call_target="tpu_custom_call", output_to_operand_aliasing={{}: (7, {})} | custom-call | tf_op jit(solution)/shard_map/pallas_call | solution.py:197
  (18 shorter events, 0.7 us)
Async XLA Ops:
  0.7 1.0 %copy-start = (f32[8,11392]{1,0:T(8,128)S(1)}, f32[8,11392]{1,0:T(8,128)}, u32[]{:S(2)}) copy-start(f32[8,11392]{1,0:T(8,128)} %series_ref.1) | copy-start | bytes 1093636
  1.9 1.8 %collective-permute-start = (f32[8,8,1280]{2,1,0:T(8,128)S(1)}, f32[8,8,1280]{2,1,0:T(8,128)S(1)}, u32[]{:S(2)}, u32[]{:S(2)}) collective-permute-start(f32[8,8,1280]{2,1,0:T(8,128)S(1)} %get-tuple-element.17), channel_id=1, source_target_pairs={{0,1},{1,0},{2,3},{3,2},{4,5},{5,4},{6,7},{7,6},{8,9},{9,8},{10,11... | collective-permute-start | bytes 983048 | tf_op jit(solution)/shard_map/ppermute | solution.py:229
  3.7 11.4 %collective-permute-start.5 = (f32[32,1280]{1,0:T(8,128)S(1)}, f32[32,1280]{1,0:T(8,128)S(1)}, u32[]{:S(2)}, u32[]{:S(2)}) collective-permute-start(f32[32,1280]{1,0:T(8,128)S(1)} %get-tuple-element.23), channel_id=1, source_target_pairs={{0,4},{2,6},{4,0},{6,2},{8,12},{10,14},{12,8},{14,10},{1,5},{3,7},... | collective-permute-start | bytes 491528 | tf_op jit(solution)/shard_map/ppermute | solution.py:226
  7.4 11.4 %collective-permute-start.1 = (f32[16,1280]{1,0:T(8,128)S(1)}, f32[16,1280]{1,0:T(8,128)S(1)}, u32[]{:S(2)}, u32[]{:S(2)}) collective-permute-start(f32[16,1280]{1,0:T(8,128)S(1)} %get-tuple-element.18), channel_id=1, source_target_pairs={{0,8},{2,10},{4,12},{6,14},{8,0},{10,2},{12,4},{14,6},{1,9},{3,11}... | collective-permute-start | bytes 245768 | tf_op jit(solution)/shard_map/ppermute | solution.py:226
  10.0 13.3 %collective-permute-start.2 = (f32[16,1280]{1,0:T(8,128)S(1)}, f32[16,1280]{1,0:T(8,128)S(1)}, u32[]{:S(2)}, u32[]{:S(2)}) collective-permute-start(f32[16,1280]{1,0:T(8,128)S(1)} %get-tuple-element.19), channel_id=1, source_target_pairs={{0,10},{2,8},{4,14},{6,12},{8,2},{10,0},{12,6},{14,4},{1,11},{3,9}... | collective-permute-start | bytes 245768 | tf_op jit(solution)/shard_map/ppermute | solution.py:226
  11.3 12.0 %collective-permute-start.3 = (f32[16,1280]{1,0:T(8,128)S(1)}, f32[16,1280]{1,0:T(8,128)S(1)}, u32[]{:S(2)}, u32[]{:S(2)}) collective-permute-start(f32[16,1280]{1,0:T(8,128)S(1)} %get-tuple-element.20), channel_id=1, source_target_pairs={{0,12},{2,14},{4,8},{6,10},{8,4},{10,6},{12,0},{14,2},{1,13},{3,15... | collective-permute-start | bytes 245768 | tf_op jit(solution)/shard_map/ppermute | solution.py:226
  13.8 9.5 %collective-permute-start.4 = (f32[16,1280]{1,0:T(8,128)S(1)}, f32[16,1280]{1,0:T(8,128)S(1)}, u32[]{:S(2)}, u32[]{:S(2)}) collective-permute-start(f32[16,1280]{1,0:T(8,128)S(1)} %get-tuple-element.21), channel_id=1, source_target_pairs={{0,14},{2,12},{4,10},{6,8},{8,6},{10,4},{12,2},{14,0},{1,15},{3,13... | collective-permute-start | bytes 245768 | tf_op jit(solution)/shard_map/ppermute | solution.py:226
  15.1 8.2 %collective-permute-start.6 = (f32[32,1280]{1,0:T(8,128)S(1)}, f32[32,1280]{1,0:T(8,128)S(1)}, u32[]{:S(2)}, u32[]{:S(2)}) collective-permute-start(f32[32,1280]{1,0:T(8,128)S(1)} %shard_map.58), channel_id=1, source_target_pairs={{0,2},{2,0},{4,6},{6,4},{8,10},{10,8},{12,14},{14,12},{1,3},{3,1},... | collective-permute-start | bytes 491528 | tf_op jit(solution)/shard_map/ppermute | solution.py:226
  16.7 0.7 %copy-start.1 = (f32[17]{0:T(128)S(1)}, f32[17]{0:T(128)}, u32[]{:S(2)}) copy-start(f32[17]{0:T(128)} %taps_ref.1) | copy-start | bytes 208
  17.4 0.7 %copy-start.2 = (s32[16]{0:T(128)S(1)}, s32[16]{0:T(128)}, u32[]{:S(2)}) copy-start(s32[16]{0:T(128)} %kept_ref.1) | copy-start | bytes 196
  23.7 5.5 %collective-permute-start.10 = (bf16[96,512]{1,0:T(8,128)(2,1)S(1)}, bf16[96,512]{1,0:T(8,128)(2,1)S(1)}, u32[]{:S(2)}, u32[]{:S(2)}) collective-permute-start(bf16[96,512]{1,0:T(8,128)(2,1)S(1)} %shard_map.60.refs_0_), channel_id=1, source_target_pairs={{0,1},{1,0},{2,3},{3,2},{4,5},{5,4},{6,7},{7,6},{8,9},{9,8},{10,11... | collective-permute-start | bytes 294920 | tf_op jit(solution)/shard_map/ppermute | solution.py:229
  23.7 7.3 %collective-permute-start.9 = (bf16[96,512]{1,0:T(8,128)(2,1)S(1)}, bf16[96,512]{1,0:T(8,128)(2,1)S(1)}, u32[]{:S(2)}, u32[]{:S(2)}) collective-permute-start(bf16[96,512]{1,0:T(8,128)(2,1)S(1)} %shard_map.60.refs_0_), channel_id=1, source_target_pairs={{0,6},{2,4},{4,2},{6,0},{8,14},{10,12},{12,10},{14,8},{1,7},{3,5},... | collective-permute-start | bytes 294920 | tf_op jit(solution)/shard_map/ppermute | solution.py:226
  27.6 5.5 %collective-permute-start.8 = (bf16[96,512]{1,0:T(8,128)(2,1)S(1)}, bf16[96,512]{1,0:T(8,128)(2,1)S(1)}, u32[]{:S(2)}, u32[]{:S(2)}) collective-permute-start(bf16[96,512]{1,0:T(8,128)(2,1)S(1)} %shard_map.60.refs_0_), channel_id=1, source_target_pairs={{0,2},{2,0},{4,6},{6,4},{8,10},{10,8},{12,14},{14,12},{1,3},{3,1},... | collective-permute-start | bytes 294920 | tf_op jit(solution)/shard_map/ppermute | solution.py:226
  28.6 4.6 %collective-permute-start.7 = (bf16[96,512]{1,0:T(8,128)(2,1)S(1)}, bf16[96,512]{1,0:T(8,128)(2,1)S(1)}, u32[]{:S(2)}, u32[]{:S(2)}) collective-permute-start(bf16[96,512]{1,0:T(8,128)(2,1)S(1)} %shard_map.60.refs_0_), channel_id=1, source_target_pairs={{0,4},{2,6},{4,0},{6,2},{8,12},{10,14},{12,8},{14,10},{1,5},{3,7},... | collective-permute-start | bytes 294920 | tf_op jit(solution)/shard_map/ppermute | solution.py:226
  33.1 1.3 %collective-permute-start.12 = (bf16[96,512]{1,0:T(8,128)(2,1)S(1)}, bf16[96,512]{1,0:T(8,128)(2,1)S(1)}, u32[]{:S(2)}, u32[]{:S(2)}) collective-permute-start(bf16[96,512]{1,0:T(8,128)(2,1)S(1)} %collective-permute-done.8.refs_1_), channel_id=1, source_target_pairs={{0,1},{1,0},{2,3},{3,2},{4,5},{5,4},{6,7},{7,6},{8,9},{9,8},{10,11... | collective-permute-start | bytes 294920 | tf_op jit(solution)/shard_map/ppermute | solution.py:229
  33.2 1.3 %collective-permute-start.11 = (bf16[96,512]{1,0:T(8,128)(2,1)S(1)}, bf16[96,512]{1,0:T(8,128)(2,1)S(1)}, u32[]{:S(2)}, u32[]{:S(2)}) collective-permute-start(bf16[96,512]{1,0:T(8,128)(2,1)S(1)} %collective-permute-done.7.refs_0_), channel_id=1, source_target_pairs={{0,1},{1,0},{2,3},{3,2},{4,5},{5,4},{6,7},{7,6},{8,9},{9,8},{10,11... | collective-permute-start | bytes 294920 | tf_op jit(solution)/shard_map/ppermute | solution.py:229
  33.6 1.3 %collective-permute-start.13 = (bf16[96,512]{1,0:T(8,128)(2,1)S(1)}, bf16[96,512]{1,0:T(8,128)(2,1)S(1)}, u32[]{:S(2)}, u32[]{:S(2)}) collective-permute-start(bf16[96,512]{1,0:T(8,128)(2,1)S(1)} %collective-permute-done.9.refs_2_), channel_id=1, source_target_pairs={{0,1},{1,0},{2,3},{3,2},{4,5},{5,4},{6,7},{7,6},{8,9},{9,8},{10,11... | collective-permute-start | bytes 294920 | tf_op jit(solution)/shard_map/ppermute | solution.py:229

commit v9 on v8

--- a/solution.py
+++ b/solution.py
@@ -77,7 +77,7 @@
             cross_ref[row, :, low:high] = jnp.where(first_core, one, zero)
 
 
-def merge_kernel(straight_ref, crossed_ref, own_ref, y_ref, z_ref, *far_refs):
+def merge_kernel(straight_ref, crossed_ref, _, own_ref, y_ref, z_ref, *far_refs):
     row = lax.axis_index("row")
     spots = [(own_ref, 0), (y_ref, 0), (z_ref, 0), (z_ref, 16), *((ref, 0) for ref in far_refs)]
     for mask, (out_ref, at) in enumerate(spots):
@@ -251,10 +251,10 @@
         own_raw, y_raw, z_raw, *far_raws = pl.pallas_call(
             merge_kernel,
             out_shape=[one, two, two] + [one] * (n_row - 4),
-            in_specs=[vmem, vmem],
+            in_specs=[vmem, vmem, smem],
             out_specs=[vmem] * (n_row - 1),
             compiler_params=params,
-        )(straight, swap_col(cross))
+        )(straight, swap_col(cross), tap_count)
         raws = [swap_row(raw, mask) for mask, raw in enumerate(far_raws, 4)]
         z_raw = swap_row(z_raw, 2)
         y_raw = pl.pallas_call(

time: 38.4 us -> 38.1 us (level)
    ppermute x5, waiting for transfers between devices: 2.43 us -> 1.9 us  [swap_col(): return lax.ppermute(x, 'col', [(0, 1), (1, 0)])]
  transfers between devices with their start and end apart: 14 -> 14, of which waited for: 8 -> 7; matrix products, arithmetic and copies ran while one was open for 0% -> 0% of each run, Pallas kernels for 8% -> 8%
where the time goes in v9:
time: 38.1 us; the launch traced here: 37.9 us
  starting transfers between devices  18 us (47%)
  waiting for transfers between devices  9.11 us (24%)
  Pallas kernels  7.04 us (18%)
  local copies, waits for them, and re-layouts  2.29 us (6%)
  between operations  1.4 us (4%)
    ppermute x9, starting transfers between devices, swap_row(): return lax.ppermute(x, 'row', [(i, i ^ bits) for i in range(n_row)])  16.9 us
    ppermute x9, waiting for transfers between devices, swap_row(): return lax.ppermute(x, 'row', [(i, i ^ bits) for i in range(n_row)])  7.21 us
    pallas_call x2, Pallas kernels, fisher_part(): pl.pallas_call(functools.partial(fisher_kernel, flips), out_shape=jax.Sha...  5.14 us
    unnamed x6, local copies, waits for them, and re-layouts  2.29 us
    ppermute x5, waiting for transfers between devices, swap_col(): return lax.ppermute(x, 'col', [(0, 1), (1, 0)])  1.9 us
    ppermute x5, starting transfers between devices, swap_col(): return lax.ppermute(x, 'col', [(0, 1), (1, 0)])  1.1 us
  transfers between devices with their start and end apart: 14, of which 7 were waited for; matrix products, arithmetic and copies ran while one was open for 0% of the time, Pallas kernels for 8%

profile of v9, /device:TPU:0, one launch (start us, length us, event | category | flops | bytes accessed | tf_op | source)
XLA Modules:
  0.0 37.9 jit_solution(14001226603610250741)
XLA Ops:
  0.7 1.0 %copy-done = f32[8,11392]{1,0:T(8,128)S(1)} copy-done((f32[8,11392]{1,0:T(8,128)S(1)}, f32[8,11392]{1,0:T(8,128)}, u32[]{:S(2)}) %copy-start) | copy-done | bytes 364568
  1.6 0.2 shard_map.56
  1.9 0.5 %collective-permute-start = (f32[8,8,1280]{2,1,0:T(8,128)S(1)}, f32[8,8,1280]{2,1,0:T(8,128)S(1)}, u32[]{:S(2)}, u32[]{:S(2)}) collective-permute-start(f32[8,8,1280]{2,1,0:T(8,128)S(1)} %get-tuple-element.17), channel_id=1, source_target_pairs={{0,1},{1,0},{2,3},{3,2},{4,5},{5,4},{6,7},{7,6},{8,9},{9,8},{10,11... | collective-permute-start | bytes 983048 | tf_op jit(solution)/shard_map/ppermute | solution.py:229
  3.1 0.6 %collective-permute-done.crossed_ref = f32[8,8,1280]{2,1,0:T(8,128)S(1)} collective-permute-done((f32[8,8,1280]{2,1,0:T(8,128)S(1)}, f32[8,8,1280]{2,1,0:T(8,128)S(1)}, u32[]{:S(2)}, u32[]{:S(2)}) %collective-permute-start) | collective-permute-done | bytes 327712 | tf_op jit(solution)/shard_map/ppermute | solution.py:229
  3.7 3.0 %collective-permute-start.5 = (f32[32,1280]{1,0:T(8,128)S(1)}, f32[32,1280]{1,0:T(8,128)S(1)}, u32[]{:S(2)}, u32[]{:S(2)}) collective-permute-start(f32[32,1280]{1,0:T(8,128)S(1)} %get-tuple-element.23), channel_id=1, source_target_pairs={{0,4},{2,6},{4,0},{6,2},{8,12},{10,14},{12,8},{14,10},{1,5},{3,7},... | collective-permute-start | bytes 491528 | tf_op jit(solution)/shard_map/ppermute | solution.py:226
  6.7 2.6 %collective-permute-start.1 = (f32[16,1280]{1,0:T(8,128)S(1)}, f32[16,1280]{1,0:T(8,128)S(1)}, u32[]{:S(2)}, u32[]{:S(2)}) collective-permute-start(f32[16,1280]{1,0:T(8,128)S(1)} %get-tuple-element.18), channel_id=1, source_target_pairs={{0,8},{2,10},{4,12},{6,14},{8,0},{10,2},{12,4},{14,6},{1,9},{3,11}... | collective-permute-start | bytes 245768 | tf_op jit(solution)/shard_map/ppermute | solution.py:226
  9.3 1.3 %collective-permute-start.2 = (f32[16,1280]{1,0:T(8,128)S(1)}, f32[16,1280]{1,0:T(8,128)S(1)}, u32[]{:S(2)}, u32[]{:S(2)}) collective-permute-start(f32[16,1280]{1,0:T(8,128)S(1)} %get-tuple-element.19), channel_id=1, source_target_pairs={{0,10},{2,8},{4,14},{6,12},{8,2},{10,0},{12,6},{14,4},{1,11},{3,9}... | collective-permute-start | bytes 245768 | tf_op jit(solution)/shard_map/ppermute | solution.py:226
  10.6 2.5 %collective-permute-start.3 = (f32[16,1280]{1,0:T(8,128)S(1)}, f32[16,1280]{1,0:T(8,128)S(1)}, u32[]{:S(2)}, u32[]{:S(2)}) collective-permute-start(f32[16,1280]{1,0:T(8,128)S(1)} %get-tuple-element.20), channel_id=1, source_target_pairs={{0,12},{2,14},{4,8},{6,10},{8,4},{10,6},{12,0},{14,2},{1,13},{3,15... | collective-permute-start | bytes 245768 | tf_op jit(solution)/shard_map/ppermute | solution.py:226
  13.1 1.3 %collective-permute-start.4 = (f32[16,1280]{1,0:T(8,128)S(1)}, f32[16,1280]{1,0:T(8,128)S(1)}, u32[]{:S(2)}, u32[]{:S(2)}) collective-permute-start(f32[16,1280]{1,0:T(8,128)S(1)} %get-tuple-element.21), channel_id=1, source_target_pairs={{0,14},{2,12},{4,10},{6,8},{8,6},{10,4},{12,2},{14,0},{1,15},{3,13... | collective-permute-start | bytes 245768 | tf_op jit(solution)/shard_map/ppermute | solution.py:226
  14.4 1.6 %collective-permute-start.6 = (f32[32,1280]{1,0:T(8,128)S(1)}, f32[32,1280]{1,0:T(8,128)S(1)}, u32[]{:S(2)}, u32[]{:S(2)}) collective-permute-start(f32[32,1280]{1,0:T(8,128)S(1)} %shard_map.58), channel_id=1, source_target_pairs={{0,2},{2,0},{4,6},{6,4},{8,10},{10,8},{12,14},{14,12},{1,3},{3,1},... | collective-permute-start | bytes 491528 | tf_op jit(solution)/shard_map/ppermute | solution.py:226
  16.0 0.7 %copy-done.1 = f32[17]{0:T(128)S(1)} copy-done((f32[17]{0:T(128)S(1)}, f32[17]{0:T(128)}, u32[]{:S(2)}) %copy-start.1) | copy-done | bytes 92
  16.6 0.7 %copy-done.2 = s32[16]{0:T(128)S(1)} copy-done((s32[16]{0:T(128)S(1)}, s32[16]{0:T(128)}, u32[]{:S(2)}) %copy-start.2) | copy-done | bytes 88
  17.3 0.7 %shard_map.55.matrix_ref = f32[96,128]{1,0:T(8,128)S(1)} custom-call(f32[17]{0:T(128)S(1)} %copy-done.1, s32[1]{0:T(128)S(6)} %copy.10.count_ref._, s32[16]{0:T(128)S(1)} %copy-done.2), custom_call_target="tpu_custom_call" | custom-call | flops 10000000000 | bytes 100000000 | tf_op jit(solution)/shard_map/pallas_call | solution.py:232
  18.0 4.9 %collective-permute-done.2.refs_1_ = f32[16,1280]{1,0:T(8,128)S(1)} collective-permute-done((f32[16,1280]{1,0:T(8,128)S(1)}, f32[16,1280]{1,0:T(8,128)S(1)}, u32[]{:S(2)}, u32[]{:S(2)}) %collective-permute-start.2) | collective-permute-done | bytes 81952 | tf_op jit(solution)/shard_map/ppermute | solution.py:226
  23.0 0.3 shard_map.60.refs_0_
  23.4 3.8 %collective-permute-start.9 = (bf16[96,512]{1,0:T(8,128)(2,1)S(1)}, bf16[96,512]{1,0:T(8,128)(2,1)S(1)}, u32[]{:S(2)}, u32[]{:S(2)}) collective-permute-start(bf16[96,512]{1,0:T(8,128)(2,1)S(1)} %shard_map.60.refs_0_), channel_id=1, source_target_pairs={{0,6},{2,4},{4,2},{6,0},{8,14},{10,12},{12,10},{14,8},{1,7},{3,5},... | collective-permute-start | bytes 294920 | tf_op jit(solution)/shard_map/ppermute | solution.py:226
  27.2 0.9 %collective-permute-start.8 = (bf16[96,512]{1,0:T(8,128)(2,1)S(1)}, bf16[96,512]{1,0:T(8,128)(2,1)S(1)}, u32[]{:S(2)}, u32[]{:S(2)}) collective-permute-start(bf16[96,512]{1,0:T(8,128)(2,1)S(1)} %shard_map.60.refs_0_), channel_id=1, source_target_pairs={{0,2},{2,0},{4,6},{6,4},{8,10},{10,8},{12,14},{14,12},{1,3},{3,1},... | collective-permute-start | bytes 294920 | tf_op jit(solution)/shard_map/ppermute | solution.py:226
  28.1 0.5 %shard_map.59.own_ref = bf16[712,96]{1,0:T(8,128)(2,1)S(1)} custom-call(f32[96,128]{1,0:T(8,128)S(1)} %shard_map.55.matrix_ref, f32[16,1280]{1,0:T(8,128)S(1)} %collective-permute-done.1.refs_0_, f32[16,1280]{1,0:T(8,128)S(1)} %collective-permute-done.2.refs_1_, f32[16,1280]{1,0:T(8,128)S(1)} %collective-permute-done.3.refs_2_, ...), custom_call_target="tpu_custom_call" | custom-call | tf_op jit(solution)/shard_map/pallas_call | solution.py:286
  28.6 1.8 %shard_map.61.refs_6_ = bf16[712,4096]{1,0:T(8,128)(2,1)} custom-call(bf16[712,96]{1,0:T(8,128)(2,1)S(1)} %shard_map.59.own_ref, bf16[96,512]{1,0:T(8,128)(2,1)S(1)} %shard_map.60.refs_0_, bf16[96,512]{1,0:T(8,128)(2,1)S(1)} %collective-permute-done.10.refs_1_), custom_call_target="tpu_custom_call" | custom-call | tf_op jit(solution)/shard_map/pallas_call | solution.py:197
  30.7 2.0 %collective-permute-done.8.refs_1_ = bf16[96,512]{1,0:T(8,128)(2,1)S(1)} collective-permute-done((bf16[96,512]{1,0:T(8,128)(2,1)S(1)}, bf16[96,512]{1,0:T(8,128)(2,1)S(1)}, u32[]{:S(2)}, u32[]{:S(2)}) %collective-permute-start.8) | collective-permute-done | bytes 98336 | tf_op jit(solution)/shard_map/ppermute | solution.py:226
  32.7 0.5 %collective-permute-start.11 = (bf16[96,512]{1,0:T(8,128)(2,1)S(1)}, bf16[96,512]{1,0:T(8,128)(2,1)S(1)}, u32[]{:S(2)}, u32[]{:S(2)}) collective-permute-start(bf16[96,512]{1,0:T(8,128)(2,1)S(1)} %collective-permute-done.7.refs_0_), channel_id=1, source_target_pairs={{0,1},{1,0},{2,3},{3,2},{4,5},{5,4},{6,7},{7,6},{8,9},{9,8},{10,11... | collective-permute-start | bytes 294920 | tf_op jit(solution)/shard_map/ppermute | solution.py:229
  33.2 0.8 %collective-permute-done.12.refs_4_ = bf16[96,512]{1,0:T(8,128)(2,1)S(1)} collective-permute-done((bf16[96,512]{1,0:T(8,128)(2,1)S(1)}, bf16[96,512]{1,0:T(8,128)(2,1)S(1)}, u32[]{:S(2)}, u32[]{:S(2)}) %collective-permute-start.12) | collective-permute-done | bytes 98336 | tf_op jit(solution)/shard_map/ppermute | solution.py:229
  34.2 0.4 collective-permute-done.13.refs_5_
  34.5 3.4 %shard_map.62 = bf16[712,4096]{1,0:T(8,128)(2,1)} custom-call(bf16[712,96]{1,0:T(8,128)(2,1)S(1)} %shard_map.59.own_ref, bf16[96,512]{1,0:T(8,128)(2,1)S(1)} %collective-permute-done.7.refs_0_, bf16[96,512]{1,0:T(8,128)(2,1)S(1)} %collective-permute-done.8.refs_1_, ...), custom_call_target="tpu_custom_call", output_to_operand_aliasing={{}: (7, {})} | custom-call | tf_op jit(solution)/shard_map/pallas_call | solution.py:197
  (18 shorter events, 0.6 us)
Async XLA Ops:
  0.7 1.0 %copy-start = (f32[8,11392]{1,0:T(8,128)S(1)}, f32[8,11392]{1,0:T(8,128)}, u32[]{:S(2)}) copy-start(f32[8,11392]{1,0:T(8,128)} %series_ref.1) | copy-start | bytes 1093636
  1.9 1.8 %collective-permute-start = (f32[8,8,1280]{2,1,0:T(8,128)S(1)}, f32[8,8,1280]{2,1,0:T(8,128)S(1)}, u32[]{:S(2)}, u32[]{:S(2)}) collective-permute-start(f32[8,8,1280]{2,1,0:T(8,128)S(1)} %get-tuple-element.17), channel_id=1, source_target_pairs={{0,1},{1,0},{2,3},{3,2},{4,5},{5,4},{6,7},{7,6},{8,9},{9,8},{10,11... | collective-permute-start | bytes 983048 | tf_op jit(solution)/shard_map/ppermute | solution.py:229
  3.7 10.7 %collective-permute-start.5 = (f32[32,1280]{1,0:T(8,128)S(1)}, f32[32,1280]{1,0:T(8,128)S(1)}, u32[]{:S(2)}, u32[]{:S(2)}) collective-permute-start(f32[32,1280]{1,0:T(8,128)S(1)} %get-tuple-element.23), channel_id=1, source_target_pairs={{0,4},{2,6},{4,0},{6,2},{8,12},{10,14},{12,8},{14,10},{1,5},{3,7},... | collective-permute-start | bytes 491528 | tf_op jit(solution)/shard_map/ppermute | solution.py:226
  6.7 11.3 %collective-permute-start.1 = (f32[16,1280]{1,0:T(8,128)S(1)}, f32[16,1280]{1,0:T(8,128)S(1)}, u32[]{:S(2)}, u32[]{:S(2)}) collective-permute-start(f32[16,1280]{1,0:T(8,128)S(1)} %get-tuple-element.18), channel_id=1, source_target_pairs={{0,8},{2,10},{4,12},{6,14},{8,0},{10,2},{12,4},{14,6},{1,9},{3,11}... | collective-permute-start | bytes 245768 | tf_op jit(solution)/shard_map/ppermute | solution.py:226
  9.3 13.6 %collective-permute-start.2 = (f32[16,1280]{1,0:T(8,128)S(1)}, f32[16,1280]{1,0:T(8,128)S(1)}, u32[]{:S(2)}, u32[]{:S(2)}) collective-permute-start(f32[16,1280]{1,0:T(8,128)S(1)} %get-tuple-element.19), channel_id=1, source_target_pairs={{0,10},{2,8},{4,14},{6,12},{8,2},{10,0},{12,6},{14,4},{1,11},{3,9}... | collective-permute-start | bytes 245768 | tf_op jit(solution)/shard_map/ppermute | solution.py:226
  10.6 12.4 %collective-permute-start.3 = (f32[16,1280]{1,0:T(8,128)S(1)}, f32[16,1280]{1,0:T(8,128)S(1)}, u32[]{:S(2)}, u32[]{:S(2)}) collective-permute-start(f32[16,1280]{1,0:T(8,128)S(1)} %get-tuple-element.20), channel_id=1, source_target_pairs={{0,12},{2,14},{4,8},{6,10},{8,4},{10,6},{12,0},{14,2},{1,13},{3,15... | collective-permute-start | bytes 245768 | tf_op jit(solution)/shard_map/ppermute | solution.py:226
  13.1 9.9 %collective-permute-start.4 = (f32[16,1280]{1,0:T(8,128)S(1)}, f32[16,1280]{1,0:T(8,128)S(1)}, u32[]{:S(2)}, u32[]{:S(2)}) collective-permute-start(f32[16,1280]{1,0:T(8,128)S(1)} %get-tuple-element.21), channel_id=1, source_target_pairs={{0,14},{2,12},{4,10},{6,8},{8,6},{10,4},{12,2},{14,0},{1,15},{3,13... | collective-permute-start | bytes 245768 | tf_op jit(solution)/shard_map/ppermute | solution.py:226
  14.4 8.6 %collective-permute-start.6 = (f32[32,1280]{1,0:T(8,128)S(1)}, f32[32,1280]{1,0:T(8,128)S(1)}, u32[]{:S(2)}, u32[]{:S(2)}) collective-permute-start(f32[32,1280]{1,0:T(8,128)S(1)} %shard_map.58), channel_id=1, source_target_pairs={{0,2},{2,0},{4,6},{6,4},{8,10},{10,8},{12,14},{14,12},{1,3},{3,1},... | collective-permute-start | bytes 491528 | tf_op jit(solution)/shard_map/ppermute | solution.py:226
  16.0 0.7 %copy-start.1 = (f32[17]{0:T(128)S(1)}, f32[17]{0:T(128)}, u32[]{:S(2)}) copy-start(f32[17]{0:T(128)} %taps_ref.1) | copy-start | bytes 208
  16.6 0.7 %copy-start.2 = (s32[16]{0:T(128)S(1)}, s32[16]{0:T(128)}, u32[]{:S(2)}) copy-start(s32[16]{0:T(128)} %kept_ref.1) | copy-start | bytes 196
  23.3 5.3 %collective-permute-start.10 = (bf16[96,512]{1,0:T(8,128)(2,1)S(1)}, bf16[96,512]{1,0:T(8,128)(2,1)S(1)}, u32[]{:S(2)}, u32[]{:S(2)}) collective-permute-start(bf16[96,512]{1,0:T(8,128)(2,1)S(1)} %shard_map.60.refs_0_), channel_id=1, source_target_pairs={{0,1},{1,0},{2,3},{3,2},{4,5},{5,4},{6,7},{7,6},{8,9},{9,8},{10,11... | collective-permute-start | bytes 294920 | tf_op jit(solution)/shard_map/ppermute | solution.py:229
  23.4 7.3 %collective-permute-start.9 = (bf16[96,512]{1,0:T(8,128)(2,1)S(1)}, bf16[96,512]{1,0:T(8,128)(2,1)S(1)}, u32[]{:S(2)}, u32[]{:S(2)}) collective-permute-start(bf16[96,512]{1,0:T(8,128)(2,1)S(1)} %shard_map.60.refs_0_), channel_id=1, source_target_pairs={{0,6},{2,4},{4,2},{6,0},{8,14},{10,12},{12,10},{14,8},{1,7},{3,5},... | collective-permute-start | bytes 294920 | tf_op jit(solution)/shard_map/ppermute | solution.py:226
  27.2 5.5 %collective-permute-start.8 = (bf16[96,512]{1,0:T(8,128)(2,1)S(1)}, bf16[96,512]{1,0:T(8,128)(2,1)S(1)}, u32[]{:S(2)}, u32[]{:S(2)}) collective-permute-start(bf16[96,512]{1,0:T(8,128)(2,1)S(1)} %shard_map.60.refs_0_), channel_id=1, source_target_pairs={{0,2},{2,0},{4,6},{6,4},{8,10},{10,8},{12,14},{14,12},{1,3},{3,1},... | collective-permute-start | bytes 294920 | tf_op jit(solution)/shard_map/ppermute | solution.py:226
  28.1 4.6 %collective-permute-start.7 = (bf16[96,512]{1,0:T(8,128)(2,1)S(1)}, bf16[96,512]{1,0:T(8,128)(2,1)S(1)}, u32[]{:S(2)}, u32[]{:S(2)}) collective-permute-start(bf16[96,512]{1,0:T(8,128)(2,1)S(1)} %shard_map.60.refs_0_), channel_id=1, source_target_pairs={{0,4},{2,6},{4,0},{6,2},{8,12},{10,14},{12,8},{14,10},{1,5},{3,7},... | collective-permute-start | bytes 294920 | tf_op jit(solution)/shard_map/ppermute | solution.py:226
  32.7 1.3 %collective-permute-start.12 = (bf16[96,512]{1,0:T(8,128)(2,1)S(1)}, bf16[96,512]{1,0:T(8,128)(2,1)S(1)}, u32[]{:S(2)}, u32[]{:S(2)}) collective-permute-start(bf16[96,512]{1,0:T(8,128)(2,1)S(1)} %collective-permute-done.8.refs_1_), channel_id=1, source_target_pairs={{0,1},{1,0},{2,3},{3,2},{4,5},{5,4},{6,7},{7,6},{8,9},{9,8},{10,11... | collective-permute-start | bytes 294920 | tf_op jit(solution)/shard_map/ppermute | solution.py:229
  32.7 1.5 %collective-permute-start.11 = (bf16[96,512]{1,0:T(8,128)(2,1)S(1)}, bf16[96,512]{1,0:T(8,128)(2,1)S(1)}, u32[]{:S(2)}, u32[]{:S(2)}) collective-permute-start(bf16[96,512]{1,0:T(8,128)(2,1)S(1)} %collective-permute-done.7.refs_0_), channel_id=1, source_target_pairs={{0,1},{1,0},{2,3},{3,2},{4,5},{5,4},{6,7},{7,6},{8,9},{9,8},{10,11... | collective-permute-start | bytes 294920 | tf_op jit(solution)/shard_map/ppermute | solution.py:229
  33.2 1.3 %collective-permute-start.13 = (bf16[96,512]{1,0:T(8,128)(2,1)S(1)}, bf16[96,512]{1,0:T(8,128)(2,1)S(1)}, u32[]{:S(2)}, u32[]{:S(2)}) collective-permute-start(bf16[96,512]{1,0:T(8,128)(2,1)S(1)} %collective-permute-done.9.refs_2_), channel_id=1, source_target_pairs={{0,1},{1,0},{2,3},{3,2},{4,5},{5,4},{6,7},{7,6},{8,9},{9,8},{10,11... | collective-permute-start | bytes 294920 | tf_op jit(solution)/shard_map/ppermute | solution.py:229

commit v10 on v9

--- a/solution.py
+++ b/solution.py
@@ -296,8 +296,8 @@
     side = swap_row(block, 1)
     out = fisher_part(own_rows, [(0, block), (4, swap_col(block))], None)
     across, out = lax.optimization_barrier((across, out))
-    late = [(2, near), (1, side), (3, across)]
-    late += [(6, swap_col(near)), (5, swap_col(side)), (7, swap_col(across))]
+    out = fisher_part(own_rows, [(1, side), (2, near), (3, across)], out)
+    late = [(5, swap_col(side)), (6, swap_col(near)), (7, swap_col(across))]
     out = fisher_part(own_rows, late, out)
     return out.T
 

time: 38.1 us -> 37.4 us (0.982)
  waiting for transfers between devices: 9.11 us -> 7.82 us
  Pallas kernels: 7.04 us -> 8.05 us
  starting transfers between devices: 18 us -> 17.5 us
    ppermute x5, waiting for transfers between devices: 1.9 us -> 0.61 us  [swap_col(): return lax.ppermute(x, 'col', [(0, 1), (1, 0)])]
    pallas_call x2 -> x3, Pallas kernels: 5.14 us -> 6.15 us  [fisher_part(): pl.pallas_call(functools.partial(fisher_kernel, flips), out_shape=jax.Sha...]
    ppermute x5, starting transfers between devices: 1.1 us -> 0.6 us  [swap_col(): return lax.ppermute(x, 'col', [(0, 1), (1, 0)])]
  transfers between devices with their start and end apart: 14 -> 14, of which waited for: 7 -> 5; matrix products, arithmetic and copies ran while one was open for 0% -> 0% of each run, Pallas kernels for 8% -> 14%
where the time goes in v10:
time: 37.4 us; the launch traced here: 37.1 us
  starting transfers between devices  17.5 us (47%)
  Pallas kernels  8.05 us (22%)
  waiting for transfers between devices  7.82 us (21%)
  local copies, waits for them, and re-layouts  2.29 us (6%)
  between operations  1.43 us (4%)
    ppermute x9, starting transfers between devices, swap_row(): return lax.ppermute(x, 'row', [(i, i ^ bits) for i in range(n_row)])  16.9 us
    ppermute x9, waiting for transfers between devices, swap_row(): return lax.ppermute(x, 'row', [(i, i ^ bits) for i in range(n_row)])  7.2 us
    pallas_call x3, Pallas kernels, fisher_part(): pl.pallas_call(functools.partial(fisher_kernel, flips), out_shape=jax.Sha...  6.15 us
    unnamed x6, local copies, waits for them, and re-layouts  2.29 us
  transfers between devices with their start and end apart: 14, of which 5 were waited for; matrix products, arithmetic and copies ran while one was open for 0% of the time, Pallas kernels for 14%

profile of v10, /device:TPU:0, one launch (start us, length us, event | category | flops | bytes accessed | tf_op | source)
XLA Modules:
  0.0 37.1 jit_solution(4861245754977054705)
XLA Ops:
  0.7 1.0 %copy-done = f32[8,11392]{1,0:T(8,128)S(1)} copy-done((f32[8,11392]{1,0:T(8,128)S(1)}, f32[8,11392]{1,0:T(8,128)}, u32[]{:S(2)}) %copy-start) | copy-done | bytes 364568
  1.6 0.2 shard_map.56
  1.9 0.5 %collective-permute-start = (f32[8,8,1280]{2,1,0:T(8,128)S(1)}, f32[8,8,1280]{2,1,0:T(8,128)S(1)}, u32[]{:S(2)}, u32[]{:S(2)}) collective-permute-start(f32[8,8,1280]{2,1,0:T(8,128)S(1)} %get-tuple-element.17), channel_id=1, source_target_pairs={{0,1},{1,0},{2,3},{3,2},{4,5},{5,4},{6,7},{7,6},{8,9},{9,8},{10,11... | collective-permute-start | bytes 983048 | tf_op jit(solution)/shard_map/ppermute | solution.py:229
  3.1 0.6 %collective-permute-done.crossed_ref = f32[8,8,1280]{2,1,0:T(8,128)S(1)} collective-permute-done((f32[8,8,1280]{2,1,0:T(8,128)S(1)}, f32[8,8,1280]{2,1,0:T(8,128)S(1)}, u32[]{:S(2)}, u32[]{:S(2)}) %collective-permute-start) | collective-permute-done | bytes 327712 | tf_op jit(solution)/shard_map/ppermute | solution.py:229
  3.7 3.0 %collective-permute-start.5 = (f32[32,1280]{1,0:T(8,128)S(1)}, f32[32,1280]{1,0:T(8,128)S(1)}, u32[]{:S(2)}, u32[]{:S(2)}) collective-permute-start(f32[32,1280]{1,0:T(8,128)S(1)} %get-tuple-element.23), channel_id=1, source_target_pairs={{0,4},{2,6},{4,0},{6,2},{8,12},{10,14},{12,8},{14,10},{1,5},{3,7},... | collective-permute-start | bytes 491528 | tf_op jit(solution)/shard_map/ppermute | solution.py:226
  6.7 2.6 %collective-permute-start.1 = (f32[16,1280]{1,0:T(8,128)S(1)}, f32[16,1280]{1,0:T(8,128)S(1)}, u32[]{:S(2)}, u32[]{:S(2)}) collective-permute-start(f32[16,1280]{1,0:T(8,128)S(1)} %get-tuple-element.18), channel_id=1, source_target_pairs={{0,8},{2,10},{4,12},{6,14},{8,0},{10,2},{12,4},{14,6},{1,9},{3,11}... | collective-permute-start | bytes 245768 | tf_op jit(solution)/shard_map/ppermute | solution.py:226
  9.3 1.3 %collective-permute-start.2 = (f32[16,1280]{1,0:T(8,128)S(1)}, f32[16,1280]{1,0:T(8,128)S(1)}, u32[]{:S(2)}, u32[]{:S(2)}) collective-permute-start(f32[16,1280]{1,0:T(8,128)S(1)} %get-tuple-element.19), channel_id=1, source_target_pairs={{0,10},{2,8},{4,14},{6,12},{8,2},{10,0},{12,6},{14,4},{1,11},{3,9}... | collective-permute-start | bytes 245768 | tf_op jit(solution)/shard_map/ppermute | solution.py:226
  10.6 2.5 %collective-permute-start.3 = (f32[16,1280]{1,0:T(8,128)S(1)}, f32[16,1280]{1,0:T(8,128)S(1)}, u32[]{:S(2)}, u32[]{:S(2)}) collective-permute-start(f32[16,1280]{1,0:T(8,128)S(1)} %get-tuple-element.20), channel_id=1, source_target_pairs={{0,12},{2,14},{4,8},{6,10},{8,4},{10,6},{12,0},{14,2},{1,13},{3,15... | collective-permute-start | bytes 245768 | tf_op jit(solution)/shard_map/ppermute | solution.py:226
  13.1 1.3 %collective-permute-start.4 = (f32[16,1280]{1,0:T(8,128)S(1)}, f32[16,1280]{1,0:T(8,128)S(1)}, u32[]{:S(2)}, u32[]{:S(2)}) collective-permute-start(f32[16,1280]{1,0:T(8,128)S(1)} %get-tuple-element.21), channel_id=1, source_target_pairs={{0,14},{2,12},{4,10},{6,8},{8,6},{10,4},{12,2},{14,0},{1,15},{3,13... | collective-permute-start | bytes 245768 | tf_op jit(solution)/shard_map/ppermute | solution.py:226
  14.4 1.6 %collective-permute-start.6 = (f32[32,1280]{1,0:T(8,128)S(1)}, f32[32,1280]{1,0:T(8,128)S(1)}, u32[]{:S(2)}, u32[]{:S(2)}) collective-permute-start(f32[32,1280]{1,0:T(8,128)S(1)} %shard_map.58), channel_id=1, source_target_pairs={{0,2},{2,0},{4,6},{6,4},{8,10},{10,8},{12,14},{14,12},{1,3},{3,1},... | collective-permute-start | bytes 491528 | tf_op jit(solution)/shard_map/ppermute | solution.py:226
  16.0 0.7 %copy-done.1 = f32[17]{0:T(128)S(1)} copy-done((f32[17]{0:T(128)S(1)}, f32[17]{0:T(128)}, u32[]{:S(2)}) %copy-start.1) | copy-done | bytes 92
  16.6 0.7 %copy-done.2 = s32[16]{0:T(128)S(1)} copy-done((s32[16]{0:T(128)S(1)}, s32[16]{0:T(128)}, u32[]{:S(2)}) %copy-start.2) | copy-done | bytes 88
  17.3 0.7 %shard_map.55.matrix_ref = f32[96,128]{1,0:T(8,128)S(1)} custom-call(f32[17]{0:T(128)S(1)} %copy-done.1, s32[1]{0:T(128)S(6)} %copy.12.count_ref._, s32[16]{0:T(128)S(1)} %copy-done.2), custom_call_target="tpu_custom_call" | custom-call | flops 10000000000 | bytes 100000000 | tf_op jit(solution)/shard_map/pallas_call | solution.py:232
  18.0 4.9 %collective-permute-done.2.refs_1_ = f32[16,1280]{1,0:T(8,128)S(1)} collective-permute-done((f32[16,1280]{1,0:T(8,128)S(1)}, f32[16,1280]{1,0:T(8,128)S(1)}, u32[]{:S(2)}, u32[]{:S(2)}) %collective-permute-start.2) | collective-permute-done | bytes 81952 | tf_op jit(solution)/shard_map/ppermute | solution.py:226
  23.0 0.3 shard_map.60.refs_0_
  23.4 3.8 %collective-permute-start.11 = (bf16[96,512]{1,0:T(8,128)(2,1)S(1)}, bf16[96,512]{1,0:T(8,128)(2,1)S(1)}, u32[]{:S(2)}, u32[]{:S(2)}) collective-permute-start(bf16[96,512]{1,0:T(8,128)(2,1)S(1)} %shard_map.60.refs_0_), channel_id=1, source_target_pairs={{0,6},{2,4},{4,2},{6,0},{8,14},{10,12},{12,10},{14,8},{1,7},{3,5},... | collective-permute-start | bytes 294920 | tf_op jit(solution)/shard_map/ppermute | solution.py:226
  27.2 0.9 %collective-permute-start.7 = (bf16[96,512]{1,0:T(8,128)(2,1)S(1)}, bf16[96,512]{1,0:T(8,128)(2,1)S(1)}, u32[]{:S(2)}, u32[]{:S(2)}) collective-permute-start(bf16[96,512]{1,0:T(8,128)(2,1)S(1)} %shard_map.60.refs_0_), channel_id=1, source_target_pairs={{0,2},{2,0},{4,6},{6,4},{8,10},{10,8},{12,14},{14,12},{1,3},{3,1},... | collective-permute-start | bytes 294920 | tf_op jit(solution)/shard_map/ppermute | solution.py:226
  28.1 0.5 %shard_map.59.own_ref = bf16[712,96]{1,0:T(8,128)(2,1)S(1)} custom-call(f32[96,128]{1,0:T(8,128)S(1)} %shard_map.55.matrix_ref, f32[16,1280]{1,0:T(8,128)S(1)} %collective-permute-done.1.refs_0_, f32[16,1280]{1,0:T(8,128)S(1)} %collective-permute-done.2.refs_1_, f32[16,1280]{1,0:T(8,128)S(1)} %collective-permute-done.3.refs_2_, ...), custom_call_target="tpu_custom_call" | custom-call | tf_op jit(solution)/shard_map/pallas_call | solution.py:286
  28.6 1.8 %shard_map.61.refs_3_ = bf16[712,4096]{1,0:T(8,128)(2,1)} custom-call(bf16[712,96]{1,0:T(8,128)(2,1)S(1)} %shard_map.59.own_ref, bf16[96,512]{1,0:T(8,128)(2,1)S(1)} %shard_map.60.refs_0_, bf16[96,512]{1,0:T(8,128)(2,1)S(1)} %collective-permute-done.12.refs_1_), custom_call_target="tpu_custom_call" | custom-call | tf_op jit(solution)/shard_map/pallas_call | solution.py:197
  30.4 0.4 %collective-permute-done.11.refs_2_ = bf16[96,512]{1,0:T(8,128)(2,1)S(1)} collective-permute-done((bf16[96,512]{1,0:T(8,128)(2,1)S(1)}, bf16[96,512]{1,0:T(8,128)(2,1)S(1)}, u32[]{:S(2)}, u32[]{:S(2)}) %collective-permute-start.11) | collective-permute-done | bytes 98336 | tf_op jit(solution)/shard_map/ppermute | solution.py:226
  30.9 1.3 %collective-permute-done.9.refs_1_ = bf16[96,512]{1,0:T(8,128)(2,1)S(1)} collective-permute-done((bf16[96,512]{1,0:T(8,128)(2,1)S(1)}, bf16[96,512]{1,0:T(8,128)(2,1)S(1)}, u32[]{:S(2)}, u32[]{:S(2)}) %collective-permute-start.9) | collective-permute-done | bytes 98336 | tf_op jit(solution)/shard_map/ppermute | solution.py:226
  32.1 0.6 %collective-permute-done.7.refs_0_ = bf16[96,512]{1,0:T(8,128)(2,1)S(1)} collective-permute-done((bf16[96,512]{1,0:T(8,128)(2,1)S(1)}, bf16[96,512]{1,0:T(8,128)(2,1)S(1)}, u32[]{:S(2)}, u32[]{:S(2)}) %collective-permute-start.7) | collective-permute-done | bytes 98336 | tf_op jit(solution)/shard_map/ppermute | solution.py:226
  32.7 2.2 %shard_map.62.refs_3_ = bf16[712,4096]{1,0:T(8,128)(2,1)} custom-call(bf16[712,96]{1,0:T(8,128)(2,1)S(1)} %shard_map.59.own_ref, bf16[96,512]{1,0:T(8,128)(2,1)S(1)} %collective-permute-done.7.refs_0_, bf16[96,512]{1,0:T(8,128)(2,1)S(1)} %collective-permute-done.9.refs_1_, ...), custom_call_target="tpu_custom_call", output_to_operand_aliasing={{}: (4, {})} | custom-call | tf_op jit(solution)/shard_map/pallas_call | solution.py:197
  34.9 2.2 %shard_map.63 = bf16[712,4096]{1,0:T(8,128)(2,1)} custom-call(bf16[712,96]{1,0:T(8,128)(2,1)S(1)} %shard_map.59.own_ref, bf16[96,512]{1,0:T(8,128)(2,1)S(1)} %collective-permute-done.8.refs_0_, bf16[96,512]{1,0:T(8,128)(2,1)S(1)} %collective-permute-done.10.refs_1_, ...), custom_call_target="tpu_custom_call", output_to_operand_aliasing={{}: (4, {})} | custom-call | tf_op jit(solution)/shard_map/pallas_call | solution.py:197
  (19 shorter events, 0.2 us)
Async XLA Ops:
  0.7 1.0 %copy-start = (f32[8,11392]{1,0:T(8,128)S(1)}, f32[8,11392]{1,0:T(8,128)}, u32[]{:S(2)}) copy-start(f32[8,11392]{1,0:T(8,128)} %series_ref.1) | copy-start | bytes 1093636
  1.9 1.8 %collective-permute-start = (f32[8,8,1280]{2,1,0:T(8,128)S(1)}, f32[8,8,1280]{2,1,0:T(8,128)S(1)}, u32[]{:S(2)}, u32[]{:S(2)}) collective-permute-start(f32[8,8,1280]{2,1,0:T(8,128)S(1)} %get-tuple-element.17), channel_id=1, source_target_pairs={{0,1},{1,0},{2,3},{3,2},{4,5},{5,4},{6,7},{7,6},{8,9},{9,8},{10,11... | collective-permute-start | bytes 983048 | tf_op jit(solution)/shard_map/ppermute | solution.py:229
  3.7 10.7 %collective-permute-start.5 = (f32[32,1280]{1,0:T(8,128)S(1)}, f32[32,1280]{1,0:T(8,128)S(1)}, u32[]{:S(2)}, u32[]{:S(2)}) collective-permute-start(f32[32,1280]{1,0:T(8,128)S(1)} %get-tuple-element.23), channel_id=1, source_target_pairs={{0,4},{2,6},{4,0},{6,2},{8,12},{10,14},{12,8},{14,10},{1,5},{3,7},... | collective-permute-start | bytes 491528 | tf_op jit(solution)/shard_map/ppermute | solution.py:226
  6.7 11.3 %collective-permute-start.1 = (f32[16,1280]{1,0:T(8,128)S(1)}, f32[16,1280]{1,0:T(8,128)S(1)}, u32[]{:S(2)}, u32[]{:S(2)}) collective-permute-start(f32[16,1280]{1,0:T(8,128)S(1)} %get-tuple-element.18), channel_id=1, source_target_pairs={{0,8},{2,10},{4,12},{6,14},{8,0},{10,2},{12,4},{14,6},{1,9},{3,11}... | collective-permute-start | bytes 245768 | tf_op jit(solution)/shard_map/ppermute | solution.py:226
  9.3 13.6 %collective-permute-start.2 = (f32[16,1280]{1,0:T(8,128)S(1)}, f32[16,1280]{1,0:T(8,128)S(1)}, u32[]{:S(2)}, u32[]{:S(2)}) collective-permute-start(f32[16,1280]{1,0:T(8,128)S(1)} %get-tuple-element.19), channel_id=1, source_target_pairs={{0,10},{2,8},{4,14},{6,12},{8,2},{10,0},{12,6},{14,4},{1,11},{3,9}... | collective-permute-start | bytes 245768 | tf_op jit(solution)/shard_map/ppermute | solution.py:226
  10.6 12.4 %collective-permute-start.3 = (f32[16,1280]{1,0:T(8,128)S(1)}, f32[16,1280]{1,0:T(8,128)S(1)}, u32[]{:S(2)}, u32[]{:S(2)}) collective-permute-start(f32[16,1280]{1,0:T(8,128)S(1)} %get-tuple-element.20), channel_id=1, source_target_pairs={{0,12},{2,14},{4,8},{6,10},{8,4},{10,6},{12,0},{14,2},{1,13},{3,15... | collective-permute-start | bytes 245768 | tf_op jit(solution)/shard_map/ppermute | solution.py:226
  13.1 9.9 %collective-permute-start.4 = (f32[16,1280]{1,0:T(8,128)S(1)}, f32[16,1280]{1,0:T(8,128)S(1)}, u32[]{:S(2)}, u32[]{:S(2)}) collective-permute-start(f32[16,1280]{1,0:T(8,128)S(1)} %get-tuple-element.21), channel_id=1, source_target_pairs={{0,14},{2,12},{4,10},{6,8},{8,6},{10,4},{12,2},{14,0},{1,15},{3,13... | collective-permute-start | bytes 245768 | tf_op jit(solution)/shard_map/ppermute | solution.py:226
  14.4 8.6 %collective-permute-start.6 = (f32[32,1280]{1,0:T(8,128)S(1)}, f32[32,1280]{1,0:T(8,128)S(1)}, u32[]{:S(2)}, u32[]{:S(2)}) collective-permute-start(f32[32,1280]{1,0:T(8,128)S(1)} %shard_map.58), channel_id=1, source_target_pairs={{0,2},{2,0},{4,6},{6,4},{8,10},{10,8},{12,14},{14,12},{1,3},{3,1},... | collective-permute-start | bytes 491528 | tf_op jit(solution)/shard_map/ppermute | solution.py:226
  16.0 0.7 %copy-start.1 = (f32[17]{0:T(128)S(1)}, f32[17]{0:T(128)}, u32[]{:S(2)}) copy-start(f32[17]{0:T(128)} %taps_ref.1) | copy-start | bytes 208
  16.6 0.7 %copy-start.2 = (s32[16]{0:T(128)S(1)}, s32[16]{0:T(128)}, u32[]{:S(2)}) copy-start(s32[16]{0:T(128)} %kept_ref.1) | copy-start | bytes 196
  23.3 5.3 %collective-permute-start.12 = (bf16[96,512]{1,0:T(8,128)(2,1)S(1)}, bf16[96,512]{1,0:T(8,128)(2,1)S(1)}, u32[]{:S(2)}, u32[]{:S(2)}) collective-permute-start(bf16[96,512]{1,0:T(8,128)(2,1)S(1)} %shard_map.60.refs_0_), channel_id=1, source_target_pairs={{0,1},{1,0},{2,3},{3,2},{4,5},{5,4},{6,7},{7,6},{8,9},{9,8},{10,11... | collective-permute-start | bytes 294920 | tf_op jit(solution)/shard_map/ppermute | solution.py:229
  23.4 7.5 %collective-permute-start.11 = (bf16[96,512]{1,0:T(8,128)(2,1)S(1)}, bf16[96,512]{1,0:T(8,128)(2,1)S(1)}, u32[]{:S(2)}, u32[]{:S(2)}) collective-permute-start(bf16[96,512]{1,0:T(8,128)(2,1)S(1)} %shard_map.60.refs_0_), channel_id=1, source_target_pairs={{0,6},{2,4},{4,2},{6,0},{8,14},{10,12},{12,10},{14,8},{1,7},{3,5},... | collective-permute-start | bytes 294920 | tf_op jit(solution)/shard_map/ppermute | solution.py:226
  27.2 4.9 %collective-permute-start.9 = (bf16[96,512]{1,0:T(8,128)(2,1)S(1)}, bf16[96,512]{1,0:T(8,128)(2,1)S(1)}, u32[]{:S(2)}, u32[]{:S(2)}) collective-permute-start(bf16[96,512]{1,0:T(8,128)(2,1)S(1)} %shard_map.60.refs_0_), channel_id=1, source_target_pairs={{0,4},{2,6},{4,0},{6,2},{8,12},{10,14},{12,8},{14,10},{1,5},{3,7},... | collective-permute-start | bytes 294920 | tf_op jit(solution)/shard_map/ppermute | solution.py:226
  27.2 5.5 %collective-permute-start.7 = (bf16[96,512]{1,0:T(8,128)(2,1)S(1)}, bf16[96,512]{1,0:T(8,128)(2,1)S(1)}, u32[]{:S(2)}, u32[]{:S(2)}) collective-permute-start(bf16[96,512]{1,0:T(8,128)(2,1)S(1)} %shard_map.60.refs_0_), channel_id=1, source_target_pairs={{0,2},{2,0},{4,6},{6,4},{8,10},{10,8},{12,14},{14,12},{1,3},{3,1},... | collective-permute-start | bytes 294920 | tf_op jit(solution)/shard_map/ppermute | solution.py:226
  30.9 4.0 %collective-permute-start.13 = (bf16[96,512]{1,0:T(8,128)(2,1)S(1)}, bf16[96,512]{1,0:T(8,128)(2,1)S(1)}, u32[]{:S(2)}, u32[]{:S(2)}) collective-permute-start(bf16[96,512]{1,0:T(8,128)(2,1)S(1)} %collective-permute-done.11.refs_2_), channel_id=1, source_target_pairs={{0,1},{1,0},{2,3},{3,2},{4,5},{5,4},{6,7},{7,6},{8,9},{9,8},{10,11... | collective-permute-start | bytes 294920 | tf_op jit(solution)/shard_map/ppermute | solution.py:229
  32.1 2.8 %collective-permute-start.10 = (bf16[96,512]{1,0:T(8,128)(2,1)S(1)}, bf16[96,512]{1,0:T(8,128)(2,1)S(1)}, u32[]{:S(2)}, u32[]{:S(2)}) collective-permute-start(bf16[96,512]{1,0:T(8,128)(2,1)S(1)} %collective-permute-done.9.refs_1_), channel_id=1, source_target_pairs={{0,1},{1,0},{2,3},{3,2},{4,5},{5,4},{6,7},{7,6},{8,9},{9,8},{10,11... | collective-permute-start | bytes 294920 | tf_op jit(solution)/shard_map/ppermute | solution.py:229
  32.7 2.2 %collective-permute-start.8 = (bf16[96,512]{1,0:T(8,128)(2,1)S(1)}, bf16[96,512]{1,0:T(8,128)(2,1)S(1)}, u32[]{:S(2)}, u32[]{:S(2)}) collective-permute-start(bf16[96,512]{1,0:T(8,128)(2,1)S(1)} %collective-permute-done.7.refs_0_), channel_id=1, source_target_pairs={{0,1},{1,0},{2,3},{3,2},{4,5},{5,4},{6,7},{7,6},{8,9},{9,8},{10,11... | collective-permute-start | bytes 294920 | tf_op jit(solution)/shard_map/ppermute | solution.py:229

commit v11 on v10

--- a/solution.py
+++ b/solution.py
@@ -180,6 +180,13 @@
         copies.append(copy)
     for copy in copies:
         copy.wait()
+
+
+def first_kernel(end, flips, count, matrix_ref, *refs):
+    raw_refs, pieces = refs[:count], refs[count : count + len(flips)]
+    out_ref, own_ref, made_ref, sems = refs[count + len(flips) :]
+    scale_own_kernel(end, matrix_ref, *raw_refs, own_ref)
+    fisher_kernel(flips, own_ref, *pieces, out_ref, made_ref, sems)
 
 
 def fisher_part(own_rows, pieces, out):
@@ -283,18 +290,23 @@
         out_specs=vmem,
         compiler_params=params,
     )(matrix, *raws)
-    own_rows = pl.pallas_call(
-        functools.partial(scale_own_kernel, own_pad),
-        out_shape=jax.ShapeDtypeStruct((own, kept), jnp.bfloat16),
-        in_specs=[vmem] * (1 + len(raws)),
-        out_specs=vmem,
-        compiler_params=params,
-    )(matrix, *raws)
-
     across = swap_row(block, 3)
     near = swap_row(block, 2)
     side = swap_row(block, 1)
-    out = fisher_part(own_rows, [(0, block), (4, swap_col(block))], None)
+    out, own_rows = pl.pallas_call(
+        functools.partial(first_kernel, own_pad, (0, 4), len(raws)),
+        out_shape=(
+            jax.ShapeDtypeStruct((own, B), jnp.bfloat16),
+            jax.ShapeDtypeStruct((own, kept), jnp.bfloat16),
+        ),
+        in_specs=[vmem] * (3 + len(raws)),
+        out_specs=(pl.BlockSpec(memory_space=pltpu.HBM), vmem),
+        scratch_shapes=[
+            pltpu.VMEM((own, 2 * share), jnp.bfloat16),
+            pltpu.SemaphoreType.DMA((2,)),
+        ],
+        compiler_params=pltpu.CompilerParams(vmem_limit_bytes=48 << 20),
+    )(matrix, *raws, block, swap_col(block))
     across, out = lax.optimization_barrier((across, out))
     out = fisher_part(own_rows, [(1, side), (2, near), (3, across)], out)
     late = [(5, swap_col(side)), (6, swap_col(near)), (7, swap_col(across))]

time: 37.4 us -> 37.4 us (level)
    pallas_call x3 -> x2, Pallas kernels: 6.15 us -> 4.36 us  [fisher_part(): pl.pallas_call(functools.partial(fisher_kernel, flips), out_shape=jax.Sha...]
    pallas_call x1, Pallas kernels: 0.53 us -> 2.28 us  [body(): pl.pallas_call(functools.partial(first_kernel, own_pad, (0, 4), len(raws)...]
where the time goes in v11:
time: 37.4 us; the launch traced here: 37.1 us
  starting transfers between devices  17.5 us (47%)
  Pallas kernels  8 us (21%)
  waiting for transfers between devices  7.87 us (21%)
  local copies, waits for them, and re-layouts  2.29 us (6%)
  between operations  1.42 us (4%)
    ppermute x9, starting transfers between devices, swap_row(): return lax.ppermute(x, 'row', [(i, i ^ bits) for i in range(n_row)])  16.9 us
    ppermute x9, waiting for transfers between devices, swap_row(): return lax.ppermute(x, 'row', [(i, i ^ bits) for i in range(n_row)])  7.25 us
    pallas_call x2, Pallas kernels, fisher_part(): pl.pallas_call(functools.partial(fisher_kernel, flips), out_shape=jax.Sha...  4.36 us
    unnamed x6, local copies, waits for them, and re-layouts  2.29 us
    pallas_call x1, Pallas kernels, body(): pl.pallas_call(functools.partial(first_kernel, own_pad, (0, 4), len(raws)...  2.28 us
  transfers between devices with their start and end apart: 14, of which 5 were waited for; matrix products, arithmetic and copies ran while one was open for 0% of the time, Pallas kernels for 14%

profile of v11, /device:TPU:0, one launch (start us, length us, event | category | flops | bytes accessed | tf_op | source)
XLA Modules:
  0.0 37.1 jit_solution(6186178002656710839)
XLA Ops:
  0.7 1.0 %copy-done = f32[8,11392]{1,0:T(8,128)S(1)} copy-done((f32[8,11392]{1,0:T(8,128)S(1)}, f32[8,11392]{1,0:T(8,128)}, u32[]{:S(2)}) %copy-start) | copy-done | bytes 364568
  1.6 0.2 shard_map.56
  1.9 0.5 %collective-permute-start = (f32[8,8,1280]{2,1,0:T(8,128)S(1)}, f32[8,8,1280]{2,1,0:T(8,128)S(1)}, u32[]{:S(2)}, u32[]{:S(2)}) collective-permute-start(f32[8,8,1280]{2,1,0:T(8,128)S(1)} %get-tuple-element.19), channel_id=1, source_target_pairs={{0,1},{1,0},{2,3},{3,2},{4,5},{5,4},{6,7},{7,6},{8,9},{9,8},{10,11... | collective-permute-start | bytes 983048 | tf_op jit(solution)/shard_map/ppermute | solution.py:236
  3.1 0.6 %collective-permute-done.crossed_ref = f32[8,8,1280]{2,1,0:T(8,128)S(1)} collective-permute-done((f32[8,8,1280]{2,1,0:T(8,128)S(1)}, f32[8,8,1280]{2,1,0:T(8,128)S(1)}, u32[]{:S(2)}, u32[]{:S(2)}) %collective-permute-start) | collective-permute-done | bytes 327712 | tf_op jit(solution)/shard_map/ppermute | solution.py:236
  3.7 3.0 %collective-permute-start.5 = (f32[32,1280]{1,0:T(8,128)S(1)}, f32[32,1280]{1,0:T(8,128)S(1)}, u32[]{:S(2)}, u32[]{:S(2)}) collective-permute-start(f32[32,1280]{1,0:T(8,128)S(1)} %get-tuple-element.25), channel_id=1, source_target_pairs={{0,4},{2,6},{4,0},{6,2},{8,12},{10,14},{12,8},{14,10},{1,5},{3,7},... | collective-permute-start | bytes 491528 | tf_op jit(solution)/shard_map/ppermute | solution.py:233
  6.7 2.6 %collective-permute-start.1 = (f32[16,1280]{1,0:T(8,128)S(1)}, f32[16,1280]{1,0:T(8,128)S(1)}, u32[]{:S(2)}, u32[]{:S(2)}) collective-permute-start(f32[16,1280]{1,0:T(8,128)S(1)} %get-tuple-element.20), channel_id=1, source_target_pairs={{0,8},{2,10},{4,12},{6,14},{8,0},{10,2},{12,4},{14,6},{1,9},{3,11}... | collective-permute-start | bytes 245768 | tf_op jit(solution)/shard_map/ppermute | solution.py:233
  9.3 1.3 %collective-permute-start.2 = (f32[16,1280]{1,0:T(8,128)S(1)}, f32[16,1280]{1,0:T(8,128)S(1)}, u32[]{:S(2)}, u32[]{:S(2)}) collective-permute-start(f32[16,1280]{1,0:T(8,128)S(1)} %get-tuple-element.21), channel_id=1, source_target_pairs={{0,10},{2,8},{4,14},{6,12},{8,2},{10,0},{12,6},{14,4},{1,11},{3,9}... | collective-permute-start | bytes 245768 | tf_op jit(solution)/shard_map/ppermute | solution.py:233
  10.6 2.5 %collective-permute-start.3 = (f32[16,1280]{1,0:T(8,128)S(1)}, f32[16,1280]{1,0:T(8,128)S(1)}, u32[]{:S(2)}, u32[]{:S(2)}) collective-permute-start(f32[16,1280]{1,0:T(8,128)S(1)} %get-tuple-element.22), channel_id=1, source_target_pairs={{0,12},{2,14},{4,8},{6,10},{8,4},{10,6},{12,0},{14,2},{1,13},{3,15... | collective-permute-start | bytes 245768 | tf_op jit(solution)/shard_map/ppermute | solution.py:233
  13.1 1.3 %collective-permute-start.4 = (f32[16,1280]{1,0:T(8,128)S(1)}, f32[16,1280]{1,0:T(8,128)S(1)}, u32[]{:S(2)}, u32[]{:S(2)}) collective-permute-start(f32[16,1280]{1,0:T(8,128)S(1)} %get-tuple-element.23), channel_id=1, source_target_pairs={{0,14},{2,12},{4,10},{6,8},{8,6},{10,4},{12,2},{14,0},{1,15},{3,13... | collective-permute-start | bytes 245768 | tf_op jit(solution)/shard_map/ppermute | solution.py:233
  14.4 1.6 %collective-permute-start.6 = (f32[32,1280]{1,0:T(8,128)S(1)}, f32[32,1280]{1,0:T(8,128)S(1)}, u32[]{:S(2)}, u32[]{:S(2)}) collective-permute-start(f32[32,1280]{1,0:T(8,128)S(1)} %shard_map.58), channel_id=1, source_target_pairs={{0,2},{2,0},{4,6},{6,4},{8,10},{10,8},{12,14},{14,12},{1,3},{3,1},... | collective-permute-start | bytes 491528 | tf_op jit(solution)/shard_map/ppermute | solution.py:233
  16.0 0.7 %copy-done.1 = f32[17]{0:T(128)S(1)} copy-done((f32[17]{0:T(128)S(1)}, f32[17]{0:T(128)}, u32[]{:S(2)}) %copy-start.1) | copy-done | bytes 92
  16.6 0.7 %copy-done.2 = s32[16]{0:T(128)S(1)} copy-done((s32[16]{0:T(128)S(1)}, s32[16]{0:T(128)}, u32[]{:S(2)}) %copy-start.2) | copy-done | bytes 88
  17.3 0.7 %shard_map.55.matrix_ref = f32[96,128]{1,0:T(8,128)S(1)} custom-call(f32[17]{0:T(128)S(1)} %copy-done.1, s32[1]{0:T(128)S(6)} %copy.12.count_ref._, s32[16]{0:T(128)S(1)} %copy-done.2), custom_call_target="tpu_custom_call" | custom-call | flops 10000000000 | bytes 100000000 | tf_op jit(solution)/shard_map/pallas_call | solution.py:239
  18.0 4.9 %collective-permute-done.2.refs_1_ = f32[16,1280]{1,0:T(8,128)S(1)} collective-permute-done((f32[16,1280]{1,0:T(8,128)S(1)}, f32[16,1280]{1,0:T(8,128)S(1)}, u32[]{:S(2)}, u32[]{:S(2)}) %collective-permute-start.2) | collective-permute-done | bytes 81952 | tf_op jit(solution)/shard_map/ppermute | solution.py:233
  23.0 0.3 shard_map.59.refs_7_
  23.3 0.1 collective-permute-start.7
  23.4 3.8 %collective-permute-start.12 = (bf16[96,512]{1,0:T(8,128)(2,1)S(1)}, bf16[96,512]{1,0:T(8,128)(2,1)S(1)}, u32[]{:S(2)}, u32[]{:S(2)}) collective-permute-start(bf16[96,512]{1,0:T(8,128)(2,1)S(1)} %shard_map.59.refs_7_), channel_id=1, source_target_pairs={{0,6},{2,4},{4,2},{6,0},{8,14},{10,12},{12,10},{14,8},{1,7},{3,5},... | collective-permute-start | bytes 294920 | tf_op jit(solution)/shard_map/ppermute | solution.py:233
  27.2 0.9 %collective-permute-start.8 = (bf16[96,512]{1,0:T(8,128)(2,1)S(1)}, bf16[96,512]{1,0:T(8,128)(2,1)S(1)}, u32[]{:S(2)}, u32[]{:S(2)}) collective-permute-start(bf16[96,512]{1,0:T(8,128)(2,1)S(1)} %shard_map.59.refs_7_), channel_id=1, source_target_pairs={{0,2},{2,0},{4,6},{6,4},{8,10},{10,8},{12,14},{14,12},{1,3},{3,1},... | collective-permute-start | bytes 294920 | tf_op jit(solution)/shard_map/ppermute | solution.py:233
  28.1 2.3 %shard_map.60 = (bf16[712,4096]{1,0:T(8,128)(2,1)}, bf16[712,96]{1,0:T(8,128)(2,1)S(1)}) custom-call(f32[96,128]{1,0:T(8,128)S(1)} %shard_map.55.matrix_ref, f32[16,1280]{1,0:T(8,128)S(1)} %collective-permute-done.1.refs_0_, f32[16,1280]{1,0:T(8,128)S(1)} %collective-permute-done.2.refs_1_, f32[16,1280]{1,0:T(8,128)S(1)} %collective-permute-done.3.refs_2_, ...), custom_call_target="tpu_custom_call" | custom-call | tf_op jit(solution)/shard_map/pallas_call | solution.py:296
  30.4 0.5 %collective-permute-done.12.refs_2_ = bf16[96,512]{1,0:T(8,128)(2,1)S(1)} collective-permute-done((bf16[96,512]{1,0:T(8,128)(2,1)S(1)}, bf16[96,512]{1,0:T(8,128)(2,1)S(1)}, u32[]{:S(2)}, u32[]{:S(2)}) %collective-permute-start.12) | collective-permute-done | bytes 98336 | tf_op jit(solution)/shard_map/ppermute | solution.py:233
  30.9 1.3 %collective-permute-done.10.refs_1_ = bf16[96,512]{1,0:T(8,128)(2,1)S(1)} collective-permute-done((bf16[96,512]{1,0:T(8,128)(2,1)S(1)}, bf16[96,512]{1,0:T(8,128)(2,1)S(1)}, u32[]{:S(2)}, u32[]{:S(2)}) %collective-permute-start.10) | collective-permute-done | bytes 98336 | tf_op jit(solution)/shard_map/ppermute | solution.py:233
  32.1 0.6 %collective-permute-done.8.refs_0_ = bf16[96,512]{1,0:T(8,128)(2,1)S(1)} collective-permute-done((bf16[96,512]{1,0:T(8,128)(2,1)S(1)}, bf16[96,512]{1,0:T(8,128)(2,1)S(1)}, u32[]{:S(2)}, u32[]{:S(2)}) %collective-permute-start.8) | collective-permute-done | bytes 98336 | tf_op jit(solution)/shard_map/ppermute | solution.py:233
  32.7 2.2 %shard_map.61.refs_3_ = bf16[712,4096]{1,0:T(8,128)(2,1)} custom-call(bf16[712,96]{1,0:T(8,128)(2,1)S(1)} %get-tuple-element.27.own_ref, bf16[96,512]{1,0:T(8,128)(2,1)S(1)} %collective-permute-done.8.refs_0_, bf16[96,512]{1,0:T(8,128)(2,1)S(1)} %collective-permute-done.10.refs_1_, ...), custom_call_target="tpu_custom_call", output_to_operand_aliasing={{}: (4, {})} | custom-call | tf_op jit(solution)/shard_map/pallas_call | solution.py:204
  34.9 2.2 %shard_map.62 = bf16[712,4096]{1,0:T(8,128)(2,1)} custom-call(bf16[712,96]{1,0:T(8,128)(2,1)S(1)} %get-tuple-element.27.own_ref, bf16[96,512]{1,0:T(8,128)(2,1)S(1)} %collective-permute-done.9.refs_0_, bf16[96,512]{1,0:T(8,128)(2,1)S(1)} %collective-permute-done.11.refs_1_, ...), custom_call_target="tpu_custom_call", output_to_operand_aliasing={{}: (4, {})} | custom-call | tf_op jit(solution)/shard_map/pallas_call | solution.py:204
  (18 shorter events, 0.1 us)
Async XLA Ops:
  0.7 1.0 %copy-start = (f32[8,11392]{1,0:T(8,128)S(1)}, f32[8,11392]{1,0:T(8,128)}, u32[]{:S(2)}) copy-start(f32[8,11392]{1,0:T(8,128)} %series_ref.1) | copy-start | bytes 1093636
  1.9 1.8 %collective-permute-start = (f32[8,8,1280]{2,1,0:T(8,128)S(1)}, f32[8,8,1280]{2,1,0:T(8,128)S(1)}, u32[]{:S(2)}, u32[]{:S(2)}) collective-permute-start(f32[8,8,1280]{2,1,0:T(8,128)S(1)} %get-tuple-element.19), channel_id=1, source_target_pairs={{0,1},{1,0},{2,3},{3,2},{4,5},{5,4},{6,7},{7,6},{8,9},{9,8},{10,11... | collective-permute-start | bytes 983048 | tf_op jit(solution)/shard_map/ppermute | solution.py:236
  3.7 10.7 %collective-permute-start.5 = (f32[32,1280]{1,0:T(8,128)S(1)}, f32[32,1280]{1,0:T(8,128)S(1)}, u32[]{:S(2)}, u32[]{:S(2)}) collective-permute-start(f32[32,1280]{1,0:T(8,128)S(1)} %get-tuple-element.25), channel_id=1, source_target_pairs={{0,4},{2,6},{4,0},{6,2},{8,12},{10,14},{12,8},{14,10},{1,5},{3,7},... | collective-permute-start | bytes 491528 | tf_op jit(solution)/shard_map/ppermute | solution.py:233
  6.7 11.3 %collective-permute-start.1 = (f32[16,1280]{1,0:T(8,128)S(1)}, f32[16,1280]{1,0:T(8,128)S(1)}, u32[]{:S(2)}, u32[]{:S(2)}) collective-permute-start(f32[16,1280]{1,0:T(8,128)S(1)} %get-tuple-element.20), channel_id=1, source_target_pairs={{0,8},{2,10},{4,12},{6,14},{8,0},{10,2},{12,4},{14,6},{1,9},{3,11}... | collective-permute-start | bytes 245768 | tf_op jit(solution)/shard_map/ppermute | solution.py:233
  9.3 13.6 %collective-permute-start.2 = (f32[16,1280]{1,0:T(8,128)S(1)}, f32[16,1280]{1,0:T(8,128)S(1)}, u32[]{:S(2)}, u32[]{:S(2)}) collective-permute-start(f32[16,1280]{1,0:T(8,128)S(1)} %get-tuple-element.21), channel_id=1, source_target_pairs={{0,10},{2,8},{4,14},{6,12},{8,2},{10,0},{12,6},{14,4},{1,11},{3,9}... | collective-permute-start | bytes 245768 | tf_op jit(solution)/shard_map/ppermute | solution.py:233
  10.6 12.4 %collective-permute-start.3 = (f32[16,1280]{1,0:T(8,128)S(1)}, f32[16,1280]{1,0:T(8,128)S(1)}, u32[]{:S(2)}, u32[]{:S(2)}) collective-permute-start(f32[16,1280]{1,0:T(8,128)S(1)} %get-tuple-element.22), channel_id=1, source_target_pairs={{0,12},{2,14},{4,8},{6,10},{8,4},{10,6},{12,0},{14,2},{1,13},{3,15... | collective-permute-start | bytes 245768 | tf_op jit(solution)/shard_map/ppermute | solution.py:233
  13.1 9.9 %collective-permute-start.4 = (f32[16,1280]{1,0:T(8,128)S(1)}, f32[16,1280]{1,0:T(8,128)S(1)}, u32[]{:S(2)}, u32[]{:S(2)}) collective-permute-start(f32[16,1280]{1,0:T(8,128)S(1)} %get-tuple-element.23), channel_id=1, source_target_pairs={{0,14},{2,12},{4,10},{6,8},{8,6},{10,4},{12,2},{14,0},{1,15},{3,13... | collective-permute-start | bytes 245768 | tf_op jit(solution)/shard_map/ppermute | solution.py:233
  14.4 8.6 %collective-permute-start.6 = (f32[32,1280]{1,0:T(8,128)S(1)}, f32[32,1280]{1,0:T(8,128)S(1)}, u32[]{:S(2)}, u32[]{:S(2)}) collective-permute-start(f32[32,1280]{1,0:T(8,128)S(1)} %shard_map.58), channel_id=1, source_target_pairs={{0,2},{2,0},{4,6},{6,4},{8,10},{10,8},{12,14},{14,12},{1,3},{3,1},... | collective-permute-start | bytes 491528 | tf_op jit(solution)/shard_map/ppermute | solution.py:233
  16.0 0.7 %copy-start.1 = (f32[17]{0:T(128)S(1)}, f32[17]{0:T(128)}, u32[]{:S(2)}) copy-start(f32[17]{0:T(128)} %taps_ref.1) | copy-start | bytes 208
  16.6 0.7 %copy-start.2 = (s32[16]{0:T(128)S(1)}, s32[16]{0:T(128)}, u32[]{:S(2)}) copy-start(s32[16]{0:T(128)} %kept_ref.1) | copy-start | bytes 196
  23.3 4.8 %collective-permute-start.7 = (bf16[96,512]{1,0:T(8,128)(2,1)S(1)}, bf16[96,512]{1,0:T(8,128)(2,1)S(1)}, u32[]{:S(2)}, u32[]{:S(2)}) collective-permute-start(bf16[96,512]{1,0:T(8,128)(2,1)S(1)} %shard_map.59.refs_7_), channel_id=1, source_target_pairs={{0,1},{1,0},{2,3},{3,2},{4,5},{5,4},{6,7},{7,6},{8,9},{9,8},{10,11... | collective-permute-start | bytes 294920 | tf_op jit(solution)/shard_map/ppermute | solution.py:236
  23.4 7.5 %collective-permute-start.12 = (bf16[96,512]{1,0:T(8,128)(2,1)S(1)}, bf16[96,512]{1,0:T(8,128)(2,1)S(1)}, u32[]{:S(2)}, u32[]{:S(2)}) collective-permute-start(bf16[96,512]{1,0:T(8,128)(2,1)S(1)} %shard_map.59.refs_7_), channel_id=1, source_target_pairs={{0,6},{2,4},{4,2},{6,0},{8,14},{10,12},{12,10},{14,8},{1,7},{3,5},... | collective-permute-start | bytes 294920 | tf_op jit(solution)/shard_map/ppermute | solution.py:233
  27.2 4.9 %collective-permute-start.10 = (bf16[96,512]{1,0:T(8,128)(2,1)S(1)}, bf16[96,512]{1,0:T(8,128)(2,1)S(1)}, u32[]{:S(2)}, u32[]{:S(2)}) collective-permute-start(bf16[96,512]{1,0:T(8,128)(2,1)S(1)} %shard_map.59.refs_7_), channel_id=1, source_target_pairs={{0,4},{2,6},{4,0},{6,2},{8,12},{10,14},{12,8},{14,10},{1,5},{3,7},... | collective-permute-start | bytes 294920 | tf_op jit(solution)/shard_map/ppermute | solution.py:233
  27.2 5.5 %collective-permute-start.8 = (bf16[96,512]{1,0:T(8,128)(2,1)S(1)}, bf16[96,512]{1,0:T(8,128)(2,1)S(1)}, u32[]{:S(2)}, u32[]{:S(2)}) collective-permute-start(bf16[96,512]{1,0:T(8,128)(2,1)S(1)} %shard_map.59.refs_7_), channel_id=1, source_target_pairs={{0,2},{2,0},{4,6},{6,4},{8,10},{10,8},{12,14},{14,12},{1,3},{3,1},... | collective-permute-start | bytes 294920 | tf_op jit(solution)/shard_map/ppermute | solution.py:233
  30.9 4.0 %collective-permute-start.13 = (bf16[96,512]{1,0:T(8,128)(2,1)S(1)}, bf16[96,512]{1,0:T(8,128)(2,1)S(1)}, u32[]{:S(2)}, u32[]{:S(2)}) collective-permute-start(bf16[96,512]{1,0:T(8,128)(2,1)S(1)} %collective-permute-done.12.refs_2_), channel_id=1, source_target_pairs={{0,1},{1,0},{2,3},{3,2},{4,5},{5,4},{6,7},{7,6},{8,9},{9,8},{10,11... | collective-permute-start | bytes 294920 | tf_op jit(solution)/shard_map/ppermute | solution.py:236
  32.1 2.8 %collective-permute-start.11 = (bf16[96,512]{1,0:T(8,128)(2,1)S(1)}, bf16[96,512]{1,0:T(8,128)(2,1)S(1)}, u32[]{:S(2)}, u32[]{:S(2)}) collective-permute-start(bf16[96,512]{1,0:T(8,128)(2,1)S(1)} %collective-permute-done.10.refs_1_), channel_id=1, source_target_pairs={{0,1},{1,0},{2,3},{3,2},{4,5},{5,4},{6,7},{7,6},{8,9},{9,8},{10,11... | collective-permute-start | bytes 294920 | tf_op jit(solution)/shard_map/ppermute | solution.py:236
  32.7 2.2 %collective-permute-start.9 = (bf16[96,512]{1,0:T(8,128)(2,1)S(1)}, bf16[96,512]{1,0:T(8,128)(2,1)S(1)}, u32[]{:S(2)}, u32[]{:S(2)}) collective-permute-start(bf16[96,512]{1,0:T(8,128)(2,1)S(1)} %collective-permute-done.8.refs_0_), channel_id=1, source_target_pairs={{0,1},{1,0},{2,3},{3,2},{4,5},{5,4},{6,7},{7,6},{8,9},{9,8},{10,11... | collective-permute-start | bytes 294920 | tf_op jit(solution)/shard_map/ppermute | solution.py:236

commit v12 on v11

--- a/solution.py
+++ b/solution.py
@@ -170,14 +170,14 @@
             c = jnp.clip(correlation, -CLIP_LIMIT, CLIP_LIMIT)
             z_value = HALF_LN2 * (jnp.log2(1.0 + c) - jnp.log2(1.0 - c))
             made_ref[:, at * share + low : at * share + low + half] = z_value.astype(jnp.bfloat16)
-        where = pl.multiple_of((place ^ flip) * share, share)
-        copy = pltpu.make_async_copy(
-            made_ref.at[:, at * share : (at + 1) * share],
-            out_ref.at[:, pl.ds(where, share)],
-            sems.at[at],
-        )
-        copy.start()
-        copies.append(copy)
+            where = pl.multiple_of((place ^ flip) * share + low, half)
+            copy = pltpu.make_async_copy(
+                made_ref.at[:, at * share + low : at * share + low + half],
+                out_ref.at[:, pl.ds(where, half)],
+                sems.at[len(copies)],
+            )
+            copy.start()
+            copies.append(copy)
     for copy in copies:
         copy.wait()
 
@@ -208,7 +208,7 @@
         out_specs=pl.BlockSpec(memory_space=pltpu.HBM),
         scratch_shapes=[
             pltpu.VMEM((own, len(arrays) * arrays[0].shape[1]), jnp.bfloat16),
-            pltpu.SemaphoreType.DMA((len(arrays),)),
+            pltpu.SemaphoreType.DMA((2 * len(arrays),)),
         ],
         input_output_aliases=aliases,
         compiler_params=pltpu.CompilerParams(vmem_limit_bytes=48 << 20),
@@ -303,7 +303,7 @@
         out_specs=(pl.BlockSpec(memory_space=pltpu.HBM), vmem),
         scratch_shapes=[
             pltpu.VMEM((own, 2 * share), jnp.bfloat16),
-            pltpu.SemaphoreType.DMA((2,)),
+            pltpu.SemaphoreType.DMA((4,)),
         ],
         compiler_params=pltpu.CompilerParams(vmem_limit_bytes=48 << 20),
     )(matrix, *raws, block, swap_col(block))

time: 37.4 us -> 37.6 us (level)
  no operation moved by 1% of the time
where the time goes in v12:
time: 37.6 us; the launch traced here: 37.3 us
  starting transfers between devices  17.5 us (47%)
  Pallas kernels  8.21 us (22%)
  waiting for transfers between devices  7.87 us (21%)
  local copies, waits for them, and re-layouts  2.29 us (6%)
  between operations  1.42 us (4%)
    ppermute x9, starting transfers between devices, swap_row(): return lax.ppermute(x, 'row', [(i, i ^ bits) for i in range(n_row)])  16.9 us
    ppermute x9, waiting for transfers between devices, swap_row(): return lax.ppermute(x, 'row', [(i, i ^ bits) for i in range(n_row)])  7.26 us
    pallas_call x2, Pallas kernels, fisher_part(): pl.pallas_call(functools.partial(fisher_kernel, flips), out_shape=jax.Sha...  4.56 us
    unnamed x6, local copies, waits for them, and re-layouts  2.29 us
    pallas_call x1, Pallas kernels, body(): pl.pallas_call(functools.partial(first_kernel, own_pad, (0, 4), len(raws)...  2.27 us
  transfers between devices with their start and end apart: 14, of which 5 were waited for; matrix products, arithmetic and copies ran while one was open for 0% of the time, Pallas kernels for 14%

profile of v12, /device:TPU:0, one launch (start us, length us, event | category | flops | bytes accessed | tf_op | source)
XLA Modules:
  0.0 37.3 jit_solution(16863002471900554042)
XLA Ops:
  0.7 1.0 %copy-done = f32[8,11392]{1,0:T(8,128)S(1)} copy-done((f32[8,11392]{1,0:T(8,128)S(1)}, f32[8,11392]{1,0:T(8,128)}, u32[]{:S(2)}) %copy-start) | copy-done | bytes 364568
  1.6 0.2 shard_map.56
  1.9 0.5 %collective-permute-start = (f32[8,8,1280]{2,1,0:T(8,128)S(1)}, f32[8,8,1280]{2,1,0:T(8,128)S(1)}, u32[]{:S(2)}, u32[]{:S(2)}) collective-permute-start(f32[8,8,1280]{2,1,0:T(8,128)S(1)} %get-tuple-element.19), channel_id=1, source_target_pairs={{0,1},{1,0},{2,3},{3,2},{4,5},{5,4},{6,7},{7,6},{8,9},{9,8},{10,11... | collective-permute-start | bytes 983048 | tf_op jit(solution)/shard_map/ppermute | solution.py:236
  3.1 0.6 %collective-permute-done.crossed_ref = f32[8,8,1280]{2,1,0:T(8,128)S(1)} collective-permute-done((f32[8,8,1280]{2,1,0:T(8,128)S(1)}, f32[8,8,1280]{2,1,0:T(8,128)S(1)}, u32[]{:S(2)}, u32[]{:S(2)}) %collective-permute-start) | collective-permute-done | bytes 327712 | tf_op jit(solution)/shard_map/ppermute | solution.py:236
  3.7 3.0 %collective-permute-start.5 = (f32[32,1280]{1,0:T(8,128)S(1)}, f32[32,1280]{1,0:T(8,128)S(1)}, u32[]{:S(2)}, u32[]{:S(2)}) collective-permute-start(f32[32,1280]{1,0:T(8,128)S(1)} %get-tuple-element.25), channel_id=1, source_target_pairs={{0,4},{2,6},{4,0},{6,2},{8,12},{10,14},{12,8},{14,10},{1,5},{3,7},... | collective-permute-start | bytes 491528 | tf_op jit(solution)/shard_map/ppermute | solution.py:233
  6.7 2.6 %collective-permute-start.1 = (f32[16,1280]{1,0:T(8,128)S(1)}, f32[16,1280]{1,0:T(8,128)S(1)}, u32[]{:S(2)}, u32[]{:S(2)}) collective-permute-start(f32[16,1280]{1,0:T(8,128)S(1)} %get-tuple-element.20), channel_id=1, source_target_pairs={{0,8},{2,10},{4,12},{6,14},{8,0},{10,2},{12,4},{14,6},{1,9},{3,11}... | collective-permute-start | bytes 245768 | tf_op jit(solution)/shard_map/ppermute | solution.py:233
  9.3 1.3 %collective-permute-start.2 = (f32[16,1280]{1,0:T(8,128)S(1)}, f32[16,1280]{1,0:T(8,128)S(1)}, u32[]{:S(2)}, u32[]{:S(2)}) collective-permute-start(f32[16,1280]{1,0:T(8,128)S(1)} %get-tuple-element.21), channel_id=1, source_target_pairs={{0,10},{2,8},{4,14},{6,12},{8,2},{10,0},{12,6},{14,4},{1,11},{3,9}... | collective-permute-start | bytes 245768 | tf_op jit(solution)/shard_map/ppermute | solution.py:233
  10.6 2.5 %collective-permute-start.3 = (f32[16,1280]{1,0:T(8,128)S(1)}, f32[16,1280]{1,0:T(8,128)S(1)}, u32[]{:S(2)}, u32[]{:S(2)}) collective-permute-start(f32[16,1280]{1,0:T(8,128)S(1)} %get-tuple-element.22), channel_id=1, source_target_pairs={{0,12},{2,14},{4,8},{6,10},{8,4},{10,6},{12,0},{14,2},{1,13},{3,15... | collective-permute-start | bytes 245768 | tf_op jit(solution)/shard_map/ppermute | solution.py:233
  13.1 1.3 %collective-permute-start.4 = (f32[16,1280]{1,0:T(8,128)S(1)}, f32[16,1280]{1,0:T(8,128)S(1)}, u32[]{:S(2)}, u32[]{:S(2)}) collective-permute-start(f32[16,1280]{1,0:T(8,128)S(1)} %get-tuple-element.23), channel_id=1, source_target_pairs={{0,14},{2,12},{4,10},{6,8},{8,6},{10,4},{12,2},{14,0},{1,15},{3,13... | collective-permute-start | bytes 245768 | tf_op jit(solution)/shard_map/ppermute | solution.py:233
  14.4 1.6 %collective-permute-start.6 = (f32[32,1280]{1,0:T(8,128)S(1)}, f32[32,1280]{1,0:T(8,128)S(1)}, u32[]{:S(2)}, u32[]{:S(2)}) collective-permute-start(f32[32,1280]{1,0:T(8,128)S(1)} %shard_map.58), channel_id=1, source_target_pairs={{0,2},{2,0},{4,6},{6,4},{8,10},{10,8},{12,14},{14,12},{1,3},{3,1},... | collective-permute-start | bytes 491528 | tf_op jit(solution)/shard_map/ppermute | solution.py:233
  16.0 0.7 %copy-done.1 = f32[17]{0:T(128)S(1)} copy-done((f32[17]{0:T(128)S(1)}, f32[17]{0:T(128)}, u32[]{:S(2)}) %copy-start.1) | copy-done | bytes 92
  16.6 0.7 %copy-done.2 = s32[16]{0:T(128)S(1)} copy-done((s32[16]{0:T(128)S(1)}, s32[16]{0:T(128)}, u32[]{:S(2)}) %copy-start.2) | copy-done | bytes 88
  17.3 0.7 %shard_map.55.matrix_ref = f32[96,128]{1,0:T(8,128)S(1)} custom-call(f32[17]{0:T(128)S(1)} %copy-done.1, s32[1]{0:T(128)S(6)} %copy.12.count_ref._, s32[16]{0:T(128)S(1)} %copy-done.2), custom_call_target="tpu_custom_call" | custom-call | flops 10000000000 | bytes 100000000 | tf_op jit(solution)/shard_map/pallas_call | solution.py:239
  18.0 4.9 %collective-permute-done.2.refs_1_ = f32[16,1280]{1,0:T(8,128)S(1)} collective-permute-done((f32[16,1280]{1,0:T(8,128)S(1)}, f32[16,1280]{1,0:T(8,128)S(1)}, u32[]{:S(2)}, u32[]{:S(2)}) %collective-permute-start.2) | collective-permute-done | bytes 81952 | tf_op jit(solution)/shard_map/ppermute | solution.py:233
  23.0 0.3 shard_map.59.refs_7_
  23.3 0.1 collective-permute-start.7
  23.4 3.8 %collective-permute-start.12 = (bf16[96,512]{1,0:T(8,128)(2,1)S(1)}, bf16[96,512]{1,0:T(8,128)(2,1)S(1)}, u32[]{:S(2)}, u32[]{:S(2)}) collective-permute-start(bf16[96,512]{1,0:T(8,128)(2,1)S(1)} %shard_map.59.refs_7_), channel_id=1, source_target_pairs={{0,6},{2,4},{4,2},{6,0},{8,14},{10,12},{12,10},{14,8},{1,7},{3,5},... | collective-permute-start | bytes 294920 | tf_op jit(solution)/shard_map/ppermute | solution.py:233
  27.2 0.9 %collective-permute-start.8 = (bf16[96,512]{1,0:T(8,128)(2,1)S(1)}, bf16[96,512]{1,0:T(8,128)(2,1)S(1)}, u32[]{:S(2)}, u32[]{:S(2)}) collective-permute-start(bf16[96,512]{1,0:T(8,128)(2,1)S(1)} %shard_map.59.refs_7_), channel_id=1, source_target_pairs={{0,2},{2,0},{4,6},{6,4},{8,10},{10,8},{12,14},{14,12},{1,3},{3,1},... | collective-permute-start | bytes 294920 | tf_op jit(solution)/shard_map/ppermute | solution.py:233
  28.1 2.3 %shard_map.60 = (bf16[712,4096]{1,0:T(8,128)(2,1)}, bf16[712,96]{1,0:T(8,128)(2,1)S(1)}) custom-call(f32[96,128]{1,0:T(8,128)S(1)} %shard_map.55.matrix_ref, f32[16,1280]{1,0:T(8,128)S(1)} %collective-permute-done.1.refs_0_, f32[16,1280]{1,0:T(8,128)S(1)} %collective-permute-done.2.refs_1_, f32[16,1280]{1,0:T(8,128)S(1)} %collective-permute-done.3.refs_2_, ...), custom_call_target="tpu_custom_call" | custom-call | tf_op jit(solution)/shard_map/pallas_call | solution.py:296
  30.4 0.5 %collective-permute-done.12.refs_2_ = bf16[96,512]{1,0:T(8,128)(2,1)S(1)} collective-permute-done((bf16[96,512]{1,0:T(8,128)(2,1)S(1)}, bf16[96,512]{1,0:T(8,128)(2,1)S(1)}, u32[]{:S(2)}, u32[]{:S(2)}) %collective-permute-start.12) | collective-permute-done | bytes 98336 | tf_op jit(solution)/shard_map/ppermute | solution.py:233
  30.9 1.3 %collective-permute-done.10.refs_1_ = bf16[96,512]{1,0:T(8,128)(2,1)S(1)} collective-permute-done((bf16[96,512]{1,0:T(8,128)(2,1)S(1)}, bf16[96,512]{1,0:T(8,128)(2,1)S(1)}, u32[]{:S(2)}, u32[]{:S(2)}) %collective-permute-start.10) | collective-permute-done | bytes 98336 | tf_op jit(solution)/shard_map/ppermute | solution.py:233
  32.1 0.6 %collective-permute-done.8.refs_0_ = bf16[96,512]{1,0:T(8,128)(2,1)S(1)} collective-permute-done((bf16[96,512]{1,0:T(8,128)(2,1)S(1)}, bf16[96,512]{1,0:T(8,128)(2,1)S(1)}, u32[]{:S(2)}, u32[]{:S(2)}) %collective-permute-start.8) | collective-permute-done | bytes 98336 | tf_op jit(solution)/shard_map/ppermute | solution.py:233
  32.7 2.3 %shard_map.61.refs_3_ = bf16[712,4096]{1,0:T(8,128)(2,1)} custom-call(bf16[712,96]{1,0:T(8,128)(2,1)S(1)} %get-tuple-element.27.own_ref, bf16[96,512]{1,0:T(8,128)(2,1)S(1)} %collective-permute-done.8.refs_0_, bf16[96,512]{1,0:T(8,128)(2,1)S(1)} %collective-permute-done.10.refs_1_, ...), custom_call_target="tpu_custom_call", output_to_operand_aliasing={{}: (4, {})} | custom-call | tf_op jit(solution)/shard_map/pallas_call | solution.py:204
  35.0 2.3 %shard_map.62 = bf16[712,4096]{1,0:T(8,128)(2,1)} custom-call(bf16[712,96]{1,0:T(8,128)(2,1)S(1)} %get-tuple-element.27.own_ref, bf16[96,512]{1,0:T(8,128)(2,1)S(1)} %collective-permute-done.9.refs_0_, bf16[96,512]{1,0:T(8,128)(2,1)S(1)} %collective-permute-done.11.refs_1_, ...), custom_call_target="tpu_custom_call", output_to_operand_aliasing={{}: (4, {})} | custom-call | tf_op jit(solution)/shard_map/pallas_call | solution.py:204
  (18 shorter events, 0.1 us)
Async XLA Ops:
  0.7 1.0 %copy-start = (f32[8,11392]{1,0:T(8,128)S(1)}, f32[8,11392]{1,0:T(8,128)}, u32[]{:S(2)}) copy-start(f32[8,11392]{1,0:T(8,128)} %series_ref.1) | copy-start | bytes 1093636
  1.9 1.8 %collective-permute-start = (f32[8,8,1280]{2,1,0:T(8,128)S(1)}, f32[8,8,1280]{2,1,0:T(8,128)S(1)}, u32[]{:S(2)}, u32[]{:S(2)}) collective-permute-start(f32[8,8,1280]{2,1,0:T(8,128)S(1)} %get-tuple-element.19), channel_id=1, source_target_pairs={{0,1},{1,0},{2,3},{3,2},{4,5},{5,4},{6,7},{7,6},{8,9},{9,8},{10,11... | collective-permute-start | bytes 983048 | tf_op jit(solution)/shard_map/ppermute | solution.py:236
  3.7 10.7 %collective-permute-start.5 = (f32[32,1280]{1,0:T(8,128)S(1)}, f32[32,1280]{1,0:T(8,128)S(1)}, u32[]{:S(2)}, u32[]{:S(2)}) collective-permute-start(f32[32,1280]{1,0:T(8,128)S(1)} %get-tuple-element.25), channel_id=1, source_target_pairs={{0,4},{2,6},{4,0},{6,2},{8,12},{10,14},{12,8},{14,10},{1,5},{3,7},... | collective-permute-start | bytes 491528 | tf_op jit(solution)/shard_map/ppermute | solution.py:233
  6.7 11.3 %collective-permute-start.1 = (f32[16,1280]{1,0:T(8,128)S(1)}, f32[16,1280]{1,0:T(8,128)S(1)}, u32[]{:S(2)}, u32[]{:S(2)}) collective-permute-start(f32[16,1280]{1,0:T(8,128)S(1)} %get-tuple-element.20), channel_id=1, source_target_pairs={{0,8},{2,10},{4,12},{6,14},{8,0},{10,2},{12,4},{14,6},{1,9},{3,11}... | collective-permute-start | bytes 245768 | tf_op jit(solution)/shard_map/ppermute | solution.py:233
  9.3 13.6 %collective-permute-start.2 = (f32[16,1280]{1,0:T(8,128)S(1)}, f32[16,1280]{1,0:T(8,128)S(1)}, u32[]{:S(2)}, u32[]{:S(2)}) collective-permute-start(f32[16,1280]{1,0:T(8,128)S(1)} %get-tuple-element.21), channel_id=1, source_target_pairs={{0,10},{2,8},{4,14},{6,12},{8,2},{10,0},{12,6},{14,4},{1,11},{3,9}... | collective-permute-start | bytes 245768 | tf_op jit(solution)/shard_map/ppermute | solution.py:233
  10.6 12.4 %collective-permute-start.3 = (f32[16,1280]{1,0:T(8,128)S(1)}, f32[16,1280]{1,0:T(8,128)S(1)}, u32[]{:S(2)}, u32[]{:S(2)}) collective-permute-start(f32[16,1280]{1,0:T(8,128)S(1)} %get-tuple-element.22), channel_id=1, source_target_pairs={{0,12},{2,14},{4,8},{6,10},{8,4},{10,6},{12,0},{14,2},{1,13},{3,15... | collective-permute-start | bytes 245768 | tf_op jit(solution)/shard_map/ppermute | solution.py:233
  13.1 9.9 %collective-permute-start.4 = (f32[16,1280]{1,0:T(8,128)S(1)}, f32[16,1280]{1,0:T(8,128)S(1)}, u32[]{:S(2)}, u32[]{:S(2)}) collective-permute-start(f32[16,1280]{1,0:T(8,128)S(1)} %get-tuple-element.23), channel_id=1, source_target_pairs={{0,14},{2,12},{4,10},{6,8},{8,6},{10,4},{12,2},{14,0},{1,15},{3,13... | collective-permute-start | bytes 245768 | tf_op jit(solution)/shard_map/ppermute | solution.py:233
  14.4 8.6 %collective-permute-start.6 = (f32[32,1280]{1,0:T(8,128)S(1)}, f32[32,1280]{1,0:T(8,128)S(1)}, u32[]{:S(2)}, u32[]{:S(2)}) collective-permute-start(f32[32,1280]{1,0:T(8,128)S(1)} %shard_map.58), channel_id=1, source_target_pairs={{0,2},{2,0},{4,6},{6,4},{8,10},{10,8},{12,14},{14,12},{1,3},{3,1},... | collective-permute-start | bytes 491528 | tf_op jit(solution)/shard_map/ppermute | solution.py:233
  16.0 0.7 %copy-start.1 = (f32[17]{0:T(128)S(1)}, f32[17]{0:T(128)}, u32[]{:S(2)}) copy-start(f32[17]{0:T(128)} %taps_ref.1) | copy-start | bytes 208
  16.6 0.7 %copy-start.2 = (s32[16]{0:T(128)S(1)}, s32[16]{0:T(128)}, u32[]{:S(2)}) copy-start(s32[16]{0:T(128)} %kept_ref.1) | copy-start | bytes 196
  23.3 4.8 %collective-permute-start.7 = (bf16[96,512]{1,0:T(8,128)(2,1)S(1)}, bf16[96,512]{1,0:T(8,128)(2,1)S(1)}, u32[]{:S(2)}, u32[]{:S(2)}) collective-permute-start(bf16[96,512]{1,0:T(8,128)(2,1)S(1)} %shard_map.59.refs_7_), channel_id=1, source_target_pairs={{0,1},{1,0},{2,3},{3,2},{4,5},{5,4},{6,7},{7,6},{8,9},{9,8},{10,11... | collective-permute-start | bytes 294920 | tf_op jit(solution)/shard_map/ppermute | solution.py:236
  23.4 7.5 %collective-permute-start.12 = (bf16[96,512]{1,0:T(8,128)(2,1)S(1)}, bf16[96,512]{1,0:T(8,128)(2,1)S(1)}, u32[]{:S(2)}, u32[]{:S(2)}) collective-permute-start(bf16[96,512]{1,0:T(8,128)(2,1)S(1)} %shard_map.59.refs_7_), channel_id=1, source_target_pairs={{0,6},{2,4},{4,2},{6,0},{8,14},{10,12},{12,10},{14,8},{1,7},{3,5},... | collective-permute-start | bytes 294920 | tf_op jit(solution)/shard_map/ppermute | solution.py:233
  27.2 4.9 %collective-permute-start.10 = (bf16[96,512]{1,0:T(8,128)(2,1)S(1)}, bf16[96,512]{1,0:T(8,128)(2,1)S(1)}, u32[]{:S(2)}, u32[]{:S(2)}) collective-permute-start(bf16[96,512]{1,0:T(8,128)(2,1)S(1)} %shard_map.59.refs_7_), channel_id=1, source_target_pairs={{0,4},{2,6},{4,0},{6,2},{8,12},{10,14},{12,8},{14,10},{1,5},{3,7},... | collective-permute-start | bytes 294920 | tf_op jit(solution)/shard_map/ppermute | solution.py:233
  27.2 5.5 %collective-permute-start.8 = (bf16[96,512]{1,0:T(8,128)(2,1)S(1)}, bf16[96,512]{1,0:T(8,128)(2,1)S(1)}, u32[]{:S(2)}, u32[]{:S(2)}) collective-permute-start(bf16[96,512]{1,0:T(8,128)(2,1)S(1)} %shard_map.59.refs_7_), channel_id=1, source_target_pairs={{0,2},{2,0},{4,6},{6,4},{8,10},{10,8},{12,14},{14,12},{1,3},{3,1},... | collective-permute-start | bytes 294920 | tf_op jit(solution)/shard_map/ppermute | solution.py:233
  30.9 4.1 %collective-permute-start.13 = (bf16[96,512]{1,0:T(8,128)(2,1)S(1)}, bf16[96,512]{1,0:T(8,128)(2,1)S(1)}, u32[]{:S(2)}, u32[]{:S(2)}) collective-permute-start(bf16[96,512]{1,0:T(8,128)(2,1)S(1)} %collective-permute-done.12.refs_2_), channel_id=1, source_target_pairs={{0,1},{1,0},{2,3},{3,2},{4,5},{5,4},{6,7},{7,6},{8,9},{9,8},{10,11... | collective-permute-start | bytes 294920 | tf_op jit(solution)/shard_map/ppermute | solution.py:236
  32.1 2.9 %collective-permute-start.11 = (bf16[96,512]{1,0:T(8,128)(2,1)S(1)}, bf16[96,512]{1,0:T(8,128)(2,1)S(1)}, u32[]{:S(2)}, u32[]{:S(2)}) collective-permute-start(bf16[96,512]{1,0:T(8,128)(2,1)S(1)} %collective-permute-done.10.refs_1_), channel_id=1, source_target_pairs={{0,1},{1,0},{2,3},{3,2},{4,5},{5,4},{6,7},{7,6},{8,9},{9,8},{10,11... | collective-permute-start | bytes 294920 | tf_op jit(solution)/shard_map/ppermute | solution.py:236
  32.7 2.3 %collective-permute-start.9 = (bf16[96,512]{1,0:T(8,128)(2,1)S(1)}, bf16[96,512]{1,0:T(8,128)(2,1)S(1)}, u32[]{:S(2)}, u32[]{:S(2)}) collective-permute-start(bf16[96,512]{1,0:T(8,128)(2,1)S(1)} %collective-permute-done.8.refs_0_), channel_id=1, source_target_pairs={{0,1},{1,0},{2,3},{3,2},{4,5},{5,4},{6,7},{7,6},{8,9},{9,8},{10,11... | collective-permute-start | bytes 294920 | tf_op jit(solution)/shard_map/ppermute | solution.py:236
